TPU v7x, 128 devices: a whole 4x4x4 slice. The times are simulated.
128 devices in a mesh: row: 8 (over y, core), col: 16 (over z, x).
Axes of the slice: x: 4, y: 4, z: 4, core: 2. Of those that a mesh axis runs over, the one named last changes fastest.
Arguments:
- b_three: bfloat16 [256, 384, 1536], P(('row', 'col')), may hold values from -0.47851562 to 0.47851562
- e_occ: float32 [256], replicated, may hold values from -1.5 to -0.3
- e_vir: float32 [384], replicated, may hold values from 0.2 to 3
- c_occ: bfloat16 [768, 256], replicated, may hold values from -0.375 to 0.375
- pair_list: int32 [128, 16, 2], P(('row', 'col')), may hold values from 0 to 255, as said below
- pair_live: int32 [128, 16], P(('row', 'col')), may hold values from 0 to 1, as said below
Outputs:
- gamma_ao: bfloat16 [384, 1536, 768], P('row', 'col')
Inputs may be any that keep to these rules, and one draw needn't show every extreme that they name: pair_list[w, p, 0] is one of the orbitals 2 w to 2 w + 1; pair_list[w, p, 1] is one of the orbitals 2 q to 2 q + 1 with q = (w // 16) * 16 + p. `pair_live`: every worker lists between 1 and 16 pairs; some worker lists all 16.
All inputs are finite; a program needn't handle non-finite values.
Results may differ from a plain program's by a relative error of at most 0.0053.
Values may be sent and summed in bfloat16 or wider, within the bound.
No kernel may reach another device: no remote copies, remote signals or barrier semaphores. Data moves between devices by JAX's collectives and lax.ppermute only.
A program may use at most 128 MiB of HBM per device.

v0:
```python
import functools

import jax
import jax.numpy as jnp
import numpy as np
from jax import lax
from jax.experimental import pallas as pl
from jax.experimental.pallas import tpu as pltpu
from jax.sharding import PartitionSpec as P


AXES = ("row", "col")
SIDE = 4


def shifted(kind, step):
    pairs = []
    for row in range(8):
        for z in range(SIDE):
            for x in range(SIDE):
                along_x = (row % 2 == 0) == (kind == "left")
                to_z, to_x = (z, (x + step) % SIDE) if along_x else ((z + step) % SIDE, x)
                pairs.append((row * 16 + z * SIDE + x, row * 16 + to_z * SIDE + to_x))
    return pairs


def send(value, kind, step):
    return lax.ppermute(value, AXES, shifted(kind, step))


def pair_body(table, place, energies, left_a, left_b, *refs, slots):
    rights = refs[:8]
    vir_row, vir_col, out_a, out_b = refs[8:12]
    left_buf, right_buf, gamma, left_sem, right_sem = refs[12:]
    outs = (out_a, out_b)

    def entry(m):
        worker, right = place[4 + m // 4], place[m % 4]
        first = table[worker * 48 + right * 2]
        second = table[worker * 48 + right * 2 + 1]
        live = table[worker * 48 + 32 + right]
        side = m // 4
        wanted = slots[0] * (1 - side) + slots[1] * side
        return first, second, (live > 0) & (first % 2 == wanted)

    left_copies = [
        pltpu.make_async_copy(left, left_buf.at[s], left_sem.at[s])
        for s, left in enumerate((left_a, left_b))
    ]
    for copy in left_copies:
        copy.start()
    for m in range(8):
        _, second, taken = entry(m)
        for s in range(2):

            @pl.when(taken & (second % 2 == s))
            def _():
                pltpu.make_async_copy(
                    rights[2 * (m % 4) + s], right_buf.at[m], right_sem.at[m]
                ).start()

    gamma[...] = jnp.zeros_like(gamma)
    for copy in left_copies:
        copy.wait()

    def step(m, carry):
        first, second, taken = entry(m)

        @pl.when(taken)
        def _():
            pltpu.make_async_copy(rights[0], right_buf.at[m], right_sem.at[m]).wait()
            right = right_buf[m]
            integrals = lax.dot_general(
                left_buf[m // 4], right, (((1,), (1,)), ((), ())),
                preferred_element_type=jnp.float32,
            )
            denominator = energies[first] + energies[second] - vir_col[...] - vir_row[...]
            weighted = ((2.0 * integrals - integrals.T) / denominator).astype(jnp.bfloat16)
            gamma[m // 4] += jnp.dot(weighted, right, preferred_element_type=jnp.float32)

        return carry

    lax.fori_loop(0, 8, step, 0)
    for s in range(2):
        outs[s][...] = gamma[s].astype(outs[s].dtype)


def partial_gamma(table, place, energies, lefts, slots, rights, vir_row, vir_col, out_dtype):
    virt, aux = lefts[0].shape
    slab = jax.ShapeDtypeStruct((virt, aux), out_dtype)
    hbm = pl.BlockSpec(memory_space=pltpu.HBM)
    smem = pl.BlockSpec(memory_space=pltpu.SMEM)
    vmem = pl.BlockSpec(memory_space=pltpu.VMEM)
    return pl.pallas_call(
        functools.partial(pair_body, slots=slots),
        out_shape=(slab, slab),
        in_specs=[smem, smem, smem] + [hbm] * 10 + [vmem, vmem],
        out_specs=(vmem, vmem),
        scratch_shapes=[
            pltpu.VMEM((2, virt, aux), jnp.bfloat16),
            pltpu.VMEM((8, virt, aux), jnp.bfloat16),
            pltpu.VMEM((2, virt, aux), jnp.float32),
            pltpu.SemaphoreType.DMA((2,)),
            pltpu.SemaphoreType.DMA((8,)),
        ],
        compiler_params=pltpu.CompilerParams(vmem_limit_bytes=40 << 20),
    )(table, place, energies, *lefts, *rights, vir_row, vir_col)


def pack_body(own_a, own_b, up_a, down_a, up_b, down_b, out, total, block):
    for slot, parts in enumerate(((own_a, up_a, down_a), (own_b, up_b, down_b))):
        for k in range(12):
            lanes = slice(k * 128, (k + 1) * 128)
            own, up, down = (part[:, lanes].astype(jnp.float32) for part in parts)
            total[slot * 12 + k] = own + up + down
    for c in range(16):
        tile, offset = divmod(c * 96, 128)
        for slot in range(2):
            pieces = []
            for q in range(4):
                rows = pl.ds(q, 96, stride=4)
                piece = total[slot * 12 + tile, rows, :]
                if offset > 32:
                    piece = jnp.concatenate([piece, total[slot * 12 + tile + 1, rows, :]], 1)
                pieces.append(piece[:, offset : offset + 96])
            value = jnp.concatenate(pieces, 1)
            for k in range(3):
                block[c % 2 * 3 + k, pl.ds(slot, 96, stride=2), :] = value[:, k * 128 : (k + 1) * 128]
        for r in range(8):
            for k in range(3):
                out[r * 16 + c, :, k * 128 : (k + 1) * 128] = block[
                    c % 2 * 3 + k, r * 24 : (r + 1) * 24
                ].astype(out.dtype)


def pack(own_a, own_b, up_a, down_a, up_b, down_b):
    vmem = pl.BlockSpec(memory_space=pltpu.VMEM)
    return pl.pallas_call(
        pack_body,
        out_shape=jax.ShapeDtypeStruct((128, 24, 384), jnp.bfloat16),
        in_specs=[vmem] * 6,
        out_specs=vmem,
        scratch_shapes=[
            pltpu.VMEM((24, 384, 128), jnp.float32),
            pltpu.VMEM((6, 192, 128), jnp.float32),
        ],
        compiler_params=pltpu.CompilerParams(vmem_limit_bytes=32 << 20),
        name="pack",
    )(own_a, own_b, up_a, down_a, up_b, down_b)


def finish_body(blocks, coeff, out, wide):
    step = pl.program_id(0)

    @pl.when(step == 0)
    def _():
        for k in range(3):
            wide[k] = blocks[:, k * 128 : (k + 1) * 128].astype(jnp.float32)

    per_step = out.shape[0] // 4
    for k in range(per_step):
        t = step * per_step + k
        rows = jnp.concatenate(
            [
                jnp.concatenate([wide[k, pl.ds(2 * t + s, 128, stride=24), :] for k in range(3)], 1)
                for s in range(2)
            ],
            0,
        ).astype(jnp.bfloat16)
        result = lax.dot_general(
            rows, coeff[...], (((0,), (1,)), ((), ())),
            preferred_element_type=jnp.float32,
        )
        out[4 * k : 4 * k + 4] = result.reshape(4, 96, 768).astype(out.dtype)


def finish(blocks, coeff):
    rows = 12
    return pl.pallas_call(
        finish_body,
        grid=(48 // rows,),
        out_shape=jax.ShapeDtypeStruct((48, 96, 768), jnp.bfloat16),
        in_specs=[
            pl.BlockSpec((128 * 24, 384), lambda s: (0, 0)),
            pl.BlockSpec((768, 256), lambda s: (0, 0)),
        ],
        out_specs=pl.BlockSpec((rows, 96, 768), lambda s: (s, 0, 0)),
        scratch_shapes=[pltpu.VMEM((3, 128 * 24, 128), jnp.float32)],
        compiler_params=pltpu.CompilerParams(vmem_limit_bytes=32 << 20),
        name="finish",
    )(blocks, coeff)


def add(first, *others):
    total = first.astype(jnp.float32)
    for other in others:
        total = total + other.astype(jnp.float32)
    return total.astype(jnp.bfloat16)


def places():
    rows = []
    for row in range(8):
        for z in range(SIDE):
            for x in range(SIDE):
                along_x = [z * SIDE + (x + d) % SIDE for d in (0, -1, 1, 2)]
                along_z = [(z + d) % SIDE * SIDE + x for d in (0, -1, 1, 2)]
                rows.append(along_z + along_x if row % 2 == 0 else along_x + along_z)
    return np.array(rows, np.int32)


def local(b_three, e_occ, e_vir, c_occ, pair_list, pair_live):
    _, virt_count, _ = b_three.shape
    device = lax.axis_index("row") * 16 + lax.axis_index("col")
    own = (b_three[0], b_three[1])

    right_low_a, right_low_b = send(own[0], "right", 1), send(own[1], "right", 1)
    right_high_a, right_high_b = send(own[0], "right", -1), send(own[1], "right", -1)

    info = jnp.concatenate([pair_list.reshape(1, 32), pair_live.reshape(1, 16)], 1)
    table = lax.all_to_all(
        jnp.broadcast_to(info, (16, 48)), "col", split_axis=0, concat_axis=0, tiled=True
    ).reshape(768)

    wave = lax.optimization_barrier(
        (*own, right_low_a, right_low_b, right_high_a, right_high_b, table)
    )
    own_a, own_b, right_low_a, right_low_b, right_high_a, right_high_b, table = wave
    left_low_a = send(own_a, "left", 1)
    left_high_b = send(own_b, "left", -1)
    right_far_a = send(right_low_a, "right", 1)
    right_far_b = send(right_high_b, "right", -1)
    wave = lax.optimization_barrier(
        (own_a, own_b, left_low_a, left_high_b, right_far_a, right_far_b)
    )
    own_a, own_b, left_low_a, left_high_b, right_far_a, right_far_b = wave
    left_far_a = send(left_low_a, "left", 1)
    left_far_b = send(left_high_b, "left", -1)
    left_low_b = send(own_b, "left", 1)
    left_high_a = send(own_a, "left", -1)

    rights = (*own, right_low_a, right_low_b, right_high_a, right_high_b, right_far_a, right_far_b)
    vir_row, vir_col = e_vir.reshape(1, virt_count), e_vir.reshape(virt_count, 1)
    place = lax.dynamic_index_in_dim(jnp.asarray(places()), device, 0, keepdims=False)

    def partial(lefts, which, slots, dtype=jnp.bfloat16):
        here = jnp.concatenate([place[:4]] + [place[4 + k : 5 + k] for k in which])
        return partial_gamma(table, here, e_occ, lefts, slots, rights, vir_row, vir_col, dtype)

    low_a, high_b = partial((left_low_a, left_high_b), (1, 2), (0, 1))
    sum_a, sum_b = partial(own, (0, 0), (0, 1), jnp.float32)
    low_a, high_b, _, _ = lax.optimization_barrier((low_a, high_b, left_far_a, left_far_b))
    up_b = send(high_b, "left", 1)
    down_a = send(low_a, "left", -1)
    far_a, far_b = partial((left_far_a, left_far_b), (3, 3), (0, 1))
    low_b, high_a = partial((left_low_b, left_high_a), (1, 2), (1, 0))

    relay_a = send(far_a, "left", 1)
    relay_b = send(far_b, "left", -1)
    up_a = send(add(high_a, relay_a), "left", 1)
    down_b = send(add(low_b, relay_b), "left", -1)

    blocks = pack(sum_a, sum_b, up_a, down_a, up_b, down_b)
    moved = lax.all_to_all(blocks, AXES, split_axis=0, concat_axis=0, tiled=True)
    coeff = c_occ.reshape(-1, 128, 2).transpose(0, 2, 1).reshape(-1, 256)
    return finish(moved.reshape(128 * 24, 384), coeff)


def solution(mesh):
    return jax.shard_map(
        local,
        mesh=mesh,
        in_specs=(
            P(AXES, None, None),
            P(),
            P(),
            P(),
            P(AXES, None, None),
            P(AXES, None),
        ),
        out_specs=P("row", "col", None),
        check_vma=False,
    )
```

profile of v0, /device:TPU:1, one launch (start us, length us, event | category | flops | bytes accessed | tf_op | source)
XLA Modules:
  0.0 193.3 jit_solution(18208511304711715846)
XLA Ops:
  0.0 1.8 slice_bitcast_fusion
  1.8 2.1 %collective-permute-start = (bf16[384,1536]{1,0:T(8,128)(2,1)S(1)}, bf16[384,1536]{1,0:T(8,128)(2,1)S(1)}, u32[]{:S(2)}, u32[]{:S(2)}) collective-permute-start(bf16[384,1536]{1,0:T(8,128)(2,1)S(1)} %get-tuple-element.40.left_a.refs_0_), channel_id=1, source_target_pairs={{0,4},{1,5},{2,6},{3,7},{4,8},{5,9},{6,10},{7,11},{8,12},{9,13},{1... | collective-permute-start | bytes 3538952 | tf_op jit(solution)/shard_map/ppermute | solution.py:28
  3.9 1.2 collective-permute-start.1
  5.1 1.5 collective-permute-start.2
  8.8 27.5 %all_to_all.11 = s32[16,1,48]{2,1,0:T(1,128)S(1)} all-to-all(s32[16,1,48]{2,1,0:T(1,128)S(1)} %broadcast_in_dim.2), channel_id=1, replica_groups=mesh['row'=8,'col'=16] {'col'}, dimensions={0} | all-to-all | bytes 6144 | tf_op jit(solution)/shard_map/all_to_all | solution.py:221
  36.9 1.2 reduce.3
  39.0 1.0 collective-permute-start.6
  40.0 1.8 collective-permute-start.7
  42.4 2.1 %collective-permute-start.5 = (bf16[384,1536]{1,0:T(8,128)(2,1)S(1)}, bf16[384,1536]{1,0:T(8,128)(2,1)}, u32[]{:S(2)}, u32[]{:S(2)}) collective-permute-start(bf16[384,1536]{1,0:T(8,128)(2,1)S(1)} %get-tuple-element.39.left_b.refs_1_), channel_id=1, source_target_pairs={{0,3},{1,0},{2,1},{3,2},{4,7},{5,4},{6,5},{7,6},{8,11},{9,8},{10,9... | collective-permute-start | bytes 3538952 | tf_op jit(solution)/shard_map/ppermute | solution.py:28
  44.5 20.3 %collective-permute-done.6.refs_6_ = bf16[384,1536]{1,0:T(8,128)(2,1)S(1)} collective-permute-done((bf16[384,1536]{1,0:T(8,128)(2,1)S(1)}, bf16[384,1536]{1,0:T(8,128)(2,1)S(1)}, u32[]{:S(2)}, u32[]{:S(2)}) %collective-permute-start.6) | collective-permute-done | bytes 1179680 | tf_op jit(solution)/shard_map/ppermute | solution.py:28
  64.8 1.0 copy-done
  65.8 1.0 copy-done.3
  66.8 1.6 collective-permute-done.4.left_a
  69.1 2.6 %collective-permute-start.11 = (bf16[384,1536]{1,0:T(8,128)(2,1)}, bf16[384,1536]{1,0:T(8,128)(2,1)}, u32[]{:S(2)}, u32[]{:S(2)}) collective-permute-start(bf16[384,1536]{1,0:T(8,128)(2,1)} %collective-permute-done.5.left_b), channel_id=1, source_target_pairs={{0,3},{1,0},{2,1},{3,2},{4,7},{5,4},{6,5},{7,6},{8,11},{9,8},{10,9... | collective-permute-start | bytes 3538952 | tf_op jit(solution)/shard_map/ppermute | solution.py:28
  73.9 2.7 %pad_add_fusion.1 = (s32[6]{0:T(128)S(1)}, s32[6]{0:T(128)S(1)}, s32[6]{0:T(128)S(1)}) fusion(s32[1]{0:T(128)} %bitcast.6, s32[1]{0:T(128)} %bitcast.5, s32[4]{0:T(128)S(1)} %slice_bitcast_fusion.2, s32[1]{0:T(128)} %bitcast.7, s32[1]{0:T(128)} %bitcast.4), kind=kLoop, calls=%fused_computation.7 | loop fusion | flops 36 | bytes 104 | tf_op jit(solution)/shard_map/concatenate | solution.py:247
  76.6 2.7 %collective-permute-start.9 = (bf16[384,1536]{1,0:T(8,128)(2,1)S(1)}, bf16[384,1536]{1,0:T(8,128)(2,1)S(1)}, u32[]{:S(2)}, u32[]{:S(2)}) collective-permute-start(bf16[384,1536]{1,0:T(8,128)(2,1)S(1)} %get-tuple-element.40.left_a.refs_0_), channel_id=1, source_target_pairs={{0,3},{1,0},{2,1},{3,2},{4,7},{5,4},{6,5},{7,6},{8,11},{9,8},{10,9... | collective-permute-start | bytes 3538952 | tf_op jit(solution)/shard_map/ppermute | solution.py:28
  79.2 6.7 %collective-permute-done.10.left_a = bf16[384,1536]{1,0:T(8,128)(2,1)} collective-permute-done((bf16[384,1536]{1,0:T(8,128)(2,1)}, bf16[384,1536]{1,0:T(8,128)(2,1)}, u32[]{:S(2)}, u32[]{:S(2)}) %collective-permute-start.10) | collective-permute-done | bytes 1179680 | tf_op jit(solution)/shard_map/ppermute | solution.py:28
  85.9 1.3 copy-done.1
  87.2 1.3 copy-done.4
  89.4 9.1 %shard_map.75 = (bf16[384,1536]{1,0:T(8,128)(2,1)S(1)}, bf16[384,1536]{1,0:T(8,128)(2,1)S(1)}) custom-call(s32[768]{0:T(1024)S(1)} %reshape.34.table, s32[6]{0:T(128)S(1)} %get-tuple-element.54.place, f32[256]{0:T(256)S(1)} %copy-done.8, bf16[384,1536]{1,0:T(8,128)(2,1)} %collective-permute-done.10.left_a, bf16[384,1536]{1,0:T(8,128)(2,1)} %collective-permute-done.11.left_b, ...), custom_call_target="tpu_custom_call" | custom-call | tf_op jit(solution)/shard_map/pallas_call | solution.py:94
  98.5 1.0 collective-permute-start.16
  100.0 9.4 %shard_map.76 = (bf16[384,1536]{1,0:T(8,128)(2,1)S(1)}, bf16[384,1536]{1,0:T(8,128)(2,1)S(1)}) custom-call(s32[768]{0:T(1024)S(1)} %reshape.34.table, s32[6]{0:T(128)S(1)} %get-tuple-element.53.place, f32[256]{0:T(256)S(1)} %copy-done.8, bf16[384,1536]{1,0:T(8,128)(2,1)} %collective-permute-done.4.left_a, bf16[384,1536]{1,0:T(8,128)(2,1)} %collective-permute-done.5.left_b, ...), custom_call_target="tpu_custom_call" | custom-call | tf_op jit(solution)/shard_map/pallas_call | solution.py:94
  109.6 1.9 %collective-permute-start.15 = (bf16[384,1536]{1,0:T(8,128)(2,1)S(1)}, bf16[384,1536]{1,0:T(8,128)(2,1)S(1)}, u32[]{:S(2)}, u32[]{:S(2)}) collective-permute-start(bf16[384,1536]{1,0:T(8,128)(2,1)S(1)} %get-tuple-element.48), channel_id=1, source_target_pairs={{0,1},{1,2},{2,3},{3,0},{4,5},{5,6},{6,7},{7,4},{8,9},{9,10},{10,1... | collective-permute-start | bytes 3538952 | tf_op jit(solution)/shard_map/ppermute | solution.py:28
  111.6 2.3 %shard_map.74 = (bf16[384,1536]{1,0:T(8,128)(2,1)S(1)}, bf16[384,1536]{1,0:T(8,128)(2,1)S(1)}) custom-call(s32[768]{0:T(1024)S(1)} %reshape.34.table, s32[6]{0:T(128)S(1)} %get-tuple-element.53.place, f32[256]{0:T(256)S(1)} %copy-done.8, bf16[384,1536]{1,0:T(8,128)(2,1)S(1)} %collective-permute-done.8.left_a, ...), custom_call_target="tpu_custom_call" | custom-call | tf_op jit(solution)/shard_map/pallas_call | solution.py:94
  114.2 4.4 %collective-permute-start.17 = (bf16[384,1536]{1,0:T(8,128)(2,1)S(1)}, bf16[384,1536]{1,0:T(8,128)(2,1)S(1)}, u32[]{:S(2)}, u32[]{:S(2)}) collective-permute-start(bf16[384,1536]{1,0:T(8,128)(2,1)S(1)} %add_convert_fusion), channel_id=1, source_target_pairs={{0,3},{1,0},{2,1},{3,2},{4,7},{5,4},{6,5},{7,6},{8,11},{9,8},{10,9... | collective-permute-start | bytes 3538952 | tf_op jit(solution)/shard_map/ppermute | solution.py:28
  120.3 9.0 %shard_map.73 = (f32[384,1536]{1,0:T(8,128)S(1)}, f32[384,1536]{1,0:T(8,128)S(1)}) custom-call(s32[768]{0:T(1024)S(1)} %reshape.34.table, s32[6]{0:T(128)S(1)} %get-tuple-element.55.place, f32[256]{0:T(256)S(1)} %copy-done.8, bf16[384,1536]{1,0:T(8,128)(2,1)S(1)} %get-tuple-element.40.left_a.refs_0_, bf16[384,1536]{1,0:T(8,128)(2,1)S(1)} %get-tuple-element.39.left_b.refs_1_, ...), custom_call_target="tpu_custom_call" | custom-call | tf_op jit(solution)/shard_map/pallas_call | solution.py:94
  129.3 9.9 %collective-permute-done.17.down_b = bf16[384,1536]{1,0:T(8,128)(2,1)S(1)} collective-permute-done((bf16[384,1536]{1,0:T(8,128)(2,1)S(1)}, bf16[384,1536]{1,0:T(8,128)(2,1)S(1)}, u32[]{:S(2)}, u32[]{:S(2)}) %collective-permute-start.17) | collective-permute-done | bytes 1179680 | tf_op jit(solution)/shard_map/ppermute | solution.py:28
  139.2 2.2 %collective-permute-done.13.up_a = bf16[384,1536]{1,0:T(8,128)(2,1)S(1)} collective-permute-done((bf16[384,1536]{1,0:T(8,128)(2,1)S(1)}, bf16[384,1536]{1,0:T(8,128)(2,1)S(1)}, u32[]{:S(2)}, u32[]{:S(2)}) %collective-permute-start.13) | collective-permute-done | bytes 1179680 | tf_op jit(solution)/shard_map/ppermute | solution.py:28
  141.4 4.1 %pack.1 = bf16[128,24,384]{2,1,0:T(8,128)(2,1)} custom-call(f32[384,1536]{1,0:T(8,128)S(1)} %get-tuple-element.37.own_a, f32[384,1536]{1,0:T(8,128)S(1)} %get-tuple-element.38.own_b, bf16[384,1536]{1,0:T(8,128)(2,1)S(1)} %collective-permute-done.13.up_a, bf16[384,1536]{1,0:T(8,128)(2,1)S(1)} %collective-permute-done.14.down_a, ...), custom_call_target="tpu_custom_call" | custom-call | tf_op jit(solution)/shard_map/pack/pallas_call | solution.py:138
  145.5 10.9 %all-to-all-start.1 = ((bf16[128,24,384]{2,1,0:T(8,128)(2,1)}), bf16[128,24,384]{2,1,0:T(8,128)(2,1)S(1)}, u32[]{:S(2)}, u32[]{:S(2)}) async-start(bf16[128,24,384]{2,1,0:T(8,128)(2,1)} %pack.1), calls=%async_computation.1 | async-start | bytes 4718592 | tf_op jit(solution)/shard_map/all_to_all | solution.py:264
  157.3 31.2 %all-to-all-done.1 = bf16[128,24,384]{2,1,0:T(8,128)(2,1)S(1)} async-done(((bf16[128,24,384]{2,1,0:T(8,128)(2,1)}), bf16[128,24,384]{2,1,0:T(8,128)(2,1)S(1)}, u32[]{:S(2)}, u32[]{:S(2)}) %all-to-all-start.1) | async-done | bytes 2359328 | tf_op jit(solution)/shard_map/all_to_all | solution.py:264
  188.6 4.8 %finish.1 = bf16[48,96,768]{2,1,0:T(8,128)(2,1)} custom-call(bf16[3072,384]{1,0:T(8,128)(2,1)S(1)} %bitcast.20, bf16[768,256]{1,0:T(8,128)(2,1)S(1)} %bitcast.21), custom_call_target="tpu_custom_call" | custom-call | tf_op jit(solution)/shard_map/finish/pallas_call | solution.py:179
  (55 shorter events, 11.6 us)
Async XLA Ops:
  0.0 71.7 %copy-start.10 = (f32[384]{0:T(512)S(1)}, f32[384]{0:T(512)}, u32[]{:S(2)}) copy-start(f32[384]{0:T(512)} %param.9) | copy-start | bytes 4612
  0.0 85.9 %copy-start.8 = (f32[256]{0:T(256)S(1)}, f32[256]{0:T(256)}, u32[]{:S(2)}) copy-start(f32[256]{0:T(256)} %energies.7) | copy-start | bytes 3076
  1.8 37.1 %collective-permute-start = (bf16[384,1536]{1,0:T(8,128)(2,1)S(1)}, bf16[384,1536]{1,0:T(8,128)(2,1)S(1)}, u32[]{:S(2)}, u32[]{:S(2)}) collective-permute-start(bf16[384,1536]{1,0:T(8,128)(2,1)S(1)} %get-tuple-element.40.left_a.refs_0_), channel_id=1, source_target_pairs={{0,4},{1,5},{2,6},{3,7},{4,8},{5,9},{6,10},{7,11},{8,12},{9,13},{1... | collective-permute-start | bytes 3538952 | tf_op jit(solution)/shard_map/ppermute | solution.py:28
  3.9 35.0 %collective-permute-start.1 = (bf16[384,1536]{1,0:T(8,128)(2,1)S(1)}, bf16[384,1536]{1,0:T(8,128)(2,1)}, u32[]{:S(2)}, u32[]{:S(2)}) collective-permute-start(bf16[384,1536]{1,0:T(8,128)(2,1)S(1)} %get-tuple-element.39.left_b.refs_1_), channel_id=1, source_target_pairs={{0,4},{1,5},{2,6},{3,7},{4,8},{5,9},{6,10},{7,11},{8,12},{9,13},{1... | collective-permute-start | bytes 3538952 | tf_op jit(solution)/shard_map/ppermute | solution.py:28
  5.1 33.8 %collective-permute-start.2 = (bf16[384,1536]{1,0:T(8,128)(2,1)S(1)}, bf16[384,1536]{1,0:T(8,128)(2,1)}, u32[]{:S(2)}, u32[]{:S(2)}) collective-permute-start(bf16[384,1536]{1,0:T(8,128)(2,1)S(1)} %get-tuple-element.40.left_a.refs_0_), channel_id=1, source_target_pairs={{0,12},{1,13},{2,14},{3,15},{4,0},{5,1},{6,2},{7,3},{8,4},{9,5},{1... | collective-permute-start | bytes 3538952 | tf_op jit(solution)/shard_map/ppermute | solution.py:28
  6.6 32.4 %collective-permute-start.3 = (bf16[384,1536]{1,0:T(8,128)(2,1)S(1)}, bf16[384,1536]{1,0:T(8,128)(2,1)}, u32[]{:S(2)}, u32[]{:S(2)}) collective-permute-start(bf16[384,1536]{1,0:T(8,128)(2,1)S(1)} %get-tuple-element.39.left_b.refs_1_), channel_id=1, source_target_pairs={{0,12},{1,13},{2,14},{3,15},{4,0},{5,1},{6,2},{7,3},{8,4},{9,5},{1... | collective-permute-start | bytes 3538952 | tf_op jit(solution)/shard_map/ppermute | solution.py:28
  39.0 25.8 %collective-permute-start.6 = (bf16[384,1536]{1,0:T(8,128)(2,1)S(1)}, bf16[384,1536]{1,0:T(8,128)(2,1)S(1)}, u32[]{:S(2)}, u32[]{:S(2)}) collective-permute-start(bf16[384,1536]{1,0:T(8,128)(2,1)S(1)} %collective-permute-done.refs_2_), channel_id=1, source_target_pairs={{0,4},{1,5},{2,6},{3,7},{4,8},{5,9},{6,10},{7,11},{8,12},{9,13},{1... | collective-permute-start | bytes 3538952 | tf_op jit(solution)/shard_map/ppermute | solution.py:28
  40.0 25.8 %collective-permute-start.7 = (bf16[384,1536]{1,0:T(8,128)(2,1)}, bf16[384,1536]{1,0:T(8,128)(2,1)S(1)}, u32[]{:S(2)}, u32[]{:S(2)}) collective-permute-start(bf16[384,1536]{1,0:T(8,128)(2,1)} %collective-permute-done.3.refs_5_), channel_id=1, source_target_pairs={{0,12},{1,13},{2,14},{3,15},{4,0},{5,1},{6,2},{7,3},{8,4},{9,5},{1... | collective-permute-start | bytes 3538952 | tf_op jit(solution)/shard_map/ppermute | solution.py:28
  41.8 26.6 %collective-permute-start.4 = (bf16[384,1536]{1,0:T(8,128)(2,1)S(1)}, bf16[384,1536]{1,0:T(8,128)(2,1)}, u32[]{:S(2)}, u32[]{:S(2)}) collective-permute-start(bf16[384,1536]{1,0:T(8,128)(2,1)S(1)} %get-tuple-element.40.left_a.refs_0_), channel_id=1, source_target_pairs={{0,1},{1,2},{2,3},{3,0},{4,5},{5,6},{6,7},{7,4},{8,9},{9,10},{10,1... | collective-permute-start | bytes 3538952 | tf_op jit(solution)/shard_map/ppermute | solution.py:28
  42.4 26.6 %collective-permute-start.5 = (bf16[384,1536]{1,0:T(8,128)(2,1)S(1)}, bf16[384,1536]{1,0:T(8,128)(2,1)}, u32[]{:S(2)}, u32[]{:S(2)}) collective-permute-start(bf16[384,1536]{1,0:T(8,128)(2,1)S(1)} %get-tuple-element.39.left_b.refs_1_), channel_id=1, source_target_pairs={{0,3},{1,0},{2,1},{3,2},{4,7},{5,4},{6,5},{7,6},{8,11},{9,8},{10,9... | collective-permute-start | bytes 3538952 | tf_op jit(solution)/shard_map/ppermute | solution.py:28
  64.8 1.0 copy-start
  65.8 1.0 copy-start.3
  69.0 16.9 %collective-permute-start.10 = (bf16[384,1536]{1,0:T(8,128)(2,1)}, bf16[384,1536]{1,0:T(8,128)(2,1)}, u32[]{:S(2)}, u32[]{:S(2)}) collective-permute-start(bf16[384,1536]{1,0:T(8,128)(2,1)} %collective-permute-done.4.left_a), channel_id=1, source_target_pairs={{0,1},{1,2},{2,3},{3,0},{4,5},{5,6},{6,7},{7,4},{8,9},{9,10},{10,1... | collective-permute-start | bytes 3538952 | tf_op jit(solution)/shard_map/ppermute | solution.py:28
  69.1 16.8 %collective-permute-start.11 = (bf16[384,1536]{1,0:T(8,128)(2,1)}, bf16[384,1536]{1,0:T(8,128)(2,1)}, u32[]{:S(2)}, u32[]{:S(2)}) collective-permute-start(bf16[384,1536]{1,0:T(8,128)(2,1)} %collective-permute-done.5.left_b), channel_id=1, source_target_pairs={{0,3},{1,0},{2,1},{3,2},{4,7},{5,4},{6,5},{7,6},{8,11},{9,8},{10,9... | collective-permute-start | bytes 3538952 | tf_op jit(solution)/shard_map/ppermute | solution.py:28
  76.5 33.1 %collective-permute-start.8 = (bf16[384,1536]{1,0:T(8,128)(2,1)S(1)}, bf16[384,1536]{1,0:T(8,128)(2,1)S(1)}, u32[]{:S(2)}, u32[]{:S(2)}) collective-permute-start(bf16[384,1536]{1,0:T(8,128)(2,1)S(1)} %get-tuple-element.39.left_b.refs_1_), channel_id=1, source_target_pairs={{0,1},{1,2},{2,3},{3,0},{4,5},{5,6},{6,7},{7,4},{8,9},{9,10},{10,1... | collective-permute-start | bytes 3538952 | tf_op jit(solution)/shard_map/ppermute | solution.py:28
  76.6 35.0 %collective-permute-start.9 = (bf16[384,1536]{1,0:T(8,128)(2,1)S(1)}, bf16[384,1536]{1,0:T(8,128)(2,1)S(1)}, u32[]{:S(2)}, u32[]{:S(2)}) collective-permute-start(bf16[384,1536]{1,0:T(8,128)(2,1)S(1)} %get-tuple-element.40.left_a.refs_0_), channel_id=1, source_target_pairs={{0,3},{1,0},{2,1},{3,2},{4,7},{5,4},{6,5},{7,6},{8,11},{9,8},{10,9... | collective-permute-start | bytes 3538952 | tf_op jit(solution)/shard_map/ppermute | solution.py:28
  85.9 1.3 copy-start.1
  87.2 1.3 copy-start.4
  88.4 0.9 copy-start.6
  98.5 15.4 %collective-permute-start.16 = (bf16[384,1536]{1,0:T(8,128)(2,1)S(1)}, bf16[384,1536]{1,0:T(8,128)(2,1)S(1)}, u32[]{:S(2)}, u32[]{:S(2)}) collective-permute-start(bf16[384,1536]{1,0:T(8,128)(2,1)S(1)} %get-tuple-element.50), channel_id=1, source_target_pairs={{0,3},{1,0},{2,1},{3,2},{4,7},{5,4},{6,5},{7,6},{8,11},{9,8},{10,9... | collective-permute-start | bytes 3538952 | tf_op jit(solution)/shard_map/ppermute | solution.py:28
  99.5 19.1 %collective-permute-start.12 = (bf16[384,1536]{1,0:T(8,128)(2,1)S(1)}, bf16[384,1536]{1,0:T(8,128)(2,1)S(1)}, u32[]{:S(2)}, u32[]{:S(2)}) collective-permute-start(bf16[384,1536]{1,0:T(8,128)(2,1)S(1)} %get-tuple-element.44), channel_id=1, source_target_pairs={{0,1},{1,2},{2,3},{3,0},{4,5},{5,6},{6,7},{7,4},{8,9},{9,10},{10,1... | collective-permute-start | bytes 3538952 | tf_op jit(solution)/shard_map/ppermute | solution.py:28
  109.5 19.8 %collective-permute-start.14 = (bf16[384,1536]{1,0:T(8,128)(2,1)S(1)}, bf16[384,1536]{1,0:T(8,128)(2,1)S(1)}, u32[]{:S(2)}, u32[]{:S(2)}) collective-permute-start(bf16[384,1536]{1,0:T(8,128)(2,1)S(1)} %get-tuple-element.47), channel_id=1, source_target_pairs={{0,3},{1,0},{2,1},{3,2},{4,7},{5,4},{6,5},{7,6},{8,11},{9,8},{10,9... | collective-permute-start | bytes 3538952 | tf_op jit(solution)/shard_map/ppermute | solution.py:28
  109.6 19.6 %collective-permute-start.15 = (bf16[384,1536]{1,0:T(8,128)(2,1)S(1)}, bf16[384,1536]{1,0:T(8,128)(2,1)S(1)}, u32[]{:S(2)}, u32[]{:S(2)}) collective-permute-start(bf16[384,1536]{1,0:T(8,128)(2,1)S(1)} %get-tuple-element.48), channel_id=1, source_target_pairs={{0,1},{1,2},{2,3},{3,0},{4,5},{5,6},{6,7},{7,4},{8,9},{9,10},{10,1... | collective-permute-start | bytes 3538952 | tf_op jit(solution)/shard_map/ppermute | solution.py:28
  114.2 25.0 %collective-permute-start.17 = (bf16[384,1536]{1,0:T(8,128)(2,1)S(1)}, bf16[384,1536]{1,0:T(8,128)(2,1)S(1)}, u32[]{:S(2)}, u32[]{:S(2)}) collective-permute-start(bf16[384,1536]{1,0:T(8,128)(2,1)S(1)} %add_convert_fusion), channel_id=1, source_target_pairs={{0,3},{1,0},{2,1},{3,2},{4,7},{5,4},{6,5},{7,6},{8,11},{9,8},{10,9... | collective-permute-start | bytes 3538952 | tf_op jit(solution)/shard_map/ppermute | solution.py:28
  118.6 1.3 copy-start.2
  118.6 1.6 copy-start.5
  118.6 1.6 copy-start.7
  118.9 22.4 %collective-permute-start.13 = (bf16[384,1536]{1,0:T(8,128)(2,1)S(1)}, bf16[384,1536]{1,0:T(8,128)(2,1)S(1)}, u32[]{:S(2)}, u32[]{:S(2)}) collective-permute-start(bf16[384,1536]{1,0:T(8,128)(2,1)S(1)} %add_convert_fusion.1), channel_id=1, source_target_pairs={{0,1},{1,2},{2,3},{3,0},{4,5},{5,6},{6,7},{7,4},{8,9},{9,10},{10,1... | collective-permute-start | bytes 3538952 | tf_op jit(solution)/shard_map/ppermute | solution.py:28
  145.5 10.9 %copy-start.9 = (bf16[768,256]{1,0:T(8,128)(2,1)S(1)}, bf16[768,256]{1,0:T(8,128)(2,1)}, u32[]{:S(2)}) copy-start(bf16[768,256]{1,0:T(8,128)(2,1)} %param.10) | copy-start | bytes 1179652
  145.5 43.1 %all-to-all-start.1 = ((bf16[128,24,384]{2,1,0:T(8,128)(2,1)}), bf16[128,24,384]{2,1,0:T(8,128)(2,1)S(1)}, u32[]{:S(2)}, u32[]{:S(2)}) async-start(bf16[128,24,384]{2,1,0:T(8,128)(2,1)} %pack.1), calls=%async_computation.1 | async-start | bytes 4718592 | tf_op jit(solution)/shard_map/all_to_all | solution.py:264
where the time goes:
time: 194 us; the launch traced here: 193 us
  waiting for transfers between devices  72.5 us (37%)
  Pallas kernels  38.7 us (20%)
  starting transfers between devices  35.6 us (18%)
  blocking collectives  27.5 us (14%)
  local copies, waits for them, and re-layouts  13.6 us (7%)
  other arithmetic  5.2 us (3%)
    ppermute x18, waiting for transfers between devices, send(): return lax.ppermute(value, AXES, shifted(kind, step))  41.3 us
    all_to_all x1, waiting for transfers between devices, local(): lax.all_to_all(blocks, AXES, split_axis=0, concat_axis=0, tiled=True)  31.2 us
    pallas_call x4, Pallas kernels, partial_gamma(): pl.pallas_call(functools.partial(pair_body, slots=slots), out_shape=(slab...  29.8 us
    all_to_all x1, blocking collectives, local(): lax.all_to_all(jnp.broadcast_to(info, (16, 48)), 'col', split_axis=0, con...  27.5 us
    ppermute x18, starting transfers between devices, send(): return lax.ppermute(value, AXES, shifted(kind, step))  24.7 us
    all_to_all x1, starting transfers between devices, local(): lax.all_to_all(blocks, AXES, split_axis=0, concat_axis=0, tiled=True)  10.9 us
    unnamed x25, local copies, waits for them, and re-layouts  6.99 us
    pallas_call x1, Pallas kernels, finish(): pl.pallas_call(finish_body, grid=(48 // rows,), out_shape=jax.ShapeDtypeS...  4.76 us
  transfers between devices with their start and end apart: 19, of which 7 were waited for; matrix products, arithmetic and copies ran while one was open for 6% of the time, Pallas kernels for 15%

commit v1 on v0

--- a/solution.py
+++ b/solution.py
@@ -28,19 +28,21 @@
     return lax.ppermute(value, AXES, shifted(kind, step))
 
 
-def pair_body(table, place, energies, left_a, left_b, *refs, slots):
+def pair_body(place, table_a, table_b, energies, left_a, left_b, *refs, slots):
     rights = refs[:8]
     vir_row, vir_col, out_a, out_b = refs[8:12]
     left_buf, right_buf, gamma, left_sem, right_sem = refs[12:]
     outs = (out_a, out_b)
 
     def entry(m):
-        worker, right = place[4 + m // 4], place[m % 4]
-        first = table[worker * 48 + right * 2]
-        second = table[worker * 48 + right * 2 + 1]
-        live = table[worker * 48 + 32 + right]
-        side = m // 4
-        wanted = slots[0] * (1 - side) + slots[1] * side
+        side, right = m // 4, place[m % 4]
+        at_a, at_b = (lambda k: table_a[0, k]), (lambda k: table_b[0, k])
+
+        def pick(k):
+            return jnp.where(side == 0, at_a(k), at_b(k))
+
+        first, second, live = pick(right * 2), pick(right * 2 + 1), pick(32 + right)
+        wanted = jnp.where(side == 0, slots[0], slots[1])
         return first, second, (live > 0) & (first % 2 == wanted)
 
     left_copies = [
@@ -85,7 +87,7 @@
         outs[s][...] = gamma[s].astype(outs[s].dtype)
 
 
-def partial_gamma(table, place, energies, lefts, slots, rights, vir_row, vir_col, out_dtype):
+def partial_gamma(place, tables, energies, lefts, slots, rights, vir_row, vir_col, out_dtype):
     virt, aux = lefts[0].shape
     slab = jax.ShapeDtypeStruct((virt, aux), out_dtype)
     hbm = pl.BlockSpec(memory_space=pltpu.HBM)
@@ -94,7 +96,7 @@
     return pl.pallas_call(
         functools.partial(pair_body, slots=slots),
         out_shape=(slab, slab),
-        in_specs=[smem, smem, smem] + [hbm] * 10 + [vmem, vmem],
+        in_specs=[smem, smem, smem, smem] + [hbm] * 10 + [vmem, vmem],
         out_specs=(vmem, vmem),
         scratch_shapes=[
             pltpu.VMEM((2, virt, aux), jnp.bfloat16),
@@ -104,7 +106,7 @@
             pltpu.SemaphoreType.DMA((8,)),
         ],
         compiler_params=pltpu.CompilerParams(vmem_limit_bytes=40 << 20),
-    )(table, place, energies, *lefts, *rights, vir_row, vir_col)
+    )(place, *tables, energies, *lefts, *rights, vir_row, vir_col)
 
 
 def pack_body(own_a, own_b, up_a, down_a, up_b, down_b, out, total, block):
@@ -198,15 +200,15 @@
     return total.astype(jnp.bfloat16)
 
 
-def places():
+def right_columns():
     rows = []
     for row in range(8):
         for z in range(SIDE):
             for x in range(SIDE):
                 along_x = [z * SIDE + (x + d) % SIDE for d in (0, -1, 1, 2)]
                 along_z = [(z + d) % SIDE * SIDE + x for d in (0, -1, 1, 2)]
-                rows.append(along_z + along_x if row % 2 == 0 else along_x + along_z)
-    return np.array(rows, np.int32)
+                rows.append(along_z if row % 2 == 0 else along_x)
+    return np.array(rows, np.int32).reshape(-1)
 
 
 def local(b_three, e_occ, e_vir, c_occ, pair_list, pair_live):
@@ -216,16 +218,13 @@
 
     right_low_a, right_low_b = send(own[0], "right", 1), send(own[1], "right", 1)
     right_high_a, right_high_b = send(own[0], "right", -1), send(own[1], "right", -1)
-
     info = jnp.concatenate([pair_list.reshape(1, 32), pair_live.reshape(1, 16)], 1)
-    table = lax.all_to_all(
-        jnp.broadcast_to(info, (16, 48)), "col", split_axis=0, concat_axis=0, tiled=True
-    ).reshape(768)
-
-    wave = lax.optimization_barrier(
-        (*own, right_low_a, right_low_b, right_high_a, right_high_b, table)
-    )
-    own_a, own_b, right_low_a, right_low_b, right_high_a, right_high_b, table = wave
+
+    tables = [info]
+    for step in (1, -1, 2):
+        tables.append(send(info, "left", step))
+    wave = lax.optimization_barrier((*own, right_low_a, right_low_b, right_high_a, right_high_b))
+    own_a, own_b, right_low_a, right_low_b, right_high_a, right_high_b = wave
     left_low_a = send(own_a, "left", 1)
     left_high_b = send(own_b, "left", -1)
     right_far_a = send(right_low_a, "right", 1)
@@ -236,27 +235,28 @@
     own_a, own_b, left_low_a, left_high_b, right_far_a, right_far_b = wave
     left_far_a = send(left_low_a, "left", 1)
     left_far_b = send(left_high_b, "left", -1)
+    own_a, own_b, left_far_a, left_far_b = lax.optimization_barrier(
+        (own_a, own_b, left_far_a, left_far_b)
+    )
     left_low_b = send(own_b, "left", 1)
     left_high_a = send(own_a, "left", -1)
 
     rights = (*own, right_low_a, right_low_b, right_high_a, right_high_b, right_far_a, right_far_b)
     vir_row, vir_col = e_vir.reshape(1, virt_count), e_vir.reshape(virt_count, 1)
-    place = lax.dynamic_index_in_dim(jnp.asarray(places()), device, 0, keepdims=False)
+    place = lax.dynamic_slice_in_dim(jnp.asarray(right_columns()), device * 4, 4)
 
     def partial(lefts, which, slots, dtype=jnp.bfloat16):
-        here = jnp.concatenate([place[:4]] + [place[4 + k : 5 + k] for k in which])
-        return partial_gamma(table, here, e_occ, lefts, slots, rights, vir_row, vir_col, dtype)
+        chosen = [tables[k] for k in which]
+        return partial_gamma(place, chosen, e_occ, lefts, slots, rights, vir_row, vir_col, dtype)
 
     low_a, high_b = partial((left_low_a, left_high_b), (1, 2), (0, 1))
-    sum_a, sum_b = partial(own, (0, 0), (0, 1), jnp.float32)
-    low_a, high_b, _, _ = lax.optimization_barrier((low_a, high_b, left_far_a, left_far_b))
     up_b = send(high_b, "left", 1)
     down_a = send(low_a, "left", -1)
+    sum_a, sum_b = partial(own, (0, 0), (0, 1), jnp.float32)
     far_a, far_b = partial((left_far_a, left_far_b), (3, 3), (0, 1))
-    low_b, high_a = partial((left_low_b, left_high_a), (1, 2), (1, 0))
-
     relay_a = send(far_a, "left", 1)
     relay_b = send(far_b, "left", -1)
+    low_b, high_a = partial((left_low_b, left_high_a), (1, 2), (1, 0))
     up_a = send(add(high_a, relay_a), "left", 1)
     down_b = send(add(low_b, relay_b), "left", -1)
 

time: 194 us -> 215 us (1.11)
  waiting for transfers between devices: 72.5 us -> 112 us
  blocking collectives: 27.5 us -> 0 us
  local copies, waits for them, and re-layouts: 13.6 us -> 19.4 us
  starting transfers between devices: 35.6 us -> 41.2 us
    ppermute x18 -> x21, waiting for transfers between devices: 41.3 us -> 80.5 us  [send(): return lax.ppermute(value, AXES, shifted(kind, step))]
    all_to_all x1 -> x0, blocking collectives: 27.5 us -> none  [local(): lax.all_to_all(jnp.broadcast_to(info, (16, 48)), 'col', split_axis=0, con...]
    unnamed x25 -> x43, local copies, waits for them, and re-layouts: 6.99 us -> 13.9 us
    all_to_all x1, starting transfers between devices: 10.9 us -> 13.8 us  [local(): lax.all_to_all(blocks, AXES, split_axis=0, concat_axis=0, tiled=True)]
    ppermute x18 -> x21, starting transfers between devices: 24.7 us -> 27.4 us  [send(): return lax.ppermute(value, AXES, shifted(kind, step))]
    concatenate x1 -> x0, other arithmetic: 2.66 us -> none  [partial(): here = jnp.concatenate([place[:4]] + [place[4 + k:5 + k] for k in which])]
    convert_element_type x2, other arithmetic: 0.55 us -> 3.03 us  [add(): return total.astype(jnp.bfloat16)]
  transfers between devices with their start and end apart: 19 -> 22, of which waited for: 7 -> 11; matrix products, arithmetic and copies ran while one was open for 6% -> 4% of each run, Pallas kernels for 15% -> 14%
where the time goes in v1:
time: 215 us
  waiting for transfers between devices  112 us (52%)
  starting transfers between devices  41.2 us (19%)
  Pallas kernels  38.6 us (18%)
  local copies, waits for them, and re-layouts  19.4 us (9%)
  other arithmetic  3.76 us (2%)
    ppermute x21, waiting for transfers between devices, send(): return lax.ppermute(value, AXES, shifted(kind, step))  80.5 us
    all_to_all x1, waiting for transfers between devices, local(): lax.all_to_all(blocks, AXES, split_axis=0, concat_axis=0, tiled=True)  31.2 us
    pallas_call x4, Pallas kernels, partial_gamma(): pl.pallas_call(functools.partial(pair_body, slots=slots), out_shape=(slab...  29.8 us
    ppermute x21, starting transfers between devices, send(): return lax.ppermute(value, AXES, shifted(kind, step))  27.4 us
    unnamed x43, local copies, waits for them, and re-layouts  13.9 us
    all_to_all x1, starting transfers between devices, local(): lax.all_to_all(blocks, AXES, split_axis=0, concat_axis=0, tiled=True)  13.8 us
    pallas_call x1, Pallas kernels, finish(): pl.pallas_call(finish_body, grid=(48 // rows,), out_shape=jax.ShapeDtypeS...  4.76 us
  transfers between devices with their start and end apart: 22, of which 11 were waited for; matrix products, arithmetic and copies ran while one was open for 4% of the time, Pallas kernels for 14%

profile of v1, /device:TPU:1, one launch (start us, length us, event | category | flops | bytes accessed | tf_op | source)
XLA Modules:
  0.0 214.8 jit_solution(6934247493121058626)
XLA Ops:
  0.0 1.8 slice_bitcast_fusion
  1.8 2.1 collective-permute-start
  5.1 1.5 collective-permute-start.2
  6.7 12.3 %collective-permute-done.refs_2_ = bf16[384,1536]{1,0:T(8,128)(2,1)S(1)} collective-permute-done((bf16[384,1536]{1,0:T(8,128)(2,1)S(1)}, bf16[384,1536]{1,0:T(8,128)(2,1)S(1)}, u32[]{:S(2)}, u32[]{:S(2)}) %collective-permute-start) | collective-permute-done | bytes 1179680 | tf_op jit(solution)/shard_map/ppermute | solution.py:28
  19.1 12.6 %collective-permute-done.1.refs_3_ = bf16[384,1536]{1,0:T(8,128)(2,1)S(1)} collective-permute-done((bf16[384,1536]{1,0:T(8,128)(2,1)S(1)}, bf16[384,1536]{1,0:T(8,128)(2,1)S(1)}, u32[]{:S(2)}, u32[]{:S(2)}) %collective-permute-start.1) | collective-permute-done | bytes 1179680 | tf_op jit(solution)/shard_map/ppermute | solution.py:28
  34.0 2.4 %collective-permute-start.7 = (bf16[384,1536]{1,0:T(8,128)(2,1)S(1)}, bf16[384,1536]{1,0:T(8,128)(2,1)S(1)}, u32[]{:S(2)}, u32[]{:S(2)}) collective-permute-start(bf16[384,1536]{1,0:T(8,128)(2,1)S(1)} %collective-permute-done.3.refs_5_), channel_id=1, source_target_pairs={{0,12},{1,13},{2,14},{3,15},{4,0},{5,1},{6,2},{7,3},{8,4},{9,5},{1... | collective-permute-start | bytes 3538952 | tf_op jit(solution)/shard_map/ppermute | solution.py:28
  37.5 1.5 collective-permute-start.4
  39.0 2.4 %collective-permute-start.5 = (bf16[384,1536]{1,0:T(8,128)(2,1)S(1)}, bf16[384,1536]{1,0:T(8,128)(2,1)}, u32[]{:S(2)}, u32[]{:S(2)}) collective-permute-start(bf16[384,1536]{1,0:T(8,128)(2,1)S(1)} %get-tuple-element.43.left_b.refs_1_), channel_id=1, source_target_pairs={{0,3},{1,0},{2,1},{3,2},{4,7},{5,4},{6,5},{7,6},{8,11},{9,8},{10,9... | collective-permute-start | bytes 3538952 | tf_op jit(solution)/shard_map/ppermute | solution.py:28
  41.4 14.4 %collective-permute-done.6.refs_6_ = bf16[384,1536]{1,0:T(8,128)(2,1)S(1)} collective-permute-done((bf16[384,1536]{1,0:T(8,128)(2,1)S(1)}, bf16[384,1536]{1,0:T(8,128)(2,1)S(1)}, u32[]{:S(2)}, u32[]{:S(2)}) %collective-permute-start.6) | collective-permute-done | bytes 1179680 | tf_op jit(solution)/shard_map/ppermute | solution.py:28
  57.9 7.9 %collective-permute-done.4.left_a = bf16[384,1536]{1,0:T(8,128)(2,1)} collective-permute-done((bf16[384,1536]{1,0:T(8,128)(2,1)S(1)}, bf16[384,1536]{1,0:T(8,128)(2,1)}, u32[]{:S(2)}, u32[]{:S(2)}) %collective-permute-start.4) | collective-permute-done | bytes 1179680 | tf_op jit(solution)/shard_map/ppermute | solution.py:28
  66.1 2.6 %collective-permute-start.11 = (bf16[384,1536]{1,0:T(8,128)(2,1)}, bf16[384,1536]{1,0:T(8,128)(2,1)}, u32[]{:S(2)}, u32[]{:S(2)}) collective-permute-start(bf16[384,1536]{1,0:T(8,128)(2,1)} %collective-permute-done.5.left_b), channel_id=1, source_target_pairs={{0,3},{1,0},{2,1},{3,2},{4,7},{5,4},{6,5},{7,6},{8,11},{9,8},{10,9... | collective-permute-start | bytes 3538952 | tf_op jit(solution)/shard_map/ppermute | solution.py:28
  70.8 1.5 reshape.24.refs_9_
  73.7 9.2 %collective-permute-done.10.left_a = bf16[384,1536]{1,0:T(8,128)(2,1)} collective-permute-done((bf16[384,1536]{1,0:T(8,128)(2,1)}, bf16[384,1536]{1,0:T(8,128)(2,1)}, u32[]{:S(2)}, u32[]{:S(2)}) %collective-permute-start.10) | collective-permute-done | bytes 1179680 | tf_op jit(solution)/shard_map/ppermute | solution.py:28
  83.8 1.8 collective-permute-start.13
  85.6 1.3 copy-done.1
  86.9 1.3 copy-done.4
  88.2 1.3 copy-done.7
  92.9 9.1 %shard_map.75 = (bf16[384,1536]{1,0:T(8,128)(2,1)S(1)}, bf16[384,1536]{1,0:T(8,128)(2,1)S(1)}) custom-call(s32[4]{0:T(128)S(1)} %dynamic_slice.3.place, s32[1,48]{1,0:T(1,128)S(1)} %collective-permute-done.14.table_a.table_b, s32[1,48]{1,0:T(1,128)S(1)} %collective-permute-done.14.table_a.table_b, f32[256]{0:T(256)S(1)} %copy-done.17, ...), custom_call_target="tpu_custom_call" | custom-call | tf_op jit(solution)/shard_map/pallas_call | solution.py:96
  102.1 1.5 collective-permute-start.15
  103.6 15.2 %collective-permute-done.8.table_a = s32[1,48]{1,0:T(1,128)S(1)} collective-permute-done((s32[1,48]{1,0:T(1,128)S(1)}, s32[1,48]{1,0:T(1,128)S(1)}, u32[]{:S(2)}, u32[]{:S(2)}) %collective-permute-start.8) | collective-permute-done | bytes 224 | tf_op jit(solution)/shard_map/ppermute | solution.py:28
  119.3 2.2 %collective-permute-done.9.table_b = s32[1,48]{1,0:T(1,128)S(1)} collective-permute-done((s32[1,48]{1,0:T(1,128)S(1)}, s32[1,48]{1,0:T(1,128)S(1)}, u32[]{:S(2)}, u32[]{:S(2)}) %collective-permute-start.9) | collective-permute-done | bytes 224 | tf_op jit(solution)/shard_map/ppermute | solution.py:28
  121.5 9.1 %shard_map.76 = (bf16[384,1536]{1,0:T(8,128)(2,1)S(1)}, bf16[384,1536]{1,0:T(8,128)(2,1)S(1)}) custom-call(s32[4]{0:T(128)S(1)} %dynamic_slice.3.place, s32[1,48]{1,0:T(1,128)S(1)} %collective-permute-done.8.table_a, s32[1,48]{1,0:T(1,128)S(1)} %collective-permute-done.9.table_b, f32[256]{0:T(256)S(1)} %copy-done.17, ...), custom_call_target="tpu_custom_call" | custom-call | tf_op jit(solution)/shard_map/pallas_call | solution.py:96
  130.6 2.1 collective-permute-start.18
  132.8 2.1 shard_map.74
  134.9 2.7 %add_convert_fusion = bf16[384,1536]{1,0:T(8,128)(2,1)} fusion(bf16[384,1536]{1,0:T(8,128)(2,1)} %collective-permute-done.19, bf16[384,1536]{1,0:T(8,128)(2,1)S(1)} %get-tuple-element.51), kind=kLoop, calls=%fused_computation | loop fusion | flops 2359296 | bytes 3538944 | tf_op jit(solution)/shard_map/convert_element_type | solution.py:200
  137.7 4.5 %collective-permute-start.20 = (bf16[384,1536]{1,0:T(8,128)(2,1)}, bf16[384,1536]{1,0:T(8,128)(2,1)S(1)}, u32[]{:S(2)}, u32[]{:S(2)}) collective-permute-start(bf16[384,1536]{1,0:T(8,128)(2,1)} %add_convert_fusion), channel_id=1, source_target_pairs={{0,3},{1,0},{2,1},{3,2},{4,7},{5,4},{6,5},{7,6},{8,11},{9,8},{10,9... | collective-permute-start | bytes 3538952 | tf_op jit(solution)/shard_map/ppermute | solution.py:28
  144.1 9.5 %shard_map.73 = (f32[384,1536]{1,0:T(8,128)S(1)}, f32[384,1536]{1,0:T(8,128)S(1)}) custom-call(s32[4]{0:T(128)S(1)} %dynamic_slice.3.place, s32[1,48]{1,0:T(1,128)S(1)} %pad_add_fusion.table_a.table_b, s32[1,48]{1,0:T(1,128)S(1)} %pad_add_fusion.table_a.table_b, f32[256]{0:T(256)S(1)} %copy-done.17, bf16[384,1536]{1,0:T(8,128)(2,1)S(1)} %get-tuple-element.44.left_a.refs_0_, ...), custom_call_target="tpu_custom_call" | custom-call | tf_op jit(solution)/shard_map/pallas_call | solution.py:96
  153.6 5.4 %collective-permute-done.20.down_b = bf16[384,1536]{1,0:T(8,128)(2,1)S(1)} collective-permute-done((bf16[384,1536]{1,0:T(8,128)(2,1)}, bf16[384,1536]{1,0:T(8,128)(2,1)S(1)}, u32[]{:S(2)}, u32[]{:S(2)}) %collective-permute-start.20) | collective-permute-done | bytes 1179680 | tf_op jit(solution)/shard_map/ppermute | solution.py:28
  160.1 4.0 %pack.1 = bf16[128,24,384]{2,1,0:T(8,128)(2,1)} custom-call(f32[384,1536]{1,0:T(8,128)S(1)} %get-tuple-element.37.own_a, f32[384,1536]{1,0:T(8,128)S(1)} %get-tuple-element.38.own_b, bf16[384,1536]{1,0:T(8,128)(2,1)S(1)} %collective-permute-done.16.up_a, bf16[384,1536]{1,0:T(8,128)(2,1)S(1)} %collective-permute-done.17.down_a, ...), custom_call_target="tpu_custom_call" | custom-call | tf_op jit(solution)/shard_map/pack/pallas_call | solution.py:140
  164.1 13.8 %all-to-all-start = ((bf16[128,24,384]{2,1,0:T(8,128)(2,1)}), bf16[128,24,384]{2,1,0:T(8,128)(2,1)S(1)}, u32[]{:S(2)}, u32[]{:S(2)}) async-start(bf16[128,24,384]{2,1,0:T(8,128)(2,1)} %pack.1), calls=%async_computation | async-start | bytes 4718592 | tf_op jit(solution)/shard_map/all_to_all | solution.py:264
  178.8 31.2 %all-to-all-done = bf16[128,24,384]{2,1,0:T(8,128)(2,1)S(1)} async-done(((bf16[128,24,384]{2,1,0:T(8,128)(2,1)}), bf16[128,24,384]{2,1,0:T(8,128)(2,1)S(1)}, u32[]{:S(2)}, u32[]{:S(2)}) %all-to-all-start) | async-done | bytes 2359328 | tf_op jit(solution)/shard_map/all_to_all | solution.py:264
  210.1 4.8 %finish.1 = bf16[48,96,768]{2,1,0:T(8,128)(2,1)} custom-call(bf16[3072,384]{1,0:T(8,128)(2,1)S(1)} %bitcast.12, bf16[768,256]{1,0:T(8,128)(2,1)S(1)} %bitcast.13), custom_call_target="tpu_custom_call" | custom-call | tf_op jit(solution)/shard_map/finish/pallas_call | solution.py:181
  (71 shorter events, 19.6 us)
Async XLA Ops:
  0.0 68.7 %copy-start.19 = (s32[1,16,2]{1,2,0:T(2,128)S(1)}, s32[1,16,2]{1,2,0:T(2,128)}, u32[]{:S(2)}) copy-start(s32[1,16,2]{1,2,0:T(2,128)} %param.11) | copy-start | bytes 388
  0.0 85.6 %copy-start.17 = (f32[256]{0:T(256)S(1)}, f32[256]{0:T(256)}, u32[]{:S(2)}) copy-start(f32[256]{0:T(256)} %energies.7) | copy-start | bytes 3076
  1.8 17.3 %collective-permute-start = (bf16[384,1536]{1,0:T(8,128)(2,1)S(1)}, bf16[384,1536]{1,0:T(8,128)(2,1)S(1)}, u32[]{:S(2)}, u32[]{:S(2)}) collective-permute-start(bf16[384,1536]{1,0:T(8,128)(2,1)S(1)} %get-tuple-element.44.left_a.refs_0_), channel_id=1, source_target_pairs={{0,4},{1,5},{2,6},{3,7},{4,8},{5,9},{6,10},{7,11},{8,12},{9,13},{1... | collective-permute-start | bytes 3538952 | tf_op jit(solution)/shard_map/ppermute | solution.py:28
  3.9 27.8 %collective-permute-start.1 = (bf16[384,1536]{1,0:T(8,128)(2,1)S(1)}, bf16[384,1536]{1,0:T(8,128)(2,1)S(1)}, u32[]{:S(2)}, u32[]{:S(2)}) collective-permute-start(bf16[384,1536]{1,0:T(8,128)(2,1)S(1)} %get-tuple-element.43.left_b.refs_1_), channel_id=1, source_target_pairs={{0,4},{1,5},{2,6},{3,7},{4,8},{5,9},{6,10},{7,11},{8,12},{9,13},{1... | collective-permute-start | bytes 3538952 | tf_op jit(solution)/shard_map/ppermute | solution.py:28
  5.1 27.6 %collective-permute-start.2 = (bf16[384,1536]{1,0:T(8,128)(2,1)S(1)}, bf16[384,1536]{1,0:T(8,128)(2,1)S(1)}, u32[]{:S(2)}, u32[]{:S(2)}) collective-permute-start(bf16[384,1536]{1,0:T(8,128)(2,1)S(1)} %get-tuple-element.44.left_a.refs_0_), channel_id=1, source_target_pairs={{0,12},{1,13},{2,14},{3,15},{4,0},{5,1},{6,2},{7,3},{8,4},{9,5},{1... | collective-permute-start | bytes 3538952 | tf_op jit(solution)/shard_map/ppermute | solution.py:28
  6.6 27.2 %collective-permute-start.3 = (bf16[384,1536]{1,0:T(8,128)(2,1)S(1)}, bf16[384,1536]{1,0:T(8,128)(2,1)S(1)}, u32[]{:S(2)}, u32[]{:S(2)}) collective-permute-start(bf16[384,1536]{1,0:T(8,128)(2,1)S(1)} %get-tuple-element.43.left_b.refs_1_), channel_id=1, source_target_pairs={{0,12},{1,13},{2,14},{3,15},{4,0},{5,1},{6,2},{7,3},{8,4},{9,5},{1... | collective-permute-start | bytes 3538952 | tf_op jit(solution)/shard_map/ppermute | solution.py:28
  33.8 22.1 %collective-permute-start.6 = (bf16[384,1536]{1,0:T(8,128)(2,1)S(1)}, bf16[384,1536]{1,0:T(8,128)(2,1)S(1)}, u32[]{:S(2)}, u32[]{:S(2)}) collective-permute-start(bf16[384,1536]{1,0:T(8,128)(2,1)S(1)} %collective-permute-done.refs_2_), channel_id=1, source_target_pairs={{0,4},{1,5},{2,6},{3,7},{4,8},{5,9},{6,10},{7,11},{8,12},{9,13},{1... | collective-permute-start | bytes 3538952 | tf_op jit(solution)/shard_map/ppermute | solution.py:28
  34.0 22.8 %collective-permute-start.7 = (bf16[384,1536]{1,0:T(8,128)(2,1)S(1)}, bf16[384,1536]{1,0:T(8,128)(2,1)S(1)}, u32[]{:S(2)}, u32[]{:S(2)}) collective-permute-start(bf16[384,1536]{1,0:T(8,128)(2,1)S(1)} %collective-permute-done.3.refs_5_), channel_id=1, source_target_pairs={{0,12},{1,13},{2,14},{3,15},{4,0},{5,1},{6,2},{7,3},{8,4},{9,5},{1... | collective-permute-start | bytes 3538952 | tf_op jit(solution)/shard_map/ppermute | solution.py:28
  37.5 28.3 %collective-permute-start.4 = (bf16[384,1536]{1,0:T(8,128)(2,1)S(1)}, bf16[384,1536]{1,0:T(8,128)(2,1)}, u32[]{:S(2)}, u32[]{:S(2)}) collective-permute-start(bf16[384,1536]{1,0:T(8,128)(2,1)S(1)} %get-tuple-element.44.left_a.refs_0_), channel_id=1, source_target_pairs={{0,1},{1,2},{2,3},{3,0},{4,5},{5,6},{6,7},{7,4},{8,9},{9,10},{10,1... | collective-permute-start | bytes 3538952 | tf_op jit(solution)/shard_map/ppermute | solution.py:28
  39.0 26.9 %collective-permute-start.5 = (bf16[384,1536]{1,0:T(8,128)(2,1)S(1)}, bf16[384,1536]{1,0:T(8,128)(2,1)}, u32[]{:S(2)}, u32[]{:S(2)}) collective-permute-start(bf16[384,1536]{1,0:T(8,128)(2,1)S(1)} %get-tuple-element.43.left_b.refs_1_), channel_id=1, source_target_pairs={{0,3},{1,0},{2,1},{3,2},{4,7},{5,4},{6,5},{7,6},{8,11},{9,8},{10,9... | collective-permute-start | bytes 3538952 | tf_op jit(solution)/shard_map/ppermute | solution.py:28
  65.9 17.0 %collective-permute-start.10 = (bf16[384,1536]{1,0:T(8,128)(2,1)}, bf16[384,1536]{1,0:T(8,128)(2,1)}, u32[]{:S(2)}, u32[]{:S(2)}) collective-permute-start(bf16[384,1536]{1,0:T(8,128)(2,1)} %collective-permute-done.4.left_a), channel_id=1, source_target_pairs={{0,1},{1,2},{2,3},{3,0},{4,5},{5,6},{6,7},{7,4},{8,9},{9,10},{10,1... | collective-permute-start | bytes 3538952 | tf_op jit(solution)/shard_map/ppermute | solution.py:28
  66.1 16.8 %collective-permute-start.11 = (bf16[384,1536]{1,0:T(8,128)(2,1)}, bf16[384,1536]{1,0:T(8,128)(2,1)}, u32[]{:S(2)}, u32[]{:S(2)}) collective-permute-start(bf16[384,1536]{1,0:T(8,128)(2,1)} %collective-permute-done.5.left_b), channel_id=1, source_target_pairs={{0,3},{1,0},{2,1},{3,2},{4,7},{5,4},{6,5},{7,6},{8,11},{9,8},{10,9... | collective-permute-start | bytes 3538952 | tf_op jit(solution)/shard_map/ppermute | solution.py:28
  69.6 16.0 %collective-permute-start.14 = (s32[1,48]{1,0:T(1,128)S(1)}, s32[1,48]{1,0:T(1,128)S(1)}, u32[]{:S(2)}, u32[]{:S(2)}) collective-permute-start(s32[1,48]{1,0:T(1,128)S(1)} %pad_add_fusion.table_a.table_b), channel_id=1, source_target_pairs={{0,2},{1,3},{2,0},{3,1},{4,6},{5,7},{6,4},{7,5},{8,10},{9,11},{10,... | collective-permute-start | bytes 584 | tf_op jit(solution)/shard_map/ppermute | solution.py:28
  82.9 47.7 %collective-permute-start.12 = (bf16[384,1536]{1,0:T(8,128)(2,1)S(1)}, bf16[384,1536]{1,0:T(8,128)(2,1)S(1)}, u32[]{:S(2)}, u32[]{:S(2)}) collective-permute-start(bf16[384,1536]{1,0:T(8,128)(2,1)S(1)} %get-tuple-element.43.left_b.refs_1_), channel_id=1, source_target_pairs={{0,1},{1,2},{2,3},{3,0},{4,5},{5,6},{6,7},{7,4},{8,9},{9,10},{10,1... | collective-permute-start | bytes 3538952 | tf_op jit(solution)/shard_map/ppermute | solution.py:28
  83.8 49.0 %collective-permute-start.13 = (bf16[384,1536]{1,0:T(8,128)(2,1)S(1)}, bf16[384,1536]{1,0:T(8,128)(2,1)S(1)}, u32[]{:S(2)}, u32[]{:S(2)}) collective-permute-start(bf16[384,1536]{1,0:T(8,128)(2,1)S(1)} %get-tuple-element.44.left_a.refs_0_), channel_id=1, source_target_pairs={{0,3},{1,0},{2,1},{3,2},{4,7},{5,4},{6,5},{7,6},{8,11},{9,8},{10,9... | collective-permute-start | bytes 3538952 | tf_op jit(solution)/shard_map/ppermute | solution.py:28
  85.6 1.3 copy-start.1
  102.0 32.9 %collective-permute-start.19 = (bf16[384,1536]{1,0:T(8,128)(2,1)S(1)}, bf16[384,1536]{1,0:T(8,128)(2,1)}, u32[]{:S(2)}, u32[]{:S(2)}) collective-permute-start(bf16[384,1536]{1,0:T(8,128)(2,1)S(1)} %get-tuple-element.52), channel_id=1, source_target_pairs={{0,3},{1,0},{2,1},{3,2},{4,7},{5,4},{6,5},{7,6},{8,11},{9,8},{10,9... | collective-permute-start | bytes 3538952 | tf_op jit(solution)/shard_map/ppermute | solution.py:28
  102.1 40.0 %collective-permute-start.15 = (bf16[384,1536]{1,0:T(8,128)(2,1)S(1)}, bf16[384,1536]{1,0:T(8,128)(2,1)S(1)}, u32[]{:S(2)}, u32[]{:S(2)}) collective-permute-start(bf16[384,1536]{1,0:T(8,128)(2,1)S(1)} %get-tuple-element.48), channel_id=1, source_target_pairs={{0,1},{1,2},{2,3},{3,0},{4,5},{5,6},{6,7},{7,4},{8,9},{9,10},{10,1... | collective-permute-start | bytes 3538952 | tf_op jit(solution)/shard_map/ppermute | solution.py:28
  103.6 15.2 %collective-permute-start.8 = (s32[1,48]{1,0:T(1,128)S(1)}, s32[1,48]{1,0:T(1,128)S(1)}, u32[]{:S(2)}, u32[]{:S(2)}) collective-permute-start(s32[1,48]{1,0:T(1,128)S(1)} %pad_add_fusion.table_a.table_b), channel_id=1, source_target_pairs={{0,1},{1,2},{2,3},{3,0},{4,5},{5,6},{6,7},{7,4},{8,9},{9,10},{10,1... | collective-permute-start | bytes 584 | tf_op jit(solution)/shard_map/ppermute | solution.py:28
  118.7 2.7 %collective-permute-start.9 = (s32[1,48]{1,0:T(1,128)S(1)}, s32[1,48]{1,0:T(1,128)S(1)}, u32[]{:S(2)}, u32[]{:S(2)}) collective-permute-start(s32[1,48]{1,0:T(1,128)S(1)} %pad_add_fusion.table_a.table_b), channel_id=1, source_target_pairs={{0,3},{1,0},{2,1},{3,2},{4,7},{5,4},{6,5},{7,6},{8,11},{9,8},{10,9... | collective-permute-start | bytes 584 | tf_op jit(solution)/shard_map/ppermute | solution.py:28
  130.5 23.1 %collective-permute-start.17 = (bf16[384,1536]{1,0:T(8,128)(2,1)S(1)}, bf16[384,1536]{1,0:T(8,128)(2,1)S(1)}, u32[]{:S(2)}, u32[]{:S(2)}) collective-permute-start(bf16[384,1536]{1,0:T(8,128)(2,1)S(1)} %get-tuple-element.49), channel_id=1, source_target_pairs={{0,3},{1,0},{2,1},{3,2},{4,7},{5,4},{6,5},{7,6},{8,11},{9,8},{10,9... | collective-permute-start | bytes 3538952 | tf_op jit(solution)/shard_map/ppermute | solution.py:28
  130.6 23.0 %collective-permute-start.18 = (bf16[384,1536]{1,0:T(8,128)(2,1)S(1)}, bf16[384,1536]{1,0:T(8,128)(2,1)S(1)}, u32[]{:S(2)}, u32[]{:S(2)}) collective-permute-start(bf16[384,1536]{1,0:T(8,128)(2,1)S(1)} %get-tuple-element.50), channel_id=1, source_target_pairs={{0,1},{1,2},{2,3},{3,0},{4,5},{5,6},{6,7},{7,4},{8,9},{9,10},{10,1... | collective-permute-start | bytes 3538952 | tf_op jit(solution)/shard_map/ppermute | solution.py:28
  134.9 8.0 %copy-start.11 = (bf16[384,1536]{1,0:T(8,128)(2,1)S(1)}, bf16[384,1536]{1,0:T(8,128)(2,1)}, u32[]{:S(2)}) copy-start(bf16[384,1536]{1,0:T(8,128)(2,1)} %copy-done.9) | copy-start | bytes 3538948
  134.9 8.0 %copy-start.14 = (bf16[384,1536]{1,0:T(8,128)(2,1)S(1)}, bf16[384,1536]{1,0:T(8,128)(2,1)}, u32[]{:S(2)}) copy-start(bf16[384,1536]{1,0:T(8,128)(2,1)} %copy-done.12) | copy-start | bytes 3538948
  134.9 8.0 %copy-start.16 = (f32[384,1]{1,0:T(8,128)S(1)}, f32[384,1]{1,0:T(8,128)}, u32[]{:S(2)}) copy-start(f32[384,1]{1,0:T(8,128)} %reshape.24.refs_9_) | copy-start | bytes 4612
  137.7 21.4 %collective-permute-start.20 = (bf16[384,1536]{1,0:T(8,128)(2,1)}, bf16[384,1536]{1,0:T(8,128)(2,1)S(1)}, u32[]{:S(2)}, u32[]{:S(2)}) collective-permute-start(bf16[384,1536]{1,0:T(8,128)(2,1)} %add_convert_fusion), channel_id=1, source_target_pairs={{0,3},{1,0},{2,1},{3,2},{4,7},{5,4},{6,5},{7,6},{8,11},{9,8},{10,9... | collective-permute-start | bytes 3538952 | tf_op jit(solution)/shard_map/ppermute | solution.py:28
  142.1 1.3 copy-start.2
  142.1 1.6 copy-start.5
  142.1 2.0 copy-start.8
  142.4 17.7 %collective-permute-start.16 = (bf16[384,1536]{1,0:T(8,128)(2,1)S(1)}, bf16[384,1536]{1,0:T(8,128)(2,1)S(1)}, u32[]{:S(2)}, u32[]{:S(2)}) collective-permute-start(bf16[384,1536]{1,0:T(8,128)(2,1)S(1)} %add_convert_fusion.1), channel_id=1, source_target_pairs={{0,1},{1,2},{2,3},{3,0},{4,5},{5,6},{6,7},{7,4},{8,9},{9,10},{10,1... | collective-permute-start | bytes 3538952 | tf_op jit(solution)/shard_map/ppermute | solution.py:28
  164.1 13.8 %copy-start.18 = (bf16[768,256]{1,0:T(8,128)(2,1)S(1)}, bf16[768,256]{1,0:T(8,128)(2,1)}, u32[]{:S(2)}) copy-start(bf16[768,256]{1,0:T(8,128)(2,1)} %param.10) | copy-start | bytes 1179652
  164.1 46.0 %all-to-all-start = ((bf16[128,24,384]{2,1,0:T(8,128)(2,1)}), bf16[128,24,384]{2,1,0:T(8,128)(2,1)S(1)}, u32[]{:S(2)}, u32[]{:S(2)}) async-start(bf16[128,24,384]{2,1,0:T(8,128)(2,1)} %pack.1), calls=%async_computation | async-start | bytes 4718592 | tf_op jit(solution)/shard_map/all_to_all | solution.py:264
  (10 other events, 11.1 us)

commit v2 on v1

--- a/solution.py
+++ b/solution.py
@@ -2,7 +2,6 @@
 
 import jax
 import jax.numpy as jnp
-import numpy as np
 from jax import lax
 from jax.experimental import pallas as pl
 from jax.experimental.pallas import tpu as pltpu
@@ -28,26 +27,36 @@
     return lax.ppermute(value, AXES, shifted(kind, step))
 
 
-def pair_body(place, table_a, table_b, energies, left_a, left_b, *refs, slots):
-    rights = refs[:8]
-    vir_row, vir_col, out_a, out_b = refs[8:12]
-    left_buf, right_buf, gamma, left_sem, right_sem = refs[12:]
+def pair_body(device, table_a, table_b, energies, own, *refs, slots):
+    lefts, rights = refs[:2], refs[2:8]
+    levels, out_a, out_b = refs[8:11]
+    left_buf, right_buf, gamma, across, left_sem, right_sem = refs[11:]
     outs = (out_a, out_b)
+    rights = (own.at[0], own.at[1], *rights)
+    if lefts[0].shape == own.shape:
+        lefts = (own.at[0], own.at[1])
+    col = device[0] % 16
+    z, x = col // SIDE, col % SIDE
+    even = device[0] // 16 % 2 == 0
+    columns = [
+        jnp.where(even, (z + d) % SIDE * SIDE + x, z * SIDE + (x + d) % SIDE) for d in (0, 3, 1, 2)
+    ]
 
     def entry(m):
-        side, right = m // 4, place[m % 4]
-        at_a, at_b = (lambda k: table_a[0, k]), (lambda k: table_b[0, k])
+        side, n = m // 4, m % 4
+        right = jnp.where(
+            n < 2, jnp.where(n == 0, columns[0], columns[1]), jnp.where(n == 2, columns[2], columns[3])
+        )
 
         def pick(k):
-            return jnp.where(side == 0, at_a(k), at_b(k))
+            return jnp.where(side == 0, table_a[0, k], table_b[0, k])
 
         first, second, live = pick(right * 2), pick(right * 2 + 1), pick(32 + right)
         wanted = jnp.where(side == 0, slots[0], slots[1])
         return first, second, (live > 0) & (first % 2 == wanted)
 
     left_copies = [
-        pltpu.make_async_copy(left, left_buf.at[s], left_sem.at[s])
-        for s, left in enumerate((left_a, left_b))
+        pltpu.make_async_copy(left, left_buf.at[s], left_sem.at[s]) for s, left in enumerate(lefts)
     ]
     for copy in left_copies:
         copy.start()
@@ -62,6 +71,8 @@
                 ).start()
 
     gamma[...] = jnp.zeros_like(gamma)
+    row = levels[...].reshape(1, levels.shape[-1])
+    across[...] = jnp.broadcast_to(row, across.shape).T
     for copy in left_copies:
         copy.wait()
 
@@ -76,7 +87,7 @@
                 left_buf[m // 4], right, (((1,), (1,)), ((), ())),
                 preferred_element_type=jnp.float32,
             )
-            denominator = energies[first] + energies[second] - vir_col[...] - vir_row[...]
+            denominator = energies[first] + energies[second] - across[...] - row
             weighted = ((2.0 * integrals - integrals.T) / denominator).astype(jnp.bfloat16)
             gamma[m // 4] += jnp.dot(weighted, right, preferred_element_type=jnp.float32)
 
@@ -87,8 +98,8 @@
         outs[s][...] = gamma[s].astype(outs[s].dtype)
 
 
-def partial_gamma(place, tables, energies, lefts, slots, rights, vir_row, vir_col, out_dtype):
-    virt, aux = lefts[0].shape
+def partial_gamma(device, tables, energies, own, lefts, slots, rights, levels, out_dtype):
+    virt, aux = own.shape[1:]
     slab = jax.ShapeDtypeStruct((virt, aux), out_dtype)
     hbm = pl.BlockSpec(memory_space=pltpu.HBM)
     smem = pl.BlockSpec(memory_space=pltpu.SMEM)
@@ -96,17 +107,18 @@
     return pl.pallas_call(
         functools.partial(pair_body, slots=slots),
         out_shape=(slab, slab),
-        in_specs=[smem, smem, smem, smem] + [hbm] * 10 + [vmem, vmem],
+        in_specs=[smem, smem, smem, smem] + [hbm] * 9 + [vmem],
         out_specs=(vmem, vmem),
         scratch_shapes=[
             pltpu.VMEM((2, virt, aux), jnp.bfloat16),
             pltpu.VMEM((8, virt, aux), jnp.bfloat16),
             pltpu.VMEM((2, virt, aux), jnp.float32),
+            pltpu.VMEM((virt, virt), jnp.float32),
             pltpu.SemaphoreType.DMA((2,)),
             pltpu.SemaphoreType.DMA((8,)),
         ],
         compiler_params=pltpu.CompilerParams(vmem_limit_bytes=40 << 20),
-    )(place, *tables, energies, *lefts, *rights, vir_row, vir_col)
+    )(device, *tables, energies, own, *lefts, *rights, levels)
 
 
 def pack_body(own_a, own_b, up_a, down_a, up_b, down_b, out, total, block):
@@ -200,63 +212,40 @@
     return total.astype(jnp.bfloat16)
 
 
-def right_columns():
-    rows = []
-    for row in range(8):
-        for z in range(SIDE):
-            for x in range(SIDE):
-                along_x = [z * SIDE + (x + d) % SIDE for d in (0, -1, 1, 2)]
-                along_z = [(z + d) % SIDE * SIDE + x for d in (0, -1, 1, 2)]
-                rows.append(along_z if row % 2 == 0 else along_x)
-    return np.array(rows, np.int32).reshape(-1)
-
-
 def local(b_three, e_occ, e_vir, c_occ, pair_list, pair_live):
-    _, virt_count, _ = b_three.shape
     device = lax.axis_index("row") * 16 + lax.axis_index("col")
-    own = (b_three[0], b_three[1])
-
-    right_low_a, right_low_b = send(own[0], "right", 1), send(own[1], "right", 1)
-    right_high_a, right_high_b = send(own[0], "right", -1), send(own[1], "right", -1)
+    own_a, own_b = b_three[0], b_three[1]
+
+    right_low_a = send(own_a, "right", 1)
+    right_high_b = send(own_b, "right", -1)
+    right_low_b = send(own_b, "right", 1)
+    right_high_a = send(own_a, "right", -1)
     info = jnp.concatenate([pair_list.reshape(1, 32), pair_live.reshape(1, 16)], 1)
-
-    tables = [info]
-    for step in (1, -1, 2):
-        tables.append(send(info, "left", step))
-    wave = lax.optimization_barrier((*own, right_low_a, right_low_b, right_high_a, right_high_b))
-    own_a, own_b, right_low_a, right_low_b, right_high_a, right_high_b = wave
-    left_low_a = send(own_a, "left", 1)
-    left_high_b = send(own_b, "left", -1)
+    tables = [info] + [send(info, "left", step) for step in (1, -1, 2)]
+    near_low_a = send(own_a, "left", 1)
+    near_high_b = send(own_b, "left", -1)
     right_far_a = send(right_low_a, "right", 1)
     right_far_b = send(right_high_b, "right", -1)
-    wave = lax.optimization_barrier(
-        (own_a, own_b, left_low_a, left_high_b, right_far_a, right_far_b)
-    )
-    own_a, own_b, left_low_a, left_high_b, right_far_a, right_far_b = wave
-    left_far_a = send(left_low_a, "left", 1)
-    left_far_b = send(left_high_b, "left", -1)
-    own_a, own_b, left_far_a, left_far_b = lax.optimization_barrier(
-        (own_a, own_b, left_far_a, left_far_b)
-    )
-    left_low_b = send(own_b, "left", 1)
-    left_high_a = send(own_a, "left", -1)
-
-    rights = (*own, right_low_a, right_low_b, right_high_a, right_high_b, right_far_a, right_far_b)
-    vir_row, vir_col = e_vir.reshape(1, virt_count), e_vir.reshape(virt_count, 1)
-    place = lax.dynamic_slice_in_dim(jnp.asarray(right_columns()), device * 4, 4)
+    far_a = send(near_low_a, "left", 1)
+    far_b = send(near_high_b, "left", -1)
+    late_low_b = send(own_b, "left", 1)
+    late_high_a = send(own_a, "left", -1)
+    rights = (right_low_a, right_low_b, right_high_a, right_high_b, right_far_a, right_far_b)
 
     def partial(lefts, which, slots, dtype=jnp.bfloat16):
         chosen = [tables[k] for k in which]
-        return partial_gamma(place, chosen, e_occ, lefts, slots, rights, vir_row, vir_col, dtype)
-
-    low_a, high_b = partial((left_low_a, left_high_b), (1, 2), (0, 1))
+        return partial_gamma(
+            device.reshape(1), chosen, e_occ, b_three, lefts, slots, rights, e_vir, dtype
+        )
+
+    low_a, high_b = partial((near_low_a, near_high_b), (1, 2), (0, 1))
     up_b = send(high_b, "left", 1)
     down_a = send(low_a, "left", -1)
-    sum_a, sum_b = partial(own, (0, 0), (0, 1), jnp.float32)
-    far_a, far_b = partial((left_far_a, left_far_b), (3, 3), (0, 1))
+    sum_a, sum_b = partial((b_three, b_three), (0, 0), (0, 1), jnp.float32)
+    far_a, far_b = partial((far_a, far_b), (3, 3), (0, 1))
     relay_a = send(far_a, "left", 1)
     relay_b = send(far_b, "left", -1)
-    low_b, high_a = partial((left_low_b, left_high_a), (1, 2), (1, 0))
+    low_b, high_a = partial((late_low_b, late_high_a), (1, 2), (1, 0))
     up_a = send(add(high_a, relay_a), "left", 1)
     down_b = send(add(low_b, relay_b), "left", -1)
 

time: 215 us -> 200 us (0.930)
  local copies, waits for them, and re-layouts: 19.4 us -> 7.94 us
  waiting for transfers between devices: 112 us -> 103 us
  starting transfers between devices: 41.2 us -> 46.6 us
    unnamed x43 -> x17, local copies, waits for them, and re-layouts: 13.9 us -> 3.3 us
    ppermute x21, waiting for transfers between devices: 80.5 us -> 71.5 us  [send(): return lax.ppermute(value, AXES, shifted(kind, step))]
    ppermute x21, starting transfers between devices: 27.4 us -> 35.6 us  [send(): return lax.ppermute(value, AXES, shifted(kind, step))]
    all_to_all x1, starting transfers between devices: 13.8 us -> 11.1 us  [local(): lax.all_to_all(blocks, AXES, split_axis=0, concat_axis=0, tiled=True)]
    reshape x2 -> x0, local copies, waits for them, and re-layouts: 2.17 us -> none  [the longest x1 1.48 us: local(): e_vir.reshape(virt_count, 1)]
  transfers between devices with their start and end apart: 22 -> 22, of which waited for: 11 -> 11; matrix products, arithmetic and copies ran while one was open for 4% -> 3% of each run, Pallas kernels for 14% -> 15%
where the time goes in v2:
time: 200 us
  waiting for transfers between devices  103 us (52%)
  starting transfers between devices  46.6 us (23%)
  Pallas kernels  38.1 us (19%)
  local copies, waits for them, and re-layouts  7.94 us (4%)
  other arithmetic  3.94 us (2%)
    ppermute x21, waiting for transfers between devices, send(): return lax.ppermute(value, AXES, shifted(kind, step))  71.5 us
    ppermute x21, starting transfers between devices, send(): return lax.ppermute(value, AXES, shifted(kind, step))  35.6 us
    all_to_all x1, waiting for transfers between devices, local(): lax.all_to_all(blocks, AXES, split_axis=0, concat_axis=0, tiled=True)  31.2 us
    pallas_call x4, Pallas kernels, partial_gamma(): pl.pallas_call(functools.partial(pair_body, slots=slots), out_shape=(slab...  29.2 us
    all_to_all x1, starting transfers between devices, local(): lax.all_to_all(blocks, AXES, split_axis=0, concat_axis=0, tiled=True)  11.1 us
    pallas_call x1, Pallas kernels, finish(): pl.pallas_call(finish_body, grid=(48 // rows,), out_shape=jax.ShapeDtypeS...  4.77 us
    pallas_call x1, Pallas kernels, pack(): pl.pallas_call(pack_body, out_shape=jax.ShapeDtypeStruct((128, 24, 384),...  4.14 us
  transfers between devices with their start and end apart: 22, of which 11 were waited for; matrix products, arithmetic and copies ran while one was open for 3% of the time, Pallas kernels for 15%

profile of v2, /device:TPU:1, one launch (start us, length us, event | category | flops | bytes accessed | tf_op | source)
XLA Modules:
  0.0 199.6 jit_solution(5225707709182421703)
XLA Ops:
  0.0 3.3 %slice_bitcast_fusion = (bf16[384,1536]{1,0:T(8,128)(2,1)}, bf16[384,1536]{1,0:T(8,128)(2,1)}) fusion(bf16[2,384,1536]{2,1,0:T(8,128)(2,1)} %own.7), kind=kLoop, calls=%fused_computation.2 | loop fusion | bytes 4718592 | tf_op jit(solution)/shard_map/squeeze | solution.py:217
  3.4 2.0 %collective-permute-start = (bf16[384,1536]{1,0:T(8,128)(2,1)}, bf16[384,1536]{1,0:T(8,128)(2,1)S(1)}, u32[]{:S(2)}, u32[]{:S(2)}) collective-permute-start(bf16[384,1536]{1,0:T(8,128)(2,1)} %get-tuple-element.22), channel_id=1, source_target_pairs={{0,4},{1,5},{2,6},{3,7},{4,8},{5,9},{6,10},{7,11},{8,12},{9,13},{1... | collective-permute-start | bytes 3538952 | tf_op jit(solution)/shard_map/ppermute | solution.py:27
  5.4 1.3 collective-permute-start.3
  8.8 3.8 %collective-permute-start.10 = (s32[1,48]{1,0:T(1,128)S(1)}, s32[1,48]{1,0:T(1,128)S(1)}, u32[]{:S(2)}, u32[]{:S(2)}) collective-permute-start(s32[1,48]{1,0:T(1,128)S(1)} %pad_add_fusion.table_a.table_b), channel_id=1, source_target_pairs={{0,2},{1,3},{2,0},{3,1},{4,6},{5,7},{6,4},{7,5},{8,10},{9,11},{10,... | collective-permute-start | bytes 584 | tf_op jit(solution)/shard_map/ppermute | solution.py:27
  13.5 3.1 %collective-permute-start.13 = (bf16[384,1536]{1,0:T(8,128)(2,1)}, bf16[384,1536]{1,0:T(8,128)(2,1)}, u32[]{:S(2)}, u32[]{:S(2)}) collective-permute-start(bf16[384,1536]{1,0:T(8,128)(2,1)} %get-tuple-element.21), channel_id=1, source_target_pairs={{0,3},{1,0},{2,1},{3,2},{4,7},{5,4},{6,5},{7,6},{8,11},{9,8},{10,9... | collective-permute-start | bytes 3538952 | tf_op jit(solution)/shard_map/ppermute | solution.py:27
  16.7 6.3 %collective-permute-done.refs_2_ = bf16[384,1536]{1,0:T(8,128)(2,1)S(1)} collective-permute-done((bf16[384,1536]{1,0:T(8,128)(2,1)}, bf16[384,1536]{1,0:T(8,128)(2,1)S(1)}, u32[]{:S(2)}, u32[]{:S(2)}) %collective-permute-start) | collective-permute-done | bytes 1179680 | tf_op jit(solution)/shard_map/ppermute | solution.py:27
  23.0 3.3 %collective-permute-start.2 = (bf16[384,1536]{1,0:T(8,128)(2,1)}, bf16[384,1536]{1,0:T(8,128)(2,1)}, u32[]{:S(2)}, u32[]{:S(2)}) collective-permute-start(bf16[384,1536]{1,0:T(8,128)(2,1)} %get-tuple-element.22), channel_id=1, source_target_pairs={{0,12},{1,13},{2,14},{3,15},{4,0},{5,1},{6,2},{7,3},{8,4},{9,5},{1... | collective-permute-start | bytes 3538952 | tf_op jit(solution)/shard_map/ppermute | solution.py:27
  26.3 19.8 %collective-permute-done.1.refs_3_ = bf16[384,1536]{1,0:T(8,128)(2,1)S(1)} collective-permute-done((bf16[384,1536]{1,0:T(8,128)(2,1)}, bf16[384,1536]{1,0:T(8,128)(2,1)S(1)}, u32[]{:S(2)}, u32[]{:S(2)}) %collective-permute-start.1) | collective-permute-done | bytes 1179680 | tf_op jit(solution)/shard_map/ppermute | solution.py:27
  47.1 1.6 collective-permute-start.5
  48.6 1.6 collective-permute-start.12
  50.3 2.2 %collective-permute-start.14 = (bf16[384,1536]{1,0:T(8,128)(2,1)}, bf16[384,1536]{1,0:T(8,128)(2,1)}, u32[]{:S(2)}, u32[]{:S(2)}) collective-permute-start(bf16[384,1536]{1,0:T(8,128)(2,1)} %collective-permute-done.13.refs_1_), channel_id=1, source_target_pairs={{0,3},{1,0},{2,1},{3,2},{4,7},{5,4},{6,5},{7,6},{8,11},{9,8},{10,9... | collective-permute-start | bytes 3538952 | tf_op jit(solution)/shard_map/ppermute | solution.py:27
  52.5 8.7 %collective-permute-done.4.refs_6_ = bf16[384,1536]{1,0:T(8,128)(2,1)} collective-permute-done((bf16[384,1536]{1,0:T(8,128)(2,1)S(1)}, bf16[384,1536]{1,0:T(8,128)(2,1)}, u32[]{:S(2)}, u32[]{:S(2)}) %collective-permute-start.4) | collective-permute-done | bytes 1179680 | tf_op jit(solution)/shard_map/ppermute | solution.py:27
  61.2 7.8 %collective-permute-start.9 = (bf16[384,1536]{1,0:T(8,128)(2,1)}, bf16[384,1536]{1,0:T(8,128)(2,1)S(1)}, u32[]{:S(2)}, u32[]{:S(2)}) collective-permute-start(bf16[384,1536]{1,0:T(8,128)(2,1)} %get-tuple-element.22), channel_id=1, source_target_pairs={{0,3},{1,0},{2,1},{3,2},{4,7},{5,4},{6,5},{7,6},{8,11},{9,8},{10,9... | collective-permute-start | bytes 3538952 | tf_op jit(solution)/shard_map/ppermute | solution.py:27
  69.0 4.4 %collective-permute-done.12.refs_0_ = bf16[384,1536]{1,0:T(8,128)(2,1)} collective-permute-done((bf16[384,1536]{1,0:T(8,128)(2,1)}, bf16[384,1536]{1,0:T(8,128)(2,1)}, u32[]{:S(2)}, u32[]{:S(2)}) %collective-permute-start.12) | collective-permute-done | bytes 1179680 | tf_op jit(solution)/shard_map/ppermute | solution.py:27
  73.5 4.8 %collective-permute-done.14.refs_1_ = bf16[384,1536]{1,0:T(8,128)(2,1)} collective-permute-done((bf16[384,1536]{1,0:T(8,128)(2,1)}, bf16[384,1536]{1,0:T(8,128)(2,1)}, u32[]{:S(2)}, u32[]{:S(2)}) %collective-permute-start.14) | collective-permute-done | bytes 1179680 | tf_op jit(solution)/shard_map/ppermute | solution.py:27
  79.5 9.0 %shard_map.66 = (bf16[384,1536]{1,0:T(8,128)(2,1)S(1)}, bf16[384,1536]{1,0:T(8,128)(2,1)S(1)}) custom-call(s32[1]{0:T(128)} %bitcast.device, s32[1,48]{1,0:T(1,128)S(1)} %collective-permute-done.10.table_a.table_b, s32[1,48]{1,0:T(1,128)S(1)} %collective-permute-done.10.table_a.table_b, f32[256]{0:T(256)S(1)} %copy-done.5, ...), custom_call_target="tpu_custom_call" | custom-call | tf_op jit(solution)/shard_map/pallas_call | solution.py:107
  88.6 1.3 collective-permute-start.19
  90.1 16.4 %collective-permute-done.6.table_a = s32[1,48]{1,0:T(1,128)S(1)} collective-permute-done((s32[1,48]{1,0:T(1,128)S(1)}, s32[1,48]{1,0:T(1,128)S(1)}, u32[]{:S(2)}, u32[]{:S(2)}) %collective-permute-start.6) | collective-permute-done | bytes 224 | tf_op jit(solution)/shard_map/ppermute | solution.py:27
  106.6 2.4 %collective-permute-done.7.table_b = s32[1,48]{1,0:T(1,128)S(1)} collective-permute-done((s32[1,48]{1,0:T(1,128)S(1)}, s32[1,48]{1,0:T(1,128)S(1)}, u32[]{:S(2)}, u32[]{:S(2)}) %collective-permute-start.7) | collective-permute-done | bytes 224 | tf_op jit(solution)/shard_map/ppermute | solution.py:27
  109.0 9.0 %shard_map.67 = (bf16[384,1536]{1,0:T(8,128)(2,1)S(1)}, bf16[384,1536]{1,0:T(8,128)(2,1)S(1)}) custom-call(s32[1]{0:T(128)} %bitcast.device, s32[1,48]{1,0:T(1,128)S(1)} %collective-permute-done.6.table_a, s32[1,48]{1,0:T(1,128)S(1)} %collective-permute-done.7.table_b, f32[256]{0:T(256)S(1)} %copy-done.5, bf16[2,384,1536]{2,1,0:T(8,128)(2,1)S(1)} %copy-done, ...), custom_call_target="tpu_custom_call" | custom-call | tf_op jit(solution)/shard_map/pallas_call | solution.py:107
  118.1 1.4 collective-permute-start.18
  119.6 2.2 %shard_map.65 = (bf16[384,1536]{1,0:T(8,128)(2,1)S(1)}, bf16[384,1536]{1,0:T(8,128)(2,1)S(1)}) custom-call(s32[1]{0:T(128)} %bitcast.device, s32[1,48]{1,0:T(1,128)S(1)} %collective-permute-done.6.table_a, s32[1,48]{1,0:T(1,128)S(1)} %collective-permute-done.7.table_b, f32[256]{0:T(256)S(1)} %copy-done.5, bf16[2,384,1536]{2,1,0:T(8,128)(2,1)S(1)} %copy-done, ...), custom_call_target="tpu_custom_call" | custom-call | tf_op jit(solution)/shard_map/pallas_call | solution.py:107
  121.8 1.6 add_convert_fusion
  123.4 5.0 %collective-permute-start.20 = (bf16[384,1536]{1,0:T(8,128)(2,1)S(1)}, bf16[384,1536]{1,0:T(8,128)(2,1)S(1)}, u32[]{:S(2)}, u32[]{:S(2)}) collective-permute-start(bf16[384,1536]{1,0:T(8,128)(2,1)S(1)} %add_convert_fusion), channel_id=1, source_target_pairs={{0,3},{1,0},{2,1},{3,2},{4,7},{5,4},{6,5},{7,6},{8,11},{9,8},{10,9... | collective-permute-start | bytes 3538952 | tf_op jit(solution)/shard_map/ppermute | solution.py:27
  128.4 1.7 add_convert_fusion.1
  130.1 8.9 %shard_map.64 = (f32[384,1536]{1,0:T(8,128)S(1)}, f32[384,1536]{1,0:T(8,128)S(1)}) custom-call(s32[1]{0:T(128)} %bitcast.device, s32[1,48]{1,0:T(1,128)S(1)} %pad_add_fusion.table_a.table_b, s32[1,48]{1,0:T(1,128)S(1)} %pad_add_fusion.table_a.table_b, f32[256]{0:T(256)S(1)} %copy-done.5, bf16[2,384,1536]{2,1,0:T(8,128)(2,1)S(1)} %copy-done, ...), custom_call_target="tpu_custom_call" | custom-call | tf_op jit(solution)/shard_map/pallas_call | solution.py:107
  139.1 7.0 %collective-permute-done.20.down_b = bf16[384,1536]{1,0:T(8,128)(2,1)S(1)} collective-permute-done((bf16[384,1536]{1,0:T(8,128)(2,1)S(1)}, bf16[384,1536]{1,0:T(8,128)(2,1)S(1)}, u32[]{:S(2)}, u32[]{:S(2)}) %collective-permute-start.20) | collective-permute-done | bytes 1179680 | tf_op jit(solution)/shard_map/ppermute | solution.py:27
  146.1 1.3 collective-permute-done.16.up_a
  147.4 4.1 %pack.1 = bf16[128,24,384]{2,1,0:T(8,128)(2,1)} custom-call(f32[384,1536]{1,0:T(8,128)S(1)} %get-tuple-element.13.own_a, f32[384,1536]{1,0:T(8,128)S(1)} %get-tuple-element.14.own_b, bf16[384,1536]{1,0:T(8,128)(2,1)S(1)} %collective-permute-done.16.up_a, bf16[384,1536]{1,0:T(8,128)(2,1)S(1)} %collective-permute-done.17.down_a, ...), custom_call_target="tpu_custom_call" | custom-call | tf_op jit(solution)/shard_map/pack/pallas_call | solution.py:152
  151.5 11.1 %all-to-all-start = ((bf16[128,24,384]{2,1,0:T(8,128)(2,1)}), bf16[128,24,384]{2,1,0:T(8,128)(2,1)S(1)}, u32[]{:S(2)}, u32[]{:S(2)}) async-start(bf16[128,24,384]{2,1,0:T(8,128)(2,1)} %pack.1), calls=%async_computation | async-start | bytes 4718592 | tf_op jit(solution)/shard_map/all_to_all | solution.py:253
  163.6 31.2 %all-to-all-done = bf16[128,24,384]{2,1,0:T(8,128)(2,1)S(1)} async-done(((bf16[128,24,384]{2,1,0:T(8,128)(2,1)}), bf16[128,24,384]{2,1,0:T(8,128)(2,1)S(1)}, u32[]{:S(2)}, u32[]{:S(2)}) %all-to-all-start) | async-done | bytes 2359328 | tf_op jit(solution)/shard_map/all_to_all | solution.py:253
  194.8 4.8 %finish.1 = bf16[48,96,768]{2,1,0:T(8,128)(2,1)} custom-call(bf16[3072,384]{1,0:T(8,128)(2,1)S(1)} %bitcast.13, bf16[768,256]{1,0:T(8,128)(2,1)S(1)} %bitcast.14), custom_call_target="tpu_custom_call" | custom-call | tf_op jit(solution)/shard_map/finish/pallas_call | solution.py:193
  (42 shorter events, 6.7 us)
Async XLA Ops:
  0.0 78.3 %copy-start.5 = (f32[256]{0:T(256)S(1)}, f32[256]{0:T(256)}, u32[]{:S(2)}) copy-start(f32[256]{0:T(256)} %energies.7) | copy-start | bytes 3076
  0.0 78.3 %copy-start.4 = (f32[384]{0:T(512)S(1)}, f32[384]{0:T(512)}, u32[]{:S(2)}) copy-start(f32[384]{0:T(512)} %refs_8_.7) | copy-start | bytes 4612
  0.0 78.3 %copy-start = (bf16[2,384,1536]{2,1,0:T(8,128)(2,1)S(1)}, bf16[2,384,1536]{2,1,0:T(8,128)(2,1)}, u32[]{:S(2)}) copy-start(bf16[2,384,1536]{2,1,0:T(8,128)(2,1)} %own.7) | copy-start | bytes 7077892
  3.4 19.6 %collective-permute-start = (bf16[384,1536]{1,0:T(8,128)(2,1)}, bf16[384,1536]{1,0:T(8,128)(2,1)S(1)}, u32[]{:S(2)}, u32[]{:S(2)}) collective-permute-start(bf16[384,1536]{1,0:T(8,128)(2,1)} %get-tuple-element.22), channel_id=1, source_target_pairs={{0,4},{1,5},{2,6},{3,7},{4,8},{5,9},{6,10},{7,11},{8,12},{9,13},{1... | collective-permute-start | bytes 3538952 | tf_op jit(solution)/shard_map/ppermute | solution.py:27
  5.4 20.9 %collective-permute-start.3 = (bf16[384,1536]{1,0:T(8,128)(2,1)}, bf16[384,1536]{1,0:T(8,128)(2,1)}, u32[]{:S(2)}, u32[]{:S(2)}) collective-permute-start(bf16[384,1536]{1,0:T(8,128)(2,1)} %get-tuple-element.21), channel_id=1, source_target_pairs={{0,12},{1,13},{2,14},{3,15},{4,0},{5,1},{6,2},{7,3},{8,4},{9,5},{1... | collective-permute-start | bytes 3538952 | tf_op jit(solution)/shard_map/ppermute | solution.py:27
  8.8 4.8 %collective-permute-start.10 = (s32[1,48]{1,0:T(1,128)S(1)}, s32[1,48]{1,0:T(1,128)S(1)}, u32[]{:S(2)}, u32[]{:S(2)}) collective-permute-start(s32[1,48]{1,0:T(1,128)S(1)} %pad_add_fusion.table_a.table_b), channel_id=1, source_target_pairs={{0,2},{1,3},{2,0},{3,1},{4,6},{5,7},{6,4},{7,5},{8,10},{9,11},{10,... | collective-permute-start | bytes 584 | tf_op jit(solution)/shard_map/ppermute | solution.py:27
  12.6 33.5 %collective-permute-start.1 = (bf16[384,1536]{1,0:T(8,128)(2,1)}, bf16[384,1536]{1,0:T(8,128)(2,1)S(1)}, u32[]{:S(2)}, u32[]{:S(2)}) collective-permute-start(bf16[384,1536]{1,0:T(8,128)(2,1)} %get-tuple-element.21), channel_id=1, source_target_pairs={{0,4},{1,5},{2,6},{3,7},{4,8},{5,9},{6,10},{7,11},{8,12},{9,13},{1... | collective-permute-start | bytes 3538952 | tf_op jit(solution)/shard_map/ppermute | solution.py:27
  12.6 36.1 %collective-permute-start.11 = (bf16[384,1536]{1,0:T(8,128)(2,1)}, bf16[384,1536]{1,0:T(8,128)(2,1)}, u32[]{:S(2)}, u32[]{:S(2)}) collective-permute-start(bf16[384,1536]{1,0:T(8,128)(2,1)} %get-tuple-element.22), channel_id=1, source_target_pairs={{0,1},{1,2},{2,3},{3,0},{4,5},{5,6},{6,7},{7,4},{8,9},{9,10},{10,1... | collective-permute-start | bytes 3538952 | tf_op jit(solution)/shard_map/ppermute | solution.py:27
  13.5 36.8 %collective-permute-start.13 = (bf16[384,1536]{1,0:T(8,128)(2,1)}, bf16[384,1536]{1,0:T(8,128)(2,1)}, u32[]{:S(2)}, u32[]{:S(2)}) collective-permute-start(bf16[384,1536]{1,0:T(8,128)(2,1)} %get-tuple-element.21), channel_id=1, source_target_pairs={{0,3},{1,0},{2,1},{3,2},{4,7},{5,4},{6,5},{7,6},{8,11},{9,8},{10,9... | collective-permute-start | bytes 3538952 | tf_op jit(solution)/shard_map/ppermute | solution.py:27
  23.0 29.5 %collective-permute-start.2 = (bf16[384,1536]{1,0:T(8,128)(2,1)}, bf16[384,1536]{1,0:T(8,128)(2,1)}, u32[]{:S(2)}, u32[]{:S(2)}) collective-permute-start(bf16[384,1536]{1,0:T(8,128)(2,1)} %get-tuple-element.22), channel_id=1, source_target_pairs={{0,12},{1,13},{2,14},{3,15},{4,0},{5,1},{6,2},{7,3},{8,4},{9,5},{1... | collective-permute-start | bytes 3538952 | tf_op jit(solution)/shard_map/ppermute | solution.py:27
  26.3 35.0 %collective-permute-start.4 = (bf16[384,1536]{1,0:T(8,128)(2,1)S(1)}, bf16[384,1536]{1,0:T(8,128)(2,1)}, u32[]{:S(2)}, u32[]{:S(2)}) collective-permute-start(bf16[384,1536]{1,0:T(8,128)(2,1)S(1)} %collective-permute-done.refs_2_), channel_id=1, source_target_pairs={{0,4},{1,5},{2,6},{3,7},{4,8},{5,9},{6,10},{7,11},{8,12},{9,13},{1... | collective-permute-start | bytes 3538952 | tf_op jit(solution)/shard_map/ppermute | solution.py:27
  46.0 1.0 copy-start.1
  47.1 22.0 %collective-permute-start.5 = (bf16[384,1536]{1,0:T(8,128)(2,1)}, bf16[384,1536]{1,0:T(8,128)(2,1)}, u32[]{:S(2)}, u32[]{:S(2)}) collective-permute-start(bf16[384,1536]{1,0:T(8,128)(2,1)} %collective-permute-done.3.refs_5_), channel_id=1, source_target_pairs={{0,12},{1,13},{2,14},{3,15},{4,0},{5,1},{6,2},{7,3},{8,4},{9,5},{1... | collective-permute-start | bytes 3538952 | tf_op jit(solution)/shard_map/ppermute | solution.py:27
  48.6 24.8 %collective-permute-start.12 = (bf16[384,1536]{1,0:T(8,128)(2,1)}, bf16[384,1536]{1,0:T(8,128)(2,1)}, u32[]{:S(2)}, u32[]{:S(2)}) collective-permute-start(bf16[384,1536]{1,0:T(8,128)(2,1)} %collective-permute-done.11.refs_0_), channel_id=1, source_target_pairs={{0,1},{1,2},{2,3},{3,0},{4,5},{5,6},{6,7},{7,4},{8,9},{9,10},{10,1... | collective-permute-start | bytes 3538952 | tf_op jit(solution)/shard_map/ppermute | solution.py:27
  50.3 28.0 %collective-permute-start.14 = (bf16[384,1536]{1,0:T(8,128)(2,1)}, bf16[384,1536]{1,0:T(8,128)(2,1)}, u32[]{:S(2)}, u32[]{:S(2)}) collective-permute-start(bf16[384,1536]{1,0:T(8,128)(2,1)} %collective-permute-done.13.refs_1_), channel_id=1, source_target_pairs={{0,3},{1,0},{2,1},{3,2},{4,7},{5,4},{6,5},{7,6},{8,11},{9,8},{10,9... | collective-permute-start | bytes 3538952 | tf_op jit(solution)/shard_map/ppermute | solution.py:27
  52.5 65.6 %collective-permute-start.8 = (bf16[384,1536]{1,0:T(8,128)(2,1)}, bf16[384,1536]{1,0:T(8,128)(2,1)S(1)}, u32[]{:S(2)}, u32[]{:S(2)}) collective-permute-start(bf16[384,1536]{1,0:T(8,128)(2,1)} %get-tuple-element.21), channel_id=1, source_target_pairs={{0,1},{1,2},{2,3},{3,0},{4,5},{5,6},{6,7},{7,4},{8,9},{9,10},{10,1... | collective-permute-start | bytes 3538952 | tf_op jit(solution)/shard_map/ppermute | solution.py:27
  61.2 58.3 %collective-permute-start.9 = (bf16[384,1536]{1,0:T(8,128)(2,1)}, bf16[384,1536]{1,0:T(8,128)(2,1)S(1)}, u32[]{:S(2)}, u32[]{:S(2)}) collective-permute-start(bf16[384,1536]{1,0:T(8,128)(2,1)} %get-tuple-element.22), channel_id=1, source_target_pairs={{0,3},{1,0},{2,1},{3,2},{4,7},{5,4},{6,5},{7,6},{8,11},{9,8},{10,9... | collective-permute-start | bytes 3538952 | tf_op jit(solution)/shard_map/ppermute | solution.py:27
  78.3 1.3 copy-start.2
  88.6 33.2 %collective-permute-start.19 = (bf16[384,1536]{1,0:T(8,128)(2,1)S(1)}, bf16[384,1536]{1,0:T(8,128)(2,1)}, u32[]{:S(2)}, u32[]{:S(2)}) collective-permute-start(bf16[384,1536]{1,0:T(8,128)(2,1)S(1)} %get-tuple-element.20), channel_id=1, source_target_pairs={{0,3},{1,0},{2,1},{3,2},{4,7},{5,4},{6,5},{7,6},{8,11},{9,8},{10,9... | collective-permute-start | bytes 3538952 | tf_op jit(solution)/shard_map/ppermute | solution.py:27
  89.9 38.5 %collective-permute-start.15 = (bf16[384,1536]{1,0:T(8,128)(2,1)S(1)}, bf16[384,1536]{1,0:T(8,128)(2,1)}, u32[]{:S(2)}, u32[]{:S(2)}) collective-permute-start(bf16[384,1536]{1,0:T(8,128)(2,1)S(1)} %get-tuple-element.16), channel_id=1, source_target_pairs={{0,1},{1,2},{2,3},{3,0},{4,5},{5,6},{6,7},{7,4},{8,9},{9,10},{10,1... | collective-permute-start | bytes 3538952 | tf_op jit(solution)/shard_map/ppermute | solution.py:27
  90.1 16.5 %collective-permute-start.6 = (s32[1,48]{1,0:T(1,128)S(1)}, s32[1,48]{1,0:T(1,128)S(1)}, u32[]{:S(2)}, u32[]{:S(2)}) collective-permute-start(s32[1,48]{1,0:T(1,128)S(1)} %pad_add_fusion.table_a.table_b), channel_id=1, source_target_pairs={{0,1},{1,2},{2,3},{3,0},{4,5},{5,6},{6,7},{7,4},{8,9},{9,10},{10,1... | collective-permute-start | bytes 584 | tf_op jit(solution)/shard_map/ppermute | solution.py:27
  106.6 2.4 %collective-permute-start.7 = (s32[1,48]{1,0:T(1,128)S(1)}, s32[1,48]{1,0:T(1,128)S(1)}, u32[]{:S(2)}, u32[]{:S(2)}) collective-permute-start(s32[1,48]{1,0:T(1,128)S(1)} %pad_add_fusion.table_a.table_b), channel_id=1, source_target_pairs={{0,3},{1,0},{2,1},{3,2},{4,7},{5,4},{6,5},{7,6},{8,11},{9,8},{10,9... | collective-permute-start | bytes 584 | tf_op jit(solution)/shard_map/ppermute | solution.py:27
  118.0 21.0 %collective-permute-start.17 = (bf16[384,1536]{1,0:T(8,128)(2,1)S(1)}, bf16[384,1536]{1,0:T(8,128)(2,1)S(1)}, u32[]{:S(2)}, u32[]{:S(2)}) collective-permute-start(bf16[384,1536]{1,0:T(8,128)(2,1)S(1)} %get-tuple-element.17), channel_id=1, source_target_pairs={{0,3},{1,0},{2,1},{3,2},{4,7},{5,4},{6,5},{7,6},{8,11},{9,8},{10,9... | collective-permute-start | bytes 3538952 | tf_op jit(solution)/shard_map/ppermute | solution.py:27
  118.1 21.0 %collective-permute-start.18 = (bf16[384,1536]{1,0:T(8,128)(2,1)S(1)}, bf16[384,1536]{1,0:T(8,128)(2,1)S(1)}, u32[]{:S(2)}, u32[]{:S(2)}) collective-permute-start(bf16[384,1536]{1,0:T(8,128)(2,1)S(1)} %get-tuple-element.18), channel_id=1, source_target_pairs={{0,1},{1,2},{2,3},{3,0},{4,5},{5,6},{6,7},{7,4},{8,9},{9,10},{10,1... | collective-permute-start | bytes 3538952 | tf_op jit(solution)/shard_map/ppermute | solution.py:27
  123.4 22.7 %collective-permute-start.20 = (bf16[384,1536]{1,0:T(8,128)(2,1)S(1)}, bf16[384,1536]{1,0:T(8,128)(2,1)S(1)}, u32[]{:S(2)}, u32[]{:S(2)}) collective-permute-start(bf16[384,1536]{1,0:T(8,128)(2,1)S(1)} %add_convert_fusion), channel_id=1, source_target_pairs={{0,3},{1,0},{2,1},{3,2},{4,7},{5,4},{6,5},{7,6},{8,11},{9,8},{10,9... | collective-permute-start | bytes 3538952 | tf_op jit(solution)/shard_map/ppermute | solution.py:27
  128.4 1.7 copy-start.3
  130.1 17.3 %collective-permute-start.16 = (bf16[384,1536]{1,0:T(8,128)(2,1)S(1)}, bf16[384,1536]{1,0:T(8,128)(2,1)S(1)}, u32[]{:S(2)}, u32[]{:S(2)}) collective-permute-start(bf16[384,1536]{1,0:T(8,128)(2,1)S(1)} %add_convert_fusion.1), channel_id=1, source_target_pairs={{0,1},{1,2},{2,3},{3,0},{4,5},{5,6},{6,7},{7,4},{8,9},{9,10},{10,1... | collective-permute-start | bytes 3538952 | tf_op jit(solution)/shard_map/ppermute | solution.py:27
  151.5 11.1 %copy-start.6 = (bf16[768,256]{1,0:T(8,128)(2,1)S(1)}, bf16[768,256]{1,0:T(8,128)(2,1)}, u32[]{:S(2)}) copy-start(bf16[768,256]{1,0:T(8,128)(2,1)} %param.9) | copy-start | bytes 1179652
  151.5 43.2 %all-to-all-start = ((bf16[128,24,384]{2,1,0:T(8,128)(2,1)}), bf16[128,24,384]{2,1,0:T(8,128)(2,1)S(1)}, u32[]{:S(2)}, u32[]{:S(2)}) async-start(bf16[128,24,384]{2,1,0:T(8,128)(2,1)} %pack.1), calls=%async_computation | async-start | bytes 4718592 | tf_op jit(solution)/shard_map/all_to_all | solution.py:253

commit v3 on v2

--- a/solution.py
+++ b/solution.py
@@ -27,26 +27,34 @@
     return lax.ppermute(value, AXES, shifted(kind, step))
 
 
-def pair_body(device, table_a, table_b, energies, own, *refs, slots):
-    lefts, rights = refs[:2], refs[2:8]
-    levels, out_a, out_b = refs[8:11]
-    left_buf, right_buf, gamma, across, left_sem, right_sem = refs[11:]
-    outs = (out_a, out_b)
-    rights = (own.at[0], own.at[1], *rights)
+def pair_body(device, table_a, table_b, energies, levels, own, *refs, slots, picks, started):
+    count = len(picks)
+    lefts, refs = refs[:2], refs[2:]
     if lefts[0].shape == own.shape:
         lefts = (own.at[0], own.at[1])
+    rights = []
+    for n in picks:
+        if n == 0:
+            rights += [own.at[0], own.at[1]]
+        else:
+            rights += refs[:2]
+            refs = refs[2:]
+    begun, refs = refs[: 2 * started], refs[2 * started :]
+    out_a, out_b, left_buf, right_buf, gamma, across, left_sem, right_sem = refs
+    outs = (out_a, out_b)
     col = device[0] % 16
     z, x = col // SIDE, col % SIDE
     even = device[0] // 16 % 2 == 0
     columns = [
-        jnp.where(even, (z + d) % SIDE * SIDE + x, z * SIDE + (x + d) % SIDE) for d in (0, 3, 1, 2)
+        jnp.where(even, (z + d) % SIDE * SIDE + x, z * SIDE + (x + d) % SIDE)
+        for d in ((0, 3, 1, 2)[n] for n in picks)
     ]
 
     def entry(m):
-        side, n = m // 4, m % 4
-        right = jnp.where(
-            n < 2, jnp.where(n == 0, columns[0], columns[1]), jnp.where(n == 2, columns[2], columns[3])
-        )
+        side, n = m // count, m % count
+        right = columns[0]
+        for k in range(1, count):
+            right = jnp.where(n == k, columns[k], right)
 
         def pick(k):
             return jnp.where(side == 0, table_a[0, k], table_b[0, k])
@@ -60,17 +68,18 @@
     ]
     for copy in left_copies:
         copy.start()
-    for m in range(8):
+    for m in range(2 * count):
         _, second, taken = entry(m)
         for s in range(2):
 
             @pl.when(taken & (second % 2 == s))
             def _():
                 pltpu.make_async_copy(
-                    rights[2 * (m % 4) + s], right_buf.at[m], right_sem.at[m]
+                    rights[2 * (m % count) + s], right_buf.at[m], right_sem.at[m]
                 ).start()
 
-    gamma[...] = jnp.zeros_like(gamma)
+    for s in range(2):
+        gamma[s] = begun[s][...] if started else jnp.zeros(gamma.shape[1:], jnp.float32)
     row = levels[...].reshape(1, levels.shape[-1])
     across[...] = jnp.broadcast_to(row, across.shape).T
     for copy in left_copies:
@@ -84,41 +93,47 @@
             pltpu.make_async_copy(rights[0], right_buf.at[m], right_sem.at[m]).wait()
             right = right_buf[m]
             integrals = lax.dot_general(
-                left_buf[m // 4], right, (((1,), (1,)), ((), ())),
+                left_buf[m // count], right, (((1,), (1,)), ((), ())),
                 preferred_element_type=jnp.float32,
             )
             denominator = energies[first] + energies[second] - across[...] - row
             weighted = ((2.0 * integrals - integrals.T) / denominator).astype(jnp.bfloat16)
-            gamma[m // 4] += jnp.dot(weighted, right, preferred_element_type=jnp.float32)
+            gamma[m // count] += jnp.dot(weighted, right, preferred_element_type=jnp.float32)
 
         return carry
 
-    lax.fori_loop(0, 8, step, 0)
+    lax.fori_loop(0, 2 * count, step, 0)
     for s in range(2):
         outs[s][...] = gamma[s].astype(outs[s].dtype)
 
 
-def partial_gamma(device, tables, energies, own, lefts, slots, rights, levels, out_dtype):
+def partial_gamma(scalars, levels, own, lefts, slots, rights, picks, begun, out_dtype):
     virt, aux = own.shape[1:]
     slab = jax.ShapeDtypeStruct((virt, aux), out_dtype)
     hbm = pl.BlockSpec(memory_space=pltpu.HBM)
     smem = pl.BlockSpec(memory_space=pltpu.SMEM)
     vmem = pl.BlockSpec(memory_space=pltpu.VMEM)
+    left_space = hbm if lefts[0] is own else vmem
+    used = [slab for n in picks if n for slab in rights[n]]
     return pl.pallas_call(
-        functools.partial(pair_body, slots=slots),
+        functools.partial(pair_body, slots=slots, picks=picks, started=bool(begun)),
         out_shape=(slab, slab),
-        in_specs=[smem, smem, smem, smem] + [hbm] * 9 + [vmem],
+        in_specs=[smem] * 4
+        + [vmem, hbm]
+        + [left_space] * 2
+        + [hbm] * len(used)
+        + [vmem] * len(begun),
         out_specs=(vmem, vmem),
         scratch_shapes=[
             pltpu.VMEM((2, virt, aux), jnp.bfloat16),
-            pltpu.VMEM((8, virt, aux), jnp.bfloat16),
+            pltpu.VMEM((2 * len(picks), virt, aux), jnp.bfloat16),
             pltpu.VMEM((2, virt, aux), jnp.float32),
             pltpu.VMEM((virt, virt), jnp.float32),
             pltpu.SemaphoreType.DMA((2,)),
-            pltpu.SemaphoreType.DMA((8,)),
+            pltpu.SemaphoreType.DMA((2 * len(picks),)),
         ],
         compiler_params=pltpu.CompilerParams(vmem_limit_bytes=40 << 20),
-    )(device, *tables, energies, own, *lefts, *rights, levels)
+    )(*scalars, levels, own, *lefts, *used, *begun)
 
 
 def pack_body(own_a, own_b, up_a, down_a, up_b, down_b, out, total, block):
@@ -228,26 +243,35 @@
     right_far_b = send(right_high_b, "right", -1)
     far_a = send(near_low_a, "left", 1)
     far_b = send(near_high_b, "left", -1)
+    own_a, own_b, right_far_a, right_far_b, far_a, far_b = lax.optimization_barrier(
+        (own_a, own_b, right_far_a, right_far_b, far_a, far_b)
+    )
     late_low_b = send(own_b, "left", 1)
     late_high_a = send(own_a, "left", -1)
-    rights = (right_low_a, right_low_b, right_high_a, right_high_b, right_far_a, right_far_b)
-
-    def partial(lefts, which, slots, dtype=jnp.bfloat16):
-        chosen = [tables[k] for k in which]
-        return partial_gamma(
-            device.reshape(1), chosen, e_occ, b_three, lefts, slots, rights, e_vir, dtype
-        )
-
-    low_a, high_b = partial((near_low_a, near_high_b), (1, 2), (0, 1))
-    up_b = send(high_b, "left", 1)
-    down_a = send(low_a, "left", -1)
-    sum_a, sum_b = partial((b_three, b_three), (0, 0), (0, 1), jnp.float32)
+    rights = (
+        None,
+        (right_low_a, right_low_b),
+        (right_high_a, right_high_b),
+        (right_far_a, right_far_b),
+    )
+
+    def partial(lefts, which, slots, dtype=jnp.bfloat16, picks=(0, 1, 2, 3), begun=()):
+        scalars = [device.reshape(1)] + [tables[k] for k in which] + [e_occ]
+        return partial_gamma(scalars, e_vir, b_three, lefts, slots, rights, picks, begun, dtype)
+
+    near = (near_low_a, near_high_b)
+    begun = partial(near, (1, 2), (0, 1), jnp.float32, (0, 1, 2))
     far_a, far_b = partial((far_a, far_b), (3, 3), (0, 1))
     relay_a = send(far_a, "left", 1)
     relay_b = send(far_b, "left", -1)
+    low_a, high_b = partial(near, (1, 2), (0, 1), picks=(3,), begun=begun)
     low_b, high_a = partial((late_low_b, late_high_a), (1, 2), (1, 0))
-    up_a = send(add(high_a, relay_a), "left", 1)
-    down_b = send(add(low_b, relay_b), "left", -1)
+    up_b = send(high_b, "left", 1)
+    down_a = send(low_a, "left", -1)
+    joint_a, joint_b = add(high_a, relay_a), add(low_b, relay_b)
+    up_a = send(joint_a, "left", 1)
+    down_b = send(joint_b, "left", -1)
+    sum_a, sum_b = partial((b_three, b_three), (0, 0), (0, 1), jnp.float32)
 
     blocks = pack(sum_a, sum_b, up_a, down_a, up_b, down_b)
     moved = lax.all_to_all(blocks, AXES, split_axis=0, concat_axis=0, tiled=True)

time: 200 us -> 221 us (1.10)
  starting transfers between devices: 46.6 us -> 68.1 us
  waiting for transfers between devices: 103 us -> 97.4 us
  Pallas kernels: 38.1 us -> 43.4 us
    all_to_all x1, starting transfers between devices: 11.1 us -> 31.5 us  [local(): lax.all_to_all(blocks, AXES, split_axis=0, concat_axis=0, tiled=True)]
    ppermute x21, waiting for transfers between devices: 71.5 us -> 66.1 us  [send(): return lax.ppermute(value, AXES, shifted(kind, step))]
    pallas_call x4 -> x5, Pallas kernels: 29.2 us -> 34.6 us  [partial_gamma(): pl.pallas_call(functools.partial(pair_body, slots=slots, picks=picks, sta...]
  transfers between devices with their start and end apart: 22 -> 22, of which waited for: 11 -> 12; matrix products, arithmetic and copies ran while one was open for 3% -> 3% of each run, Pallas kernels for 15% -> 16%
where the time goes in v3:
time: 221 us
  waiting for transfers between devices  97.4 us (44%)
  starting transfers between devices  68.1 us (31%)
  Pallas kernels  43.4 us (20%)
  local copies, waits for them, and re-layouts  7.95 us (4%)
  other arithmetic  3.84 us (2%)
    ppermute x21, waiting for transfers between devices, send(): return lax.ppermute(value, AXES, shifted(kind, step))  66.1 us
    ppermute x21, starting transfers between devices, send(): return lax.ppermute(value, AXES, shifted(kind, step))  36.5 us
    pallas_call x5, Pallas kernels, partial_gamma(): pl.pallas_call(functools.partial(pair_body, slots=slots, picks=picks, sta...  34.6 us
    all_to_all x1, starting transfers between devices, local(): lax.all_to_all(blocks, AXES, split_axis=0, concat_axis=0, tiled=True)  31.5 us
    all_to_all x1, waiting for transfers between devices, local(): lax.all_to_all(blocks, AXES, split_axis=0, concat_axis=0, tiled=True)  31.2 us
    pallas_call x1, Pallas kernels, finish(): pl.pallas_call(finish_body, grid=(48 // rows,), out_shape=jax.ShapeDtypeS...  4.76 us
  transfers between devices with their start and end apart: 22, of which 12 were waited for; matrix products, arithmetic and copies ran while one was open for 3% of the time, Pallas kernels for 16%

profile of v3, /device:TPU:1, one launch (start us, length us, event | category | flops | bytes accessed | tf_op | source)
XLA Modules:
  0.0 220.8 jit_solution(18386288740720870850)
XLA Ops:
  0.0 3.3 %slice_bitcast_fusion = (bf16[384,1536]{1,0:T(8,128)(2,1)}, bf16[384,1536]{1,0:T(8,128)(2,1)}) fusion(bf16[2,384,1536]{2,1,0:T(8,128)(2,1)} %own.9), kind=kLoop, calls=%fused_computation.2 | loop fusion | bytes 4718592 | tf_op jit(solution)/shard_map/squeeze | solution.py:232
  3.4 2.0 collective-permute-start
  5.4 1.3 collective-permute-start.3
  6.7 1.8 collective-permute-start.6
  8.5 2.1 collective-permute-start.8
  10.6 17.5 %collective-permute-done.refs_2_ = bf16[384,1536]{1,0:T(8,128)(2,1)S(1)} collective-permute-done((bf16[384,1536]{1,0:T(8,128)(2,1)}, bf16[384,1536]{1,0:T(8,128)(2,1)S(1)}, u32[]{:S(2)}, u32[]{:S(2)}) %collective-permute-start) | collective-permute-done | bytes 1179680 | tf_op jit(solution)/shard_map/ppermute | solution.py:27
  28.5 2.3 %collective-permute-start.5 = (bf16[384,1536]{1,0:T(8,128)(2,1)}, bf16[384,1536]{1,0:T(8,128)(2,1)}, u32[]{:S(2)}, u32[]{:S(2)}) collective-permute-start(bf16[384,1536]{1,0:T(8,128)(2,1)} %collective-permute-done.3.refs_5_), channel_id=1, source_target_pairs={{0,12},{1,13},{2,14},{3,15},{4,0},{5,1},{6,2},{7,3},{8,4},{9,5},{1... | collective-permute-start | bytes 3538952 | tf_op jit(solution)/shard_map/ppermute | solution.py:27
  30.8 4.5 %collective-permute-done.6.refs_0_ = bf16[384,1536]{1,0:T(8,128)(2,1)} collective-permute-done((bf16[384,1536]{1,0:T(8,128)(2,1)}, bf16[384,1536]{1,0:T(8,128)(2,1)}, u32[]{:S(2)}, u32[]{:S(2)}) %collective-permute-start.6) | collective-permute-done | bytes 1179680 | tf_op jit(solution)/shard_map/ppermute | solution.py:27
  35.5 2.8 %collective-permute-start.9 = (bf16[384,1536]{1,0:T(8,128)(2,1)}, bf16[384,1536]{1,0:T(8,128)(2,1)}, u32[]{:S(2)}, u32[]{:S(2)}) collective-permute-start(bf16[384,1536]{1,0:T(8,128)(2,1)} %collective-permute-done.8.refs_1_), channel_id=1, source_target_pairs={{0,3},{1,0},{2,1},{3,2},{4,7},{5,4},{6,5},{7,6},{8,11},{9,8},{10,9... | collective-permute-start | bytes 3538952 | tf_op jit(solution)/shard_map/ppermute | solution.py:27
  39.5 9.6 %collective-permute-done.4.refs_6_.refs_2_ = bf16[384,1536]{1,0:T(8,128)(2,1)S(1)} collective-permute-done((bf16[384,1536]{1,0:T(8,128)(2,1)S(1)}, bf16[384,1536]{1,0:T(8,128)(2,1)S(1)}, u32[]{:S(2)}, u32[]{:S(2)}) %collective-permute-start.4) | collective-permute-done | bytes 1179680 | tf_op jit(solution)/shard_map/ppermute | solution.py:27
  53.5 7.5 %collective-permute-start.14 = (s32[1,48]{1,0:T(1,128)S(1)}, s32[1,48]{1,0:T(1,128)S(1)}, u32[]{:S(2)}, u32[]{:S(2)}) collective-permute-start(s32[1,48]{1,0:T(1,128)S(1)} %pad_add_fusion.table_a.table_b), channel_id=1, source_target_pairs={{0,2},{1,3},{2,0},{3,1},{4,6},{5,7},{6,4},{7,5},{8,10},{9,11},{10,... | collective-permute-start | bytes 584 | tf_op jit(solution)/shard_map/ppermute | solution.py:27
  61.0 3.9 %collective-permute-done.7.refs_0_ = bf16[384,1536]{1,0:T(8,128)(2,1)} collective-permute-done((bf16[384,1536]{1,0:T(8,128)(2,1)}, bf16[384,1536]{1,0:T(8,128)(2,1)}, u32[]{:S(2)}, u32[]{:S(2)}) %collective-permute-start.7) | collective-permute-done | bytes 1179680 | tf_op jit(solution)/shard_map/ppermute | solution.py:27
  65.1 2.5 %collective-permute-start.13 = (bf16[384,1536]{1,0:T(8,128)(2,1)}, bf16[384,1536]{1,0:T(8,128)(2,1)S(1)}, u32[]{:S(2)}, u32[]{:S(2)}) collective-permute-start(bf16[384,1536]{1,0:T(8,128)(2,1)} %get-tuple-element.26), channel_id=1, source_target_pairs={{0,3},{1,0},{2,1},{3,2},{4,7},{5,4},{6,5},{7,6},{8,11},{9,8},{10,9... | collective-permute-start | bytes 3538952 | tf_op jit(solution)/shard_map/ppermute | solution.py:27
  67.5 3.9 %collective-permute-done.1.refs_3_ = bf16[384,1536]{1,0:T(8,128)(2,1)} collective-permute-done((bf16[384,1536]{1,0:T(8,128)(2,1)}, bf16[384,1536]{1,0:T(8,128)(2,1)}, u32[]{:S(2)}, u32[]{:S(2)}) %collective-permute-start.1) | collective-permute-done | bytes 1179680 | tf_op jit(solution)/shard_map/ppermute | solution.py:27
  72.9 10.0 %shard_map.66 = (bf16[384,1536]{1,0:T(8,128)(2,1)S(1)}, bf16[384,1536]{1,0:T(8,128)(2,1)S(1)}) custom-call(s32[1]{0:T(128)} %bitcast.device, s32[1,48]{1,0:T(1,128)S(1)} %collective-permute-done.14.table_a.table_b, s32[1,48]{1,0:T(1,128)S(1)} %collective-permute-done.14.table_a.table_b, f32[256]{0:T(256)S(1)} %copy-done.5, f32[384]{0:T(512)S(1)} %copy-done.4, ...), custom_call_target="tpu_custom_call" | custom-call | tf_op jit(solution)/shard_map/pallas_call | solution.py:118
  82.9 3.1 %collective-permute-start.19 = (bf16[384,1536]{1,0:T(8,128)(2,1)S(1)}, bf16[384,1536]{1,0:T(8,128)(2,1)}, u32[]{:S(2)}, u32[]{:S(2)}) collective-permute-start(bf16[384,1536]{1,0:T(8,128)(2,1)S(1)} %get-tuple-element.36), channel_id=1, source_target_pairs={{0,3},{1,0},{2,1},{3,2},{4,7},{5,4},{6,5},{7,6},{8,11},{9,8},{10,9... | collective-permute-start | bytes 3538952 | tf_op jit(solution)/shard_map/ppermute | solution.py:27
  87.1 15.2 %collective-permute-done.10.table_a = s32[1,48]{1,0:T(1,128)S(1)} collective-permute-done((s32[1,48]{1,0:T(1,128)S(1)}, s32[1,48]{1,0:T(1,128)S(1)}, u32[]{:S(2)}, u32[]{:S(2)}) %collective-permute-start.10) | collective-permute-done | bytes 224 | tf_op jit(solution)/shard_map/ppermute | solution.py:27
  102.8 2.6 %collective-permute-done.11.table_b = s32[1,48]{1,0:T(1,128)S(1)} collective-permute-done((s32[1,48]{1,0:T(1,128)S(1)}, s32[1,48]{1,0:T(1,128)S(1)}, u32[]{:S(2)}, u32[]{:S(2)}) %collective-permute-start.11) | collective-permute-done | bytes 224 | tf_op jit(solution)/shard_map/ppermute | solution.py:27
  105.4 8.7 %shard_map.67 = (f32[384,1536]{1,0:T(8,128)S(1)}, f32[384,1536]{1,0:T(8,128)S(1)}) custom-call(s32[1]{0:T(128)} %bitcast.device, s32[1,48]{1,0:T(1,128)S(1)} %collective-permute-done.10.table_a, s32[1,48]{1,0:T(1,128)S(1)} %collective-permute-done.11.table_b, f32[256]{0:T(256)S(1)} %copy-done.5, f32[384]{0:T(512)S(1)} %copy-done.4, ...), custom_call_target="tpu_custom_call" | custom-call | tf_op jit(solution)/shard_map/pallas_call | solution.py:118
  114.1 4.8 %shard_map.68 = (bf16[384,1536]{1,0:T(8,128)(2,1)S(1)}, bf16[384,1536]{1,0:T(8,128)(2,1)S(1)}) custom-call(s32[1]{0:T(128)} %bitcast.device, s32[1,48]{1,0:T(1,128)S(1)} %collective-permute-done.10.table_a, s32[1,48]{1,0:T(1,128)S(1)} %collective-permute-done.11.table_b, f32[256]{0:T(256)S(1)} %copy-done.5, f32[384]{0:T(512)S(1)} %copy-done.4, ...), custom_call_target="tpu_custom_call" | custom-call | tf_op jit(solution)/shard_map/pallas_call | solution.py:118
  119.0 1.4 collective-permute-start.18
  120.5 2.1 shard_map.65
  122.6 1.6 add_convert_fusion
  124.1 5.0 %collective-permute-start.20 = (bf16[384,1536]{1,0:T(8,128)(2,1)S(1)}, bf16[384,1536]{1,0:T(8,128)(2,1)S(1)}, u32[]{:S(2)}, u32[]{:S(2)}) collective-permute-start(bf16[384,1536]{1,0:T(8,128)(2,1)S(1)} %add_convert_fusion), channel_id=1, source_target_pairs={{0,3},{1,0},{2,1},{3,2},{4,7},{5,4},{6,5},{7,6},{8,11},{9,8},{10,9... | collective-permute-start | bytes 3538952 | tf_op jit(solution)/shard_map/ppermute | solution.py:27
  129.1 1.6 add_convert_fusion.1
  130.8 9.0 %shard_map.64 = (f32[384,1536]{1,0:T(8,128)S(1)}, f32[384,1536]{1,0:T(8,128)S(1)}) custom-call(s32[1]{0:T(128)} %bitcast.device, s32[1,48]{1,0:T(1,128)S(1)} %pad_add_fusion.table_a.table_b, s32[1,48]{1,0:T(1,128)S(1)} %pad_add_fusion.table_a.table_b, f32[256]{0:T(256)S(1)} %copy-done.5, f32[384]{0:T(512)S(1)} %copy-done.4, ...), custom_call_target="tpu_custom_call" | custom-call | tf_op jit(solution)/shard_map/pallas_call | solution.py:118
  139.8 7.2 %collective-permute-done.20.down_b = bf16[384,1536]{1,0:T(8,128)(2,1)S(1)} collective-permute-done((bf16[384,1536]{1,0:T(8,128)(2,1)S(1)}, bf16[384,1536]{1,0:T(8,128)(2,1)S(1)}, u32[]{:S(2)}, u32[]{:S(2)}) %collective-permute-start.20) | collective-permute-done | bytes 1179680 | tf_op jit(solution)/shard_map/ppermute | solution.py:27
  147.0 1.3 collective-permute-done.16.up_a
  148.3 4.0 %pack.1 = bf16[128,24,384]{2,1,0:T(8,128)(2,1)} custom-call(f32[384,1536]{1,0:T(8,128)S(1)} %get-tuple-element.23.own_a, f32[384,1536]{1,0:T(8,128)S(1)} %get-tuple-element.24.own_b, bf16[384,1536]{1,0:T(8,128)(2,1)S(1)} %collective-permute-done.16.up_a, bf16[384,1536]{1,0:T(8,128)(2,1)S(1)} %collective-permute-done.17.down_a, ...), custom_call_target="tpu_custom_call" | custom-call | tf_op jit(solution)/shard_map/pack/pallas_call | solution.py:167
  152.3 31.5 %all-to-all-start = ((bf16[128,24,384]{2,1,0:T(8,128)(2,1)}), bf16[128,24,384]{2,1,0:T(8,128)(2,1)S(1)}, u32[]{:S(2)}, u32[]{:S(2)}) async-start(bf16[128,24,384]{2,1,0:T(8,128)(2,1)} %pack.1), calls=%async_computation | async-start | bytes 4718592 | tf_op jit(solution)/shard_map/all_to_all | solution.py:277
  184.8 31.2 %all-to-all-done = bf16[128,24,384]{2,1,0:T(8,128)(2,1)S(1)} async-done(((bf16[128,24,384]{2,1,0:T(8,128)(2,1)}), bf16[128,24,384]{2,1,0:T(8,128)(2,1)S(1)}, u32[]{:S(2)}, u32[]{:S(2)}) %all-to-all-start) | async-done | bytes 2359328 | tf_op jit(solution)/shard_map/all_to_all | solution.py:277
  216.0 4.8 %finish.1 = bf16[48,96,768]{2,1,0:T(8,128)(2,1)} custom-call(bf16[3072,384]{1,0:T(8,128)(2,1)S(1)} %bitcast.13, bf16[768,256]{1,0:T(8,128)(2,1)S(1)} %bitcast.14), custom_call_target="tpu_custom_call" | custom-call | tf_op jit(solution)/shard_map/finish/pallas_call | solution.py:208
  (43 shorter events, 10.5 us)
Async XLA Ops:
  0.0 71.6 %copy-start.5 = (f32[256]{0:T(256)S(1)}, f32[256]{0:T(256)}, u32[]{:S(2)}) copy-start(f32[256]{0:T(256)} %energies.9) | copy-start | bytes 3076
  0.0 71.6 %copy-start.4 = (f32[384]{0:T(512)S(1)}, f32[384]{0:T(512)}, u32[]{:S(2)}) copy-start(f32[384]{0:T(512)} %levels.9) | copy-start | bytes 4612
  0.0 71.6 %copy-start = (bf16[2,384,1536]{2,1,0:T(8,128)(2,1)S(1)}, bf16[2,384,1536]{2,1,0:T(8,128)(2,1)}, u32[]{:S(2)}) copy-start(bf16[2,384,1536]{2,1,0:T(8,128)(2,1)} %own.9) | copy-start | bytes 7077892
  3.4 24.8 %collective-permute-start = (bf16[384,1536]{1,0:T(8,128)(2,1)}, bf16[384,1536]{1,0:T(8,128)(2,1)S(1)}, u32[]{:S(2)}, u32[]{:S(2)}) collective-permute-start(bf16[384,1536]{1,0:T(8,128)(2,1)} %get-tuple-element.26), channel_id=1, source_target_pairs={{0,4},{1,5},{2,6},{3,7},{4,8},{5,9},{6,10},{7,11},{8,12},{9,13},{1... | collective-permute-start | bytes 3538952 | tf_op jit(solution)/shard_map/ppermute | solution.py:27
  5.4 23.1 %collective-permute-start.3 = (bf16[384,1536]{1,0:T(8,128)(2,1)}, bf16[384,1536]{1,0:T(8,128)(2,1)}, u32[]{:S(2)}, u32[]{:S(2)}) collective-permute-start(bf16[384,1536]{1,0:T(8,128)(2,1)} %get-tuple-element.25), channel_id=1, source_target_pairs={{0,12},{1,13},{2,14},{3,15},{4,0},{5,1},{6,2},{7,3},{8,4},{9,5},{1... | collective-permute-start | bytes 3538952 | tf_op jit(solution)/shard_map/ppermute | solution.py:27
  6.7 28.7 %collective-permute-start.6 = (bf16[384,1536]{1,0:T(8,128)(2,1)}, bf16[384,1536]{1,0:T(8,128)(2,1)}, u32[]{:S(2)}, u32[]{:S(2)}) collective-permute-start(bf16[384,1536]{1,0:T(8,128)(2,1)} %get-tuple-element.26), channel_id=1, source_target_pairs={{0,1},{1,2},{2,3},{3,0},{4,5},{5,6},{6,7},{7,4},{8,9},{9,10},{10,1... | collective-permute-start | bytes 3538952 | tf_op jit(solution)/shard_map/ppermute | solution.py:27
  8.5 27.0 %collective-permute-start.8 = (bf16[384,1536]{1,0:T(8,128)(2,1)}, bf16[384,1536]{1,0:T(8,128)(2,1)}, u32[]{:S(2)}, u32[]{:S(2)}) collective-permute-start(bf16[384,1536]{1,0:T(8,128)(2,1)} %get-tuple-element.25), channel_id=1, source_target_pairs={{0,3},{1,0},{2,1},{3,2},{4,7},{5,4},{6,5},{7,6},{8,11},{9,8},{10,9... | collective-permute-start | bytes 3538952 | tf_op jit(solution)/shard_map/ppermute | solution.py:27
  28.1 21.0 %collective-permute-start.4 = (bf16[384,1536]{1,0:T(8,128)(2,1)S(1)}, bf16[384,1536]{1,0:T(8,128)(2,1)S(1)}, u32[]{:S(2)}, u32[]{:S(2)}) collective-permute-start(bf16[384,1536]{1,0:T(8,128)(2,1)S(1)} %collective-permute-done.refs_2_), channel_id=1, source_target_pairs={{0,4},{1,5},{2,6},{3,7},{4,8},{5,9},{6,10},{7,11},{8,12},{9,13},{1... | collective-permute-start | bytes 3538952 | tf_op jit(solution)/shard_map/ppermute | solution.py:27
  28.5 25.0 %collective-permute-start.5 = (bf16[384,1536]{1,0:T(8,128)(2,1)}, bf16[384,1536]{1,0:T(8,128)(2,1)}, u32[]{:S(2)}, u32[]{:S(2)}) collective-permute-start(bf16[384,1536]{1,0:T(8,128)(2,1)} %collective-permute-done.3.refs_5_), channel_id=1, source_target_pairs={{0,12},{1,13},{2,14},{3,15},{4,0},{5,1},{6,2},{7,3},{8,4},{9,5},{1... | collective-permute-start | bytes 3538952 | tf_op jit(solution)/shard_map/ppermute | solution.py:27
  35.3 29.5 %collective-permute-start.7 = (bf16[384,1536]{1,0:T(8,128)(2,1)}, bf16[384,1536]{1,0:T(8,128)(2,1)}, u32[]{:S(2)}, u32[]{:S(2)}) collective-permute-start(bf16[384,1536]{1,0:T(8,128)(2,1)} %collective-permute-done.6.refs_0_), channel_id=1, source_target_pairs={{0,1},{1,2},{2,3},{3,0},{4,5},{5,6},{6,7},{7,4},{8,9},{9,10},{10,1... | collective-permute-start | bytes 3538952 | tf_op jit(solution)/shard_map/ppermute | solution.py:27
  35.5 29.3 %collective-permute-start.9 = (bf16[384,1536]{1,0:T(8,128)(2,1)}, bf16[384,1536]{1,0:T(8,128)(2,1)}, u32[]{:S(2)}, u32[]{:S(2)}) collective-permute-start(bf16[384,1536]{1,0:T(8,128)(2,1)} %collective-permute-done.8.refs_1_), channel_id=1, source_target_pairs={{0,3},{1,0},{2,1},{3,2},{4,7},{5,4},{6,5},{7,6},{8,11},{9,8},{10,9... | collective-permute-start | bytes 3538952 | tf_op jit(solution)/shard_map/ppermute | solution.py:27
  38.3 33.1 %collective-permute-start.1 = (bf16[384,1536]{1,0:T(8,128)(2,1)}, bf16[384,1536]{1,0:T(8,128)(2,1)}, u32[]{:S(2)}, u32[]{:S(2)}) collective-permute-start(bf16[384,1536]{1,0:T(8,128)(2,1)} %get-tuple-element.25), channel_id=1, source_target_pairs={{0,4},{1,5},{2,6},{3,7},{4,8},{5,9},{6,10},{7,11},{8,12},{9,13},{1... | collective-permute-start | bytes 3538952 | tf_op jit(solution)/shard_map/ppermute | solution.py:27
  49.1 1.1 copy-start.1
  50.2 21.4 %collective-permute-start.2 = (bf16[384,1536]{1,0:T(8,128)(2,1)}, bf16[384,1536]{1,0:T(8,128)(2,1)}, u32[]{:S(2)}, u32[]{:S(2)}) collective-permute-start(bf16[384,1536]{1,0:T(8,128)(2,1)} %get-tuple-element.26), channel_id=1, source_target_pairs={{0,12},{1,13},{2,14},{3,15},{4,0},{5,1},{6,2},{7,3},{8,4},{9,5},{1... | collective-permute-start | bytes 3538952 | tf_op jit(solution)/shard_map/ppermute | solution.py:27
  53.5 14.1 %collective-permute-start.14 = (s32[1,48]{1,0:T(1,128)S(1)}, s32[1,48]{1,0:T(1,128)S(1)}, u32[]{:S(2)}, u32[]{:S(2)}) collective-permute-start(s32[1,48]{1,0:T(1,128)S(1)} %pad_add_fusion.table_a.table_b), channel_id=1, source_target_pairs={{0,2},{1,3},{2,0},{3,1},{4,6},{5,7},{6,4},{7,5},{8,10},{9,11},{10,... | collective-permute-start | bytes 584 | tf_op jit(solution)/shard_map/ppermute | solution.py:27
  64.8 54.2 %collective-permute-start.12 = (bf16[384,1536]{1,0:T(8,128)(2,1)}, bf16[384,1536]{1,0:T(8,128)(2,1)S(1)}, u32[]{:S(2)}, u32[]{:S(2)}) collective-permute-start(bf16[384,1536]{1,0:T(8,128)(2,1)} %get-tuple-element.25), channel_id=1, source_target_pairs={{0,1},{1,2},{2,3},{3,0},{4,5},{5,6},{6,7},{7,4},{8,9},{9,10},{10,1... | collective-permute-start | bytes 3538952 | tf_op jit(solution)/shard_map/ppermute | solution.py:27
  65.1 55.4 %collective-permute-start.13 = (bf16[384,1536]{1,0:T(8,128)(2,1)}, bf16[384,1536]{1,0:T(8,128)(2,1)S(1)}, u32[]{:S(2)}, u32[]{:S(2)}) collective-permute-start(bf16[384,1536]{1,0:T(8,128)(2,1)} %get-tuple-element.26), channel_id=1, source_target_pairs={{0,3},{1,0},{2,1},{3,2},{4,7},{5,4},{6,5},{7,6},{8,11},{9,8},{10,9... | collective-permute-start | bytes 3538952 | tf_op jit(solution)/shard_map/ppermute | solution.py:27
  71.6 1.3 copy-start.2
  82.9 39.7 %collective-permute-start.19 = (bf16[384,1536]{1,0:T(8,128)(2,1)S(1)}, bf16[384,1536]{1,0:T(8,128)(2,1)}, u32[]{:S(2)}, u32[]{:S(2)}) collective-permute-start(bf16[384,1536]{1,0:T(8,128)(2,1)S(1)} %get-tuple-element.36), channel_id=1, source_target_pairs={{0,3},{1,0},{2,1},{3,2},{4,7},{5,4},{6,5},{7,6},{8,11},{9,8},{10,9... | collective-permute-start | bytes 3538952 | tf_op jit(solution)/shard_map/ppermute | solution.py:27
  86.0 28.1 %copy-start.3 = (bf16[384,1536]{1,0:T(8,128)(2,1)S(1)}, bf16[384,1536]{1,0:T(8,128)(2,1)}, u32[]{:S(2)}) copy-start(bf16[384,1536]{1,0:T(8,128)(2,1)} %copy-done.1) | copy-start | bytes 3538948
  86.0 43.2 %collective-permute-start.15 = (bf16[384,1536]{1,0:T(8,128)(2,1)S(1)}, bf16[384,1536]{1,0:T(8,128)(2,1)}, u32[]{:S(2)}, u32[]{:S(2)}) collective-permute-start(bf16[384,1536]{1,0:T(8,128)(2,1)S(1)} %get-tuple-element.30), channel_id=1, source_target_pairs={{0,1},{1,2},{2,3},{3,0},{4,5},{5,6},{6,7},{7,4},{8,9},{9,10},{10,1... | collective-permute-start | bytes 3538952 | tf_op jit(solution)/shard_map/ppermute | solution.py:27
  86.0 16.4 %collective-permute-start.10 = (s32[1,48]{1,0:T(1,128)S(1)}, s32[1,48]{1,0:T(1,128)S(1)}, u32[]{:S(2)}, u32[]{:S(2)}) collective-permute-start(s32[1,48]{1,0:T(1,128)S(1)} %pad_add_fusion.table_a.table_b), channel_id=1, source_target_pairs={{0,1},{1,2},{2,3},{3,0},{4,5},{5,6},{6,7},{7,4},{8,9},{9,10},{10,1... | collective-permute-start | bytes 584 | tf_op jit(solution)/shard_map/ppermute | solution.py:27
  102.4 3.0 %collective-permute-start.11 = (s32[1,48]{1,0:T(1,128)S(1)}, s32[1,48]{1,0:T(1,128)S(1)}, u32[]{:S(2)}, u32[]{:S(2)}) collective-permute-start(s32[1,48]{1,0:T(1,128)S(1)} %pad_add_fusion.table_a.table_b), channel_id=1, source_target_pairs={{0,3},{1,0},{2,1},{3,2},{4,7},{5,4},{6,5},{7,6},{8,11},{9,8},{10,9... | collective-permute-start | bytes 584 | tf_op jit(solution)/shard_map/ppermute | solution.py:27
  118.9 20.9 %collective-permute-start.17 = (bf16[384,1536]{1,0:T(8,128)(2,1)S(1)}, bf16[384,1536]{1,0:T(8,128)(2,1)S(1)}, u32[]{:S(2)}, u32[]{:S(2)}) collective-permute-start(bf16[384,1536]{1,0:T(8,128)(2,1)S(1)} %get-tuple-element.33), channel_id=1, source_target_pairs={{0,3},{1,0},{2,1},{3,2},{4,7},{5,4},{6,5},{7,6},{8,11},{9,8},{10,9... | collective-permute-start | bytes 3538952 | tf_op jit(solution)/shard_map/ppermute | solution.py:27
  119.0 20.8 %collective-permute-start.18 = (bf16[384,1536]{1,0:T(8,128)(2,1)S(1)}, bf16[384,1536]{1,0:T(8,128)(2,1)S(1)}, u32[]{:S(2)}, u32[]{:S(2)}) collective-permute-start(bf16[384,1536]{1,0:T(8,128)(2,1)S(1)} %get-tuple-element.34), channel_id=1, source_target_pairs={{0,1},{1,2},{2,3},{3,0},{4,5},{5,6},{6,7},{7,4},{8,9},{9,10},{10,1... | collective-permute-start | bytes 3538952 | tf_op jit(solution)/shard_map/ppermute | solution.py:27
  124.1 22.8 %collective-permute-start.20 = (bf16[384,1536]{1,0:T(8,128)(2,1)S(1)}, bf16[384,1536]{1,0:T(8,128)(2,1)S(1)}, u32[]{:S(2)}, u32[]{:S(2)}) collective-permute-start(bf16[384,1536]{1,0:T(8,128)(2,1)S(1)} %add_convert_fusion), channel_id=1, source_target_pairs={{0,3},{1,0},{2,1},{3,2},{4,7},{5,4},{6,5},{7,6},{8,11},{9,8},{10,9... | collective-permute-start | bytes 3538952 | tf_op jit(solution)/shard_map/ppermute | solution.py:27
  130.7 17.6 %collective-permute-start.16 = (bf16[384,1536]{1,0:T(8,128)(2,1)S(1)}, bf16[384,1536]{1,0:T(8,128)(2,1)S(1)}, u32[]{:S(2)}, u32[]{:S(2)}) collective-permute-start(bf16[384,1536]{1,0:T(8,128)(2,1)S(1)} %add_convert_fusion.1), channel_id=1, source_target_pairs={{0,1},{1,2},{2,3},{3,0},{4,5},{5,6},{6,7},{7,4},{8,9},{9,10},{10,1... | collective-permute-start | bytes 3538952 | tf_op jit(solution)/shard_map/ppermute | solution.py:27
  152.3 31.5 %copy-start.6 = (bf16[768,256]{1,0:T(8,128)(2,1)S(1)}, bf16[768,256]{1,0:T(8,128)(2,1)}, u32[]{:S(2)}) copy-start(bf16[768,256]{1,0:T(8,128)(2,1)} %param.9) | copy-start | bytes 1179652
  152.3 63.7 %all-to-all-start = ((bf16[128,24,384]{2,1,0:T(8,128)(2,1)}), bf16[128,24,384]{2,1,0:T(8,128)(2,1)S(1)}, u32[]{:S(2)}, u32[]{:S(2)}) async-start(bf16[128,24,384]{2,1,0:T(8,128)(2,1)} %pack.1), calls=%async_computation | async-start | bytes 4718592 | tf_op jit(solution)/shard_map/all_to_all | solution.py:277

commit v4 on v3

--- a/solution.py
+++ b/solution.py
@@ -9,6 +9,7 @@
 
 
 AXES = ("row", "col")
+PARTS = ((0, 16), (16, 48))
 SIDE = 4
 
 
@@ -34,14 +35,16 @@
         lefts = (own.at[0], own.at[1])
     rights = []
     for n in picks:
-        if n == 0:
-            rights += [own.at[0], own.at[1]]
-        else:
+        if n == 3:
             rights += refs[:2]
             refs = refs[2:]
+        elif n:
+            rights += [refs[0].at[0], refs[0].at[1]]
+            refs = refs[1:]
+        else:
+            rights += [own.at[0], own.at[1]]
     begun, refs = refs[: 2 * started], refs[2 * started :]
-    out_a, out_b, left_buf, right_buf, gamma, across, left_sem, right_sem = refs
-    outs = (out_a, out_b)
+    *outs, left_buf, right_buf, gamma, across, left_sem, right_sem = refs
     col = device[0] % 16
     z, x = col // SIDE, col % SIDE
     even = device[0] // 16 % 2 == 0
@@ -104,12 +107,22 @@
 
     lax.fori_loop(0, 2 * count, step, 0)
     for s in range(2):
-        outs[s][...] = gamma[s].astype(outs[s].dtype)
-
-
-def partial_gamma(scalars, levels, own, lefts, slots, rights, picks, begun, out_dtype):
+        if len(outs) == 2:
+            outs[s][...] = gamma[s]
+            continue
+        for part, (low, high) in enumerate(PARTS):
+            out = outs[2 * s + part]
+            rows = high - low
+            for block in range(8):
+                out[block * rows : (block + 1) * rows] = gamma[
+                    s, block * 48 + low : block * 48 + high
+                ].astype(out.dtype)
+
+
+def partial_gamma(scalars, levels, own, lefts, slots, rights, picks, begun, out_dtype, split):
     virt, aux = own.shape[1:]
-    slab = jax.ShapeDtypeStruct((virt, aux), out_dtype)
+    heights = [(high - low) * 8 for low, high in PARTS] if split else [virt]
+    out_shape = [jax.ShapeDtypeStruct((height, aux), out_dtype) for height in heights] * 2
     hbm = pl.BlockSpec(memory_space=pltpu.HBM)
     smem = pl.BlockSpec(memory_space=pltpu.SMEM)
     vmem = pl.BlockSpec(memory_space=pltpu.VMEM)
@@ -117,13 +130,13 @@
     used = [slab for n in picks if n for slab in rights[n]]
     return pl.pallas_call(
         functools.partial(pair_body, slots=slots, picks=picks, started=bool(begun)),
-        out_shape=(slab, slab),
+        out_shape=out_shape,
         in_specs=[smem] * 4
         + [vmem, hbm]
         + [left_space] * 2
         + [hbm] * len(used)
         + [vmem] * len(begun),
-        out_specs=(vmem, vmem),
+        out_specs=[vmem] * len(out_shape),
         scratch_shapes=[
             pltpu.VMEM((2, virt, aux), jnp.bfloat16),
             pltpu.VMEM((2 * len(picks), virt, aux), jnp.bfloat16),
@@ -137,6 +150,7 @@
 
 
 def pack_body(own_a, own_b, up_a, down_a, up_b, down_b, out, total, block):
+    height, rows = own_a.shape[0], out.shape[1]
     for slot, parts in enumerate(((own_a, up_a, down_a), (own_b, up_b, down_b))):
         for k in range(12):
             lanes = slice(k * 128, (k + 1) * 128)
@@ -147,77 +161,84 @@
         for slot in range(2):
             pieces = []
             for q in range(4):
-                rows = pl.ds(q, 96, stride=4)
-                piece = total[slot * 12 + tile, rows, :]
+                picked = pl.ds(q, height // 4, stride=4)
+                piece = total[slot * 12 + tile, picked, :]
                 if offset > 32:
-                    piece = jnp.concatenate([piece, total[slot * 12 + tile + 1, rows, :]], 1)
+                    piece = jnp.concatenate([piece, total[slot * 12 + tile + 1, picked, :]], 1)
                 pieces.append(piece[:, offset : offset + 96])
             value = jnp.concatenate(pieces, 1)
             for k in range(3):
-                block[c % 2 * 3 + k, pl.ds(slot, 96, stride=2), :] = value[:, k * 128 : (k + 1) * 128]
+                block[c % 2 * 3 + k, pl.ds(slot, height // 4, stride=2), :] = value[
+                    :, k * 128 : (k + 1) * 128
+                ]
         for r in range(8):
             for k in range(3):
                 out[r * 16 + c, :, k * 128 : (k + 1) * 128] = block[
-                    c % 2 * 3 + k, r * 24 : (r + 1) * 24
+                    c % 2 * 3 + k, r * rows : (r + 1) * rows
                 ].astype(out.dtype)
 
 
 def pack(own_a, own_b, up_a, down_a, up_b, down_b):
+    height = own_a.shape[0]
     vmem = pl.BlockSpec(memory_space=pltpu.VMEM)
     return pl.pallas_call(
         pack_body,
-        out_shape=jax.ShapeDtypeStruct((128, 24, 384), jnp.bfloat16),
+        out_shape=jax.ShapeDtypeStruct((128, height // 16, 384), jnp.bfloat16),
         in_specs=[vmem] * 6,
         out_specs=vmem,
         scratch_shapes=[
-            pltpu.VMEM((24, 384, 128), jnp.float32),
-            pltpu.VMEM((6, 192, 128), jnp.float32),
+            pltpu.VMEM((24, height, 128), jnp.float32),
+            pltpu.VMEM((6, height // 2, 128), jnp.float32),
         ],
         compiler_params=pltpu.CompilerParams(vmem_limit_bytes=32 << 20),
-        name="pack",
     )(own_a, own_b, up_a, down_a, up_b, down_b)
 
 
-def finish_body(blocks, coeff, out, wide):
+def finish_body(tail, head, coeff, out, wide_tail, wide_head):
     step = pl.program_id(0)
+
+    def run(wide, stride, first):
+        for k in range(4):
+            picked = [pl.ds(first + 2 * k + s, 128, stride=stride) for s in range(2)]
+            rows = jnp.concatenate(
+                [jnp.concatenate([wide[lane, rows, :] for lane in range(3)], 1) for rows in picked], 0
+            ).astype(jnp.bfloat16)
+            result = lax.dot_general(
+                rows, coeff[...], (((0,), (1,)), ((), ())), preferred_element_type=jnp.float32
+            )
+            out[4 * k : 4 * k + 4] = result.reshape(4, 96, 768).astype(out.dtype)
 
     @pl.when(step == 0)
     def _():
         for k in range(3):
-            wide[k] = blocks[:, k * 128 : (k + 1) * 128].astype(jnp.float32)
-
-    per_step = out.shape[0] // 4
-    for k in range(per_step):
-        t = step * per_step + k
-        rows = jnp.concatenate(
-            [
-                jnp.concatenate([wide[k, pl.ds(2 * t + s, 128, stride=24), :] for k in range(3)], 1)
-                for s in range(2)
-            ],
-            0,
-        ).astype(jnp.bfloat16)
-        result = lax.dot_general(
-            rows, coeff[...], (((0,), (1,)), ((), ())),
-            preferred_element_type=jnp.float32,
-        )
-        out[4 * k : 4 * k + 4] = result.reshape(4, 96, 768).astype(out.dtype)
-
-
-def finish(blocks, coeff):
-    rows = 12
+            wide_head[k] = head[:, k * 128 : (k + 1) * 128].astype(jnp.float32)
+            wide_tail[k] = tail[:, k * 128 : (k + 1) * 128].astype(jnp.float32)
+        run(wide_head, 8, 0)
+
+    @pl.when(step > 0)
+    def _():
+        run(wide_tail, 16, 8 * step - 8)
+
+
+def finish(tail, head, coeff):
+    whole = lambda s: (0, 0)
     return pl.pallas_call(
         finish_body,
-        grid=(48 // rows,),
+        grid=(3,),
         out_shape=jax.ShapeDtypeStruct((48, 96, 768), jnp.bfloat16),
         in_specs=[
-            pl.BlockSpec((128 * 24, 384), lambda s: (0, 0)),
-            pl.BlockSpec((768, 256), lambda s: (0, 0)),
+            pl.BlockSpec((128 * 16, 384), whole),
+            pl.BlockSpec((128 * 8, 384), whole),
+            pl.BlockSpec((768, 256), whole),
         ],
-        out_specs=pl.BlockSpec((rows, 96, 768), lambda s: (s, 0, 0)),
-        scratch_shapes=[pltpu.VMEM((3, 128 * 24, 128), jnp.float32)],
+        out_specs=pl.BlockSpec((16, 96, 768), lambda s: (s, 0, 0)),
+        scratch_shapes=[
+            pltpu.VMEM((3, 128 * 16, 128), jnp.float32),
+            pltpu.VMEM((3, 128 * 8, 128), jnp.float32),
+        ],
         compiler_params=pltpu.CompilerParams(vmem_limit_bytes=32 << 20),
         name="finish",
-    )(blocks, coeff)
+    )(tail, head, coeff)
 
 
 def add(first, *others):
@@ -229,18 +250,16 @@
 
 def local(b_three, e_occ, e_vir, c_occ, pair_list, pair_live):
     device = lax.axis_index("row") * 16 + lax.axis_index("col")
+
+    right_low = send(b_three, "right", 1)
+    right_high = send(b_three, "right", -1)
     own_a, own_b = b_three[0], b_three[1]
-
-    right_low_a = send(own_a, "right", 1)
-    right_high_b = send(own_b, "right", -1)
-    right_low_b = send(own_b, "right", 1)
-    right_high_a = send(own_a, "right", -1)
     info = jnp.concatenate([pair_list.reshape(1, 32), pair_live.reshape(1, 16)], 1)
     tables = [info] + [send(info, "left", step) for step in (1, -1, 2)]
     near_low_a = send(own_a, "left", 1)
     near_high_b = send(own_b, "left", -1)
-    right_far_a = send(right_low_a, "right", 1)
-    right_far_b = send(right_high_b, "right", -1)
+    right_far_a = send(right_low[0], "right", 1)
+    right_far_b = send(right_high[1], "right", -1)
     far_a = send(near_low_a, "left", 1)
     far_b = send(near_high_b, "left", -1)
     own_a, own_b, right_far_a, right_far_b, far_a, far_b = lax.optimization_barrier(
@@ -248,35 +267,33 @@
     )
     late_low_b = send(own_b, "left", 1)
     late_high_a = send(own_a, "left", -1)
-    rights = (
-        None,
-        (right_low_a, right_low_b),
-        (right_high_a, right_high_b),
-        (right_far_a, right_far_b),
-    )
-
-    def partial(lefts, which, slots, dtype=jnp.bfloat16, picks=(0, 1, 2, 3), begun=()):
+    rights = ((), (right_low,), (right_high,), (right_far_a, right_far_b))
+
+    def partial(lefts, which, slots, dtype=jnp.bfloat16, picks=(0, 1, 2, 3), begun=(), split=True):
         scalars = [device.reshape(1)] + [tables[k] for k in which] + [e_occ]
-        return partial_gamma(scalars, e_vir, b_three, lefts, slots, rights, picks, begun, dtype)
+        return partial_gamma(
+            scalars, e_vir, b_three, lefts, slots, rights, picks, begun, dtype, split
+        )
 
     near = (near_low_a, near_high_b)
-    begun = partial(near, (1, 2), (0, 1), jnp.float32, (0, 1, 2))
-    far_a, far_b = partial((far_a, far_b), (3, 3), (0, 1))
-    relay_a = send(far_a, "left", 1)
-    relay_b = send(far_b, "left", -1)
-    low_a, high_b = partial(near, (1, 2), (0, 1), picks=(3,), begun=begun)
-    low_b, high_a = partial((late_low_b, late_high_a), (1, 2), (1, 0))
-    up_b = send(high_b, "left", 1)
-    down_a = send(low_a, "left", -1)
-    joint_a, joint_b = add(high_a, relay_a), add(low_b, relay_b)
-    up_a = send(joint_a, "left", 1)
-    down_b = send(joint_b, "left", -1)
-    sum_a, sum_b = partial((b_three, b_three), (0, 0), (0, 1), jnp.float32)
-
-    blocks = pack(sum_a, sum_b, up_a, down_a, up_b, down_b)
-    moved = lax.all_to_all(blocks, AXES, split_axis=0, concat_axis=0, tiled=True)
+    begun = partial(near, (1, 2), (0, 1), jnp.float32, (0, 1, 2), split=False)
+    far = partial((far_a, far_b), (3, 3), (0, 1))
+    relay = [send(far[k], "left", 1 if k < 2 else -1) for k in range(4)]
+    rest = partial(near, (1, 2), (0, 1), picks=(3,), begun=begun)
+    late = partial((late_low_b, late_high_a), (1, 2), (1, 0))
+    sums = partial((b_three, b_three), (0, 0), (0, 1), jnp.float32)
+    moved = []
+    for k in range(2):
+        up_b = send(rest[2 + k], "left", 1)
+        down_a = send(rest[k], "left", -1)
+        joint_a, joint_b = add(late[2 + k], relay[k]), add(late[k], relay[2 + k])
+        up_a = send(joint_a, "left", 1)
+        down_b = send(joint_b, "left", -1)
+        blocks = pack(sums[k], sums[2 + k], up_a, down_a, up_b, down_b)
+        blocks = lax.all_to_all(blocks, AXES, split_axis=0, concat_axis=0, tiled=True)
+        moved.append(blocks.reshape(-1, 384))
     coeff = c_occ.reshape(-1, 128, 2).transpose(0, 2, 1).reshape(-1, 256)
-    return finish(moved.reshape(128 * 24, 384), coeff)
+    return finish(moved[1], moved[0], coeff)
 
 
 def solution(mesh):

time: 221 us -> 236 us (1.068)
  local copies, waits for them, and re-layouts: 7.95 us -> 22.1 us
  starting transfers between devices: 68.1 us -> 56 us
  waiting for transfers between devices: 97.4 us -> 107 us
  Pallas kernels: 43.4 us -> 46.5 us
    unnamed x17 -> x53, local copies, waits for them, and re-layouts: 3.37 us -> 17.4 us
    all_to_all x1 -> x2, starting transfers between devices: 31.5 us -> 21.6 us  [local(): lax.all_to_all(blocks, AXES, split_axis=0, concat_axis=0, tiled=True)]
    ppermute x21 -> x25, waiting for transfers between devices: 66.1 us -> 73.3 us  [send(): return lax.ppermute(value, AXES, shifted(kind, step))]
    all_to_all x1 -> x2, waiting for transfers between devices: 31.2 us -> 33.9 us  [local(): lax.all_to_all(blocks, AXES, split_axis=0, concat_axis=0, tiled=True)]
    pallas_call x2 -> x3, Pallas kernels: 8.77 us -> 11.2 us  [the longest x2 6.41 us: pack(): pl.pallas_call(pack_body, out_shape=jax.ShapeDtypeStruct((128, height //...]
    ppermute x21 -> x25, starting transfers between devices: 36.5 us -> 34.4 us  [send(): return lax.ppermute(value, AXES, shifted(kind, step))]
  transfers between devices with their start and end apart: 22 -> 27, of which waited for: 12 -> 13; matrix products, arithmetic and copies ran while one was open for 3% -> 4% of each run, Pallas kernels for 16% -> 18%
where the time goes in v4:
time: 236 us; the launch traced here: 235 us
  waiting for transfers between devices  107 us (45%)
  starting transfers between devices  56 us (24%)
  Pallas kernels  46.5 us (20%)
  local copies, waits for them, and re-layouts  22.1 us (9%)
  other arithmetic  3.15 us (1%)
    ppermute x25, waiting for transfers between devices, send(): return lax.ppermute(value, AXES, shifted(kind, step))  73.3 us
    pallas_call x5, Pallas kernels, partial_gamma(): pl.pallas_call(functools.partial(pair_body, slots=slots, picks=picks, sta...  35.2 us
    ppermute x25, starting transfers between devices, send(): return lax.ppermute(value, AXES, shifted(kind, step))  34.4 us
    all_to_all x2, waiting for transfers between devices, local(): lax.all_to_all(blocks, AXES, split_axis=0, concat_axis=0, tiled=True)  33.9 us
    all_to_all x2, starting transfers between devices, local(): lax.all_to_all(blocks, AXES, split_axis=0, concat_axis=0, tiled=True)  21.6 us
    unnamed x53, local copies, waits for them, and re-layouts  17.4 us
    pallas_call x2, Pallas kernels, pack(): pl.pallas_call(pack_body, out_shape=jax.ShapeDtypeStruct((128, height //...  6.41 us
    pallas_call x1, Pallas kernels, finish(): pl.pallas_call(finish_body, grid=(3,), out_shape=jax.ShapeDtypeStruct((48...  4.82 us
  transfers between devices with their start and end apart: 27, of which 13 were waited for; matrix products, arithmetic and copies ran while one was open for 4% of the time, Pallas kernels for 18%

profile of v4, /device:TPU:1, one launch (start us, length us, event | category | flops | bytes accessed | tf_op | source)
XLA Modules:
  0.0 235.2 jit_solution(17500118539186105771)
XLA Ops:
  0.0 2.0 collective-permute-start
  3.3 3.3 %slice_bitcast_fusion.2 = (bf16[384,1536]{1,0:T(8,128)(2,1)}, bf16[384,1536]{1,0:T(8,128)(2,1)}) fusion(bf16[2,384,1536]{2,1,0:T(8,128)(2,1)} %own.9), kind=kLoop, calls=%fused_computation.4 | loop fusion | bytes 4718592 | tf_op jit(solution)/shard_map/squeeze | solution.py:256
  6.6 1.8 collective-permute-start.4
  8.4 2.1 collective-permute-start.6
  10.5 26.7 %collective-permute-done.4.refs_0_ = bf16[384,1536]{1,0:T(8,128)(2,1)S(1)} collective-permute-done((bf16[384,1536]{1,0:T(8,128)(2,1)}, bf16[384,1536]{1,0:T(8,128)(2,1)S(1)}, u32[]{:S(2)}, u32[]{:S(2)}) %collective-permute-start.4) | collective-permute-done | bytes 1179680 | tf_op jit(solution)/shard_map/ppermute | solution.py:28
  38.3 2.7 %collective-permute-start.7 = (bf16[384,1536]{1,0:T(8,128)(2,1)S(1)}, bf16[384,1536]{1,0:T(8,128)(2,1)S(1)}, u32[]{:S(2)}, u32[]{:S(2)}) collective-permute-start(bf16[384,1536]{1,0:T(8,128)(2,1)S(1)} %collective-permute-done.6.refs_1_), channel_id=1, source_target_pairs={{0,3},{1,0},{2,1},{3,2},{4,7},{5,4},{6,5},{7,6},{8,11},{9,8},{10,9... | collective-permute-start | bytes 3538952 | tf_op jit(solution)/shard_map/ppermute | solution.py:28
  44.1 2.1 collective-permute-start.3
  46.2 15.0 %collective-permute-done.5.refs_0_ = bf16[384,1536]{1,0:T(8,128)(2,1)S(1)} collective-permute-done((bf16[384,1536]{1,0:T(8,128)(2,1)S(1)}, bf16[384,1536]{1,0:T(8,128)(2,1)S(1)}, u32[]{:S(2)}, u32[]{:S(2)}) %collective-permute-start.5) | collective-permute-done | bytes 1179680 | tf_op jit(solution)/shard_map/ppermute | solution.py:28
  63.3 5.4 %collective-permute-done.2.refs_4_.refs_2_ = bf16[384,1536]{1,0:T(8,128)(2,1)S(1)} collective-permute-done((bf16[384,1536]{1,0:T(8,128)(2,1)S(1)}, bf16[384,1536]{1,0:T(8,128)(2,1)S(1)}, u32[]{:S(2)}, u32[]{:S(2)}) %collective-permute-start.2) | collective-permute-done | bytes 1179680 | tf_op jit(solution)/shard_map/ppermute | solution.py:28
  70.8 2.2 collective-permute-start.11
  76.3 11.6 %collective-permute-done.12.table_a.table_b = s32[1,48]{1,0:T(1,128)S(1)} collective-permute-done((s32[1,48]{1,0:T(1,128)S(1)}, s32[1,48]{1,0:T(1,128)S(1)}, u32[]{:S(2)}, u32[]{:S(2)}) %collective-permute-start.12) | collective-permute-done | bytes 224 | tf_op jit(solution)/shard_map/ppermute | solution.py:28
  87.9 1.7 copy-done.2
  89.6 1.7 copy-done.5
  95.1 10.1 %shard_map.66 = (bf16[128,1536]{1,0:T(8,128)(2,1)}, bf16[256,1536]{1,0:T(8,128)(2,1)S(1)}, bf16[128,1536]{1,0:T(8,128)(2,1)}, bf16[256,1536]{1,0:T(8,128)(2,1)S(1)}) custom-call(s32[1]{0:T(128)} %bitcast.device, s32[1,48]{1,0:T(1,128)S(1)} %collective-permute-done.12.table_a.table_b, s32[1,48]{1,0:T(1,128)S(1)} %collective-permute-done.12.table_a.table_b, ...), custom_call_target="tpu_custom_call" | custom-call | tf_op jit(solution)/shard_map/pallas_call | solution.py:131
  109.0 3.4 %collective-permute-done.9.table_b = s32[1,48]{1,0:T(1,128)S(1)} collective-permute-done((s32[1,48]{1,0:T(1,128)S(1)}, s32[1,48]{1,0:T(1,128)S(1)}, u32[]{:S(2)}, u32[]{:S(2)}) %collective-permute-start.9) | collective-permute-done | bytes 224 | tf_op jit(solution)/shard_map/ppermute | solution.py:28
  112.4 7.6 %shard_map.67 = (f32[384,1536]{1,0:T(8,128)S(1)}, f32[384,1536]{1,0:T(8,128)S(1)}) custom-call(s32[1]{0:T(128)} %bitcast.device, s32[1,48]{1,0:T(1,128)S(1)} %collective-permute-done.8.table_a, s32[1,48]{1,0:T(1,128)S(1)} %collective-permute-done.9.table_b, f32[256]{0:T(256)S(1)} %copy-done.23, f32[384]{0:T(512)S(1)} %copy-done.22, ...), custom_call_target="tpu_custom_call" | custom-call | tf_op jit(solution)/shard_map/pallas_call | solution.py:131
  121.3 4.8 %shard_map.68 = (bf16[128,1536]{1,0:T(8,128)(2,1)S(1)}, bf16[256,1536]{1,0:T(8,128)(2,1)}, bf16[128,1536]{1,0:T(8,128)(2,1)S(1)}, bf16[256,1536]{1,0:T(8,128)(2,1)}) custom-call(s32[1]{0:T(128)} %bitcast.device, s32[1,48]{1,0:T(1,128)S(1)} %collective-permute-done.8.table_a, s32[1,48]{1,0:T(1,128)S(1)} %collective-permute-done.9.table_b, f32[256]{0:T(256)S(1)} %copy-done.23, ...), custom_call_target="tpu_custom_call" | custom-call | tf_op jit(solution)/shard_map/pallas_call | solution.py:131
  127.7 2.7 %collective-permute-start.17 = (bf16[256,1536]{1,0:T(8,128)(2,1)S(1)}, bf16[256,1536]{1,0:T(8,128)(2,1)S(1)}, u32[]{:S(2)}, u32[]{:S(2)}) collective-permute-start(bf16[256,1536]{1,0:T(8,128)(2,1)S(1)} %get-tuple-element.44), channel_id=1, source_target_pairs={{0,3},{1,0},{2,1},{3,2},{4,7},{5,4},{6,5},{7,6},{8,11},{9,8},{10,9... | collective-permute-start | bytes 2359304 | tf_op jit(solution)/shard_map/ppermute | solution.py:28
  130.3 3.2 %shard_map.65 = (bf16[128,1536]{1,0:T(8,128)(2,1)S(1)}, bf16[256,1536]{1,0:T(8,128)(2,1)S(1)}, bf16[128,1536]{1,0:T(8,128)(2,1)S(1)}, bf16[256,1536]{1,0:T(8,128)(2,1)S(1)}) custom-call(s32[1]{0:T(128)} %bitcast.device, s32[1,48]{1,0:T(1,128)S(1)} %collective-permute-done.8.table_a, s32[1,48]{1,0:T(1,128)S(1)} %collective-permute-done.9.table_b, ...), custom_call_target="tpu_custom_call" | custom-call | tf_op jit(solution)/shard_map/pallas_call | solution.py:131
  133.6 3.7 %collective-permute-start.15 = (bf16[256,1536]{1,0:T(8,128)(2,1)}, bf16[256,1536]{1,0:T(8,128)(2,1)}, u32[]{:S(2)}, u32[]{:S(2)}) collective-permute-start(bf16[256,1536]{1,0:T(8,128)(2,1)} %get-tuple-element.41), channel_id=1, source_target_pairs={{0,3},{1,0},{2,1},{3,2},{4,7},{5,4},{6,5},{7,6},{8,11},{9,8},{10,9... | collective-permute-start | bytes 2359304 | tf_op jit(solution)/shard_map/ppermute | solution.py:28
  137.6 3.6 %collective-permute-done.17 = bf16[256,1536]{1,0:T(8,128)(2,1)S(1)} collective-permute-done((bf16[256,1536]{1,0:T(8,128)(2,1)S(1)}, bf16[256,1536]{1,0:T(8,128)(2,1)S(1)}, u32[]{:S(2)}, u32[]{:S(2)}) %collective-permute-start.17) | collective-permute-done | bytes 786464 | tf_op jit(solution)/shard_map/ppermute | solution.py:28
  141.2 2.7 %collective-permute-start.24 = (bf16[128,1536]{1,0:T(8,128)(2,1)S(1)}, bf16[128,1536]{1,0:T(8,128)(2,1)S(1)}, u32[]{:S(2)}, u32[]{:S(2)}) collective-permute-start(bf16[128,1536]{1,0:T(8,128)(2,1)S(1)} %add_convert_fusion.2), channel_id=1, source_target_pairs={{0,3},{1,0},{2,1},{3,2},{4,7},{5,4},{6,5},{7,6},{8,11},{9,8},{10,9... | collective-permute-start | bytes 1179656 | tf_op jit(solution)/shard_map/ppermute | solution.py:28
  145.0 4.8 %collective-permute-done.13 = bf16[256,1536]{1,0:T(8,128)(2,1)S(1)} collective-permute-done((bf16[256,1536]{1,0:T(8,128)(2,1)S(1)}, bf16[256,1536]{1,0:T(8,128)(2,1)S(1)}, u32[]{:S(2)}, u32[]{:S(2)}) %collective-permute-start.13) | collective-permute-done | bytes 786464 | tf_op jit(solution)/shard_map/ppermute | solution.py:28
  150.9 2.7 %collective-permute-start.18 = (bf16[256,1536]{1,0:T(8,128)(2,1)}, bf16[256,1536]{1,0:T(8,128)(2,1)}, u32[]{:S(2)}, u32[]{:S(2)}) collective-permute-start(bf16[256,1536]{1,0:T(8,128)(2,1)} %add_convert_fusion), channel_id=1, source_target_pairs={{0,3},{1,0},{2,1},{3,2},{4,7},{5,4},{6,5},{7,6},{8,11},{9,8},{10,9... | collective-permute-start | bytes 2359304 | tf_op jit(solution)/shard_map/ppermute | solution.py:28
  154.2 9.5 %shard_map.64 = (f32[128,1536]{1,0:T(8,128)S(1)}, f32[256,1536]{1,0:T(8,128)S(1)}, f32[128,1536]{1,0:T(8,128)S(1)}, f32[256,1536]{1,0:T(8,128)S(1)}) custom-call(s32[1]{0:T(128)} %bitcast.device, s32[1,48]{1,0:T(1,128)S(1)} %pad_add_fusion.table_a.table_b, s32[1,48]{1,0:T(1,128)S(1)} %pad_add_fusion.table_a.table_b, f32[256]{0:T(256)S(1)} %copy-done.23, ...), custom_call_target="tpu_custom_call" | custom-call | tf_op jit(solution)/shard_map/pallas_call | solution.py:131
  166.0 1.7 shard_map.70
  167.8 17.5 %all-to-all-start.1 = ((bf16[128,8,384]{2,1,0:T(8,128)(2,1)}), bf16[128,8,384]{2,1,0:T(8,128)(2,1)S(1)}, u32[]{:S(2)}, u32[]{:S(2)}) async-start(bf16[128,8,384]{2,1,0:T(8,128)(2,1)} %shard_map.70), calls=%async_computation.1 | async-start | bytes 1572864 | tf_op jit(solution)/shard_map/all_to_all | solution.py:293
  186.8 4.7 %shard_map.69 = bf16[128,16,384]{2,1,0:T(8,128)(2,1)} custom-call(f32[256,1536]{1,0:T(8,128)S(1)} %copy-done.15, f32[256,1536]{1,0:T(8,128)S(1)} %copy-done.17, bf16[256,1536]{1,0:T(8,128)(2,1)} %collective-permute-done.14.up_a, bf16[256,1536]{1,0:T(8,128)(2,1)} %collective-permute-done.15.down_a, bf16[256,1536]{1,0:T(8,128)(2,1)} %collective-permute-done.16.up_b, ...), custom_call_target="tpu_custom_call" | custom-call | tf_op jit(solution)/shard_map/pallas_call | solution.py:184
  191.4 10.6 %all-to-all-done.1 = bf16[128,8,384]{2,1,0:T(8,128)(2,1)S(1)} async-done(((bf16[128,8,384]{2,1,0:T(8,128)(2,1)}), bf16[128,8,384]{2,1,0:T(8,128)(2,1)S(1)}, u32[]{:S(2)}, u32[]{:S(2)}) %all-to-all-start.1) | async-done | bytes 786464 | tf_op jit(solution)/shard_map/all_to_all | solution.py:293
  202.1 4.1 %all-to-all-start = ((bf16[128,16,384]{2,1,0:T(8,128)(2,1)}), bf16[128,16,384]{2,1,0:T(8,128)(2,1)S(1)}, u32[]{:S(2)}, u32[]{:S(2)}) async-start(bf16[128,16,384]{2,1,0:T(8,128)(2,1)} %shard_map.69), calls=%async_computation | async-start | bytes 3145728 | tf_op jit(solution)/shard_map/all_to_all | solution.py:293
  207.1 23.3 %all-to-all-done = bf16[128,16,384]{2,1,0:T(8,128)(2,1)S(1)} async-done(((bf16[128,16,384]{2,1,0:T(8,128)(2,1)}), bf16[128,16,384]{2,1,0:T(8,128)(2,1)S(1)}, u32[]{:S(2)}, u32[]{:S(2)}) %all-to-all-start) | async-done | bytes 1572896 | tf_op jit(solution)/shard_map/all_to_all | solution.py:293
  230.4 4.8 %finish.1 = bf16[48,96,768]{2,1,0:T(8,128)(2,1)} custom-call(bf16[2048,384]{1,0:T(8,128)(2,1)S(1)} %bitcast.18, bf16[1024,384]{1,0:T(8,128)(2,1)S(1)} %bitcast.19, bf16[768,256]{1,0:T(8,128)(2,1)S(1)} %bitcast.20), custom_call_target="tpu_custom_call" | custom-call | tf_op jit(solution)/shard_map/finish/pallas_call | solution.py:225
  (94 shorter events, 31.0 us)
Async XLA Ops:
  0.0 42.7 %collective-permute-start = (bf16[2,384,1536]{2,1,0:T(8,128)(2,1)}, bf16[2,384,1536]{2,1,0:T(8,128)(2,1)S(1)}, u32[]{:S(2)}, u32[]{:S(2)}) collective-permute-start(bf16[2,384,1536]{2,1,0:T(8,128)(2,1)} %own.9), channel_id=1, source_target_pairs={{0,4},{1,5},{2,6},{3,7},{4,8},{5,9},{6,10},{7,11},{8,12},{9,13},{1... | collective-permute-start | bytes 7077896 | tf_op jit(solution)/shard_map/ppermute | solution.py:28
  2.0 41.7 %collective-permute-start.1 = (bf16[2,384,1536]{2,1,0:T(8,128)(2,1)}, bf16[2,384,1536]{2,1,0:T(8,128)(2,1)S(1)}, u32[]{:S(2)}, u32[]{:S(2)}) collective-permute-start(bf16[2,384,1536]{2,1,0:T(8,128)(2,1)} %own.9), channel_id=1, source_target_pairs={{0,12},{1,13},{2,14},{3,15},{4,0},{5,1},{6,2},{7,3},{8,4},{9,5},{1... | collective-permute-start | bytes 7077896 | tf_op jit(solution)/shard_map/ppermute | solution.py:28
  6.6 30.7 %collective-permute-start.4 = (bf16[384,1536]{1,0:T(8,128)(2,1)}, bf16[384,1536]{1,0:T(8,128)(2,1)S(1)}, u32[]{:S(2)}, u32[]{:S(2)}) collective-permute-start(bf16[384,1536]{1,0:T(8,128)(2,1)} %get-tuple-element.34), channel_id=1, source_target_pairs={{0,1},{1,2},{2,3},{3,0},{4,5},{5,6},{6,7},{7,4},{8,9},{9,10},{10,1... | collective-permute-start | bytes 3538952 | tf_op jit(solution)/shard_map/ppermute | solution.py:28
  8.4 29.9 %collective-permute-start.6 = (bf16[384,1536]{1,0:T(8,128)(2,1)}, bf16[384,1536]{1,0:T(8,128)(2,1)S(1)}, u32[]{:S(2)}, u32[]{:S(2)}) collective-permute-start(bf16[384,1536]{1,0:T(8,128)(2,1)} %get-tuple-element.33), channel_id=1, source_target_pairs={{0,3},{1,0},{2,1},{3,2},{4,7},{5,4},{6,5},{7,6},{8,11},{9,8},{10,9... | collective-permute-start | bytes 3538952 | tf_op jit(solution)/shard_map/ppermute | solution.py:28
  37.2 24.0 %collective-permute-start.5 = (bf16[384,1536]{1,0:T(8,128)(2,1)S(1)}, bf16[384,1536]{1,0:T(8,128)(2,1)S(1)}, u32[]{:S(2)}, u32[]{:S(2)}) collective-permute-start(bf16[384,1536]{1,0:T(8,128)(2,1)S(1)} %collective-permute-done.4.refs_0_), channel_id=1, source_target_pairs={{0,1},{1,2},{2,3},{3,0},{4,5},{5,6},{6,7},{7,4},{8,9},{9,10},{10,1... | collective-permute-start | bytes 3538952 | tf_op jit(solution)/shard_map/ppermute | solution.py:28
  38.3 23.9 %collective-permute-start.7 = (bf16[384,1536]{1,0:T(8,128)(2,1)S(1)}, bf16[384,1536]{1,0:T(8,128)(2,1)S(1)}, u32[]{:S(2)}, u32[]{:S(2)}) collective-permute-start(bf16[384,1536]{1,0:T(8,128)(2,1)S(1)} %collective-permute-done.6.refs_1_), channel_id=1, source_target_pairs={{0,3},{1,0},{2,1},{3,2},{4,7},{5,4},{6,5},{7,6},{8,11},{9,8},{10,9... | collective-permute-start | bytes 3538952 | tf_op jit(solution)/shard_map/ppermute | solution.py:28
  42.8 45.2 %copy-start = (bf16[2,384,1536]{2,1,0:T(8,128)(2,1)S(1)}, bf16[2,384,1536]{2,1,0:T(8,128)(2,1)}, u32[]{:S(2)}) copy-start(bf16[2,384,1536]{2,1,0:T(8,128)(2,1)} %own.9) | copy-start | bytes 7077892
  42.8 45.2 %copy-start.22 = (f32[384]{0:T(512)S(1)}, f32[384]{0:T(512)}, u32[]{:S(2)}) copy-start(f32[384]{0:T(512)} %levels.9) | copy-start | bytes 4612
  42.8 45.1 %copy-start.23 = (f32[256]{0:T(256)S(1)}, f32[256]{0:T(256)}, u32[]{:S(2)}) copy-start(f32[256]{0:T(256)} %energies.9) | copy-start | bytes 3076
  42.8 25.9 %collective-permute-start.2 = (bf16[384,1536]{1,0:T(8,128)(2,1)S(1)}, bf16[384,1536]{1,0:T(8,128)(2,1)S(1)}, u32[]{:S(2)}, u32[]{:S(2)}) collective-permute-start(bf16[384,1536]{1,0:T(8,128)(2,1)S(1)} %slice_bitcast_fusion.1), channel_id=1, source_target_pairs={{0,4},{1,5},{2,6},{3,7},{4,8},{5,9},{6,10},{7,11},{8,12},{9,13},{1... | collective-permute-start | bytes 3538952 | tf_op jit(solution)/shard_map/ppermute | solution.py:28
  44.1 25.3 %collective-permute-start.3 = (bf16[384,1536]{1,0:T(8,128)(2,1)S(1)}, bf16[384,1536]{1,0:T(8,128)(2,1)S(1)}, u32[]{:S(2)}, u32[]{:S(2)}) collective-permute-start(bf16[384,1536]{1,0:T(8,128)(2,1)S(1)} %slice_bitcast_fusion), channel_id=1, source_target_pairs={{0,12},{1,13},{2,14},{3,15},{4,0},{5,1},{6,2},{7,3},{8,4},{9,5},{1... | collective-permute-start | bytes 3538952 | tf_op jit(solution)/shard_map/ppermute | solution.py:28
  70.4 57.3 %collective-permute-start.10 = (bf16[384,1536]{1,0:T(8,128)(2,1)}, bf16[384,1536]{1,0:T(8,128)(2,1)}, u32[]{:S(2)}, u32[]{:S(2)}) collective-permute-start(bf16[384,1536]{1,0:T(8,128)(2,1)} %get-tuple-element.33), channel_id=1, source_target_pairs={{0,1},{1,2},{2,3},{3,0},{4,5},{5,6},{6,7},{7,4},{8,9},{9,10},{10,1... | collective-permute-start | bytes 3538952 | tf_op jit(solution)/shard_map/ppermute | solution.py:28
  70.8 56.9 %collective-permute-start.11 = (bf16[384,1536]{1,0:T(8,128)(2,1)}, bf16[384,1536]{1,0:T(8,128)(2,1)}, u32[]{:S(2)}, u32[]{:S(2)}) collective-permute-start(bf16[384,1536]{1,0:T(8,128)(2,1)} %get-tuple-element.34), channel_id=1, source_target_pairs={{0,3},{1,0},{2,1},{3,2},{4,7},{5,4},{6,5},{7,6},{8,11},{9,8},{10,9... | collective-permute-start | bytes 3538952 | tf_op jit(solution)/shard_map/ppermute | solution.py:28
  75.2 12.8 %collective-permute-start.12 = (s32[1,48]{1,0:T(1,128)S(1)}, s32[1,48]{1,0:T(1,128)S(1)}, u32[]{:S(2)}, u32[]{:S(2)}) collective-permute-start(s32[1,48]{1,0:T(1,128)S(1)} %pad_add_fusion.table_a.table_b), channel_id=1, source_target_pairs={{0,2},{1,3},{2,0},{3,1},{4,6},{5,7},{6,4},{7,5},{8,10},{9,11},{10,... | collective-permute-start | bytes 584 | tf_op jit(solution)/shard_map/ppermute | solution.py:28
  95.1 17.3 %copy-start.13 = (bf16[384,1536]{1,0:T(8,128)(2,1)S(1)}, bf16[384,1536]{1,0:T(8,128)(2,1)}, u32[]{:S(2)}) copy-start(bf16[384,1536]{1,0:T(8,128)(2,1)} %copy-done.12) | copy-start | bytes 3538948
  105.2 28.4 %collective-permute-start.23 = (bf16[128,1536]{1,0:T(8,128)(2,1)}, bf16[128,1536]{1,0:T(8,128)(2,1)S(1)}, u32[]{:S(2)}, u32[]{:S(2)}) collective-permute-start(bf16[128,1536]{1,0:T(8,128)(2,1)} %get-tuple-element.52), channel_id=1, source_target_pairs={{0,3},{1,0},{2,1},{3,2},{4,7},{5,4},{6,5},{7,6},{8,11},{9,8},{10,9... | collective-permute-start | bytes 1179656 | tf_op jit(solution)/shard_map/ppermute | solution.py:28
  105.3 3.7 %collective-permute-start.8 = (s32[1,48]{1,0:T(1,128)S(1)}, s32[1,48]{1,0:T(1,128)S(1)}, u32[]{:S(2)}, u32[]{:S(2)}) collective-permute-start(s32[1,48]{1,0:T(1,128)S(1)} %pad_add_fusion.table_a.table_b), channel_id=1, source_target_pairs={{0,1},{1,2},{2,3},{3,0},{4,5},{5,6},{6,7},{7,4},{8,9},{9,10},{10,1... | collective-permute-start | bytes 584 | tf_op jit(solution)/shard_map/ppermute | solution.py:28
  106.7 5.7 %collective-permute-start.9 = (s32[1,48]{1,0:T(1,128)S(1)}, s32[1,48]{1,0:T(1,128)S(1)}, u32[]{:S(2)}, u32[]{:S(2)}) collective-permute-start(s32[1,48]{1,0:T(1,128)S(1)} %pad_add_fusion.table_a.table_b), channel_id=1, source_target_pairs={{0,3},{1,0},{2,1},{3,2},{4,7},{5,4},{6,5},{7,6},{8,11},{9,8},{10,9... | collective-permute-start | bytes 584 | tf_op jit(solution)/shard_map/ppermute | solution.py:28
  120.0 17.4 %collective-permute-start.19 = (bf16[128,1536]{1,0:T(8,128)(2,1)}, bf16[128,1536]{1,0:T(8,128)(2,1)S(1)}, u32[]{:S(2)}, u32[]{:S(2)}) collective-permute-start(bf16[128,1536]{1,0:T(8,128)(2,1)} %get-tuple-element.48), channel_id=1, source_target_pairs={{0,1},{1,2},{2,3},{3,0},{4,5},{5,6},{6,7},{7,4},{8,9},{9,10},{10,1... | collective-permute-start | bytes 1179656 | tf_op jit(solution)/shard_map/ppermute | solution.py:28
  126.1 24.8 %collective-permute-start.21 = (bf16[128,1536]{1,0:T(8,128)(2,1)S(1)}, bf16[128,1536]{1,0:T(8,128)(2,1)S(1)}, u32[]{:S(2)}, u32[]{:S(2)}) collective-permute-start(bf16[128,1536]{1,0:T(8,128)(2,1)S(1)} %get-tuple-element.49), channel_id=1, source_target_pairs={{0,3},{1,0},{2,1},{3,2},{4,7},{5,4},{6,5},{7,6},{8,11},{9,8},{10,9... | collective-permute-start | bytes 1179656 | tf_op jit(solution)/shard_map/ppermute | solution.py:28
  127.7 23.3 %collective-permute-start.22 = (bf16[128,1536]{1,0:T(8,128)(2,1)S(1)}, bf16[128,1536]{1,0:T(8,128)(2,1)S(1)}, u32[]{:S(2)}, u32[]{:S(2)}) collective-permute-start(bf16[128,1536]{1,0:T(8,128)(2,1)S(1)} %get-tuple-element.50), channel_id=1, source_target_pairs={{0,1},{1,2},{2,3},{3,0},{4,5},{5,6},{6,7},{7,4},{8,9},{9,10},{10,1... | collective-permute-start | bytes 1179656 | tf_op jit(solution)/shard_map/ppermute | solution.py:28
  127.7 13.6 %collective-permute-start.17 = (bf16[256,1536]{1,0:T(8,128)(2,1)S(1)}, bf16[256,1536]{1,0:T(8,128)(2,1)S(1)}, u32[]{:S(2)}, u32[]{:S(2)}) collective-permute-start(bf16[256,1536]{1,0:T(8,128)(2,1)S(1)} %get-tuple-element.44), channel_id=1, source_target_pairs={{0,3},{1,0},{2,1},{3,2},{4,7},{5,4},{6,5},{7,6},{8,11},{9,8},{10,9... | collective-permute-start | bytes 2359304 | tf_op jit(solution)/shard_map/ppermute | solution.py:28
  133.6 51.7 %collective-permute-start.15 = (bf16[256,1536]{1,0:T(8,128)(2,1)}, bf16[256,1536]{1,0:T(8,128)(2,1)}, u32[]{:S(2)}, u32[]{:S(2)}) collective-permute-start(bf16[256,1536]{1,0:T(8,128)(2,1)} %get-tuple-element.41), channel_id=1, source_target_pairs={{0,3},{1,0},{2,1},{3,2},{4,7},{5,4},{6,5},{7,6},{8,11},{9,8},{10,9... | collective-permute-start | bytes 2359304 | tf_op jit(solution)/shard_map/ppermute | solution.py:28
  137.4 12.4 %collective-permute-start.13 = (bf16[256,1536]{1,0:T(8,128)(2,1)S(1)}, bf16[256,1536]{1,0:T(8,128)(2,1)S(1)}, u32[]{:S(2)}, u32[]{:S(2)}) collective-permute-start(bf16[256,1536]{1,0:T(8,128)(2,1)S(1)} %get-tuple-element.38), channel_id=1, source_target_pairs={{0,1},{1,2},{2,3},{3,0},{4,5},{5,6},{6,7},{7,4},{8,9},{9,10},{10,1... | collective-permute-start | bytes 2359304 | tf_op jit(solution)/shard_map/ppermute | solution.py:28
  141.2 12.9 %collective-permute-start.24 = (bf16[128,1536]{1,0:T(8,128)(2,1)S(1)}, bf16[128,1536]{1,0:T(8,128)(2,1)S(1)}, u32[]{:S(2)}, u32[]{:S(2)}) collective-permute-start(bf16[128,1536]{1,0:T(8,128)(2,1)S(1)} %add_convert_fusion.2), channel_id=1, source_target_pairs={{0,3},{1,0},{2,1},{3,2},{4,7},{5,4},{6,5},{7,6},{8,11},{9,8},{10,9... | collective-permute-start | bytes 1179656 | tf_op jit(solution)/shard_map/ppermute | solution.py:28
  149.9 16.2 %collective-permute-start.20 = (bf16[128,1536]{1,0:T(8,128)(2,1)S(1)}, bf16[128,1536]{1,0:T(8,128)(2,1)S(1)}, u32[]{:S(2)}, u32[]{:S(2)}) collective-permute-start(bf16[128,1536]{1,0:T(8,128)(2,1)S(1)} %add_convert_fusion.3), channel_id=1, source_target_pairs={{0,1},{1,2},{2,3},{3,0},{4,5},{5,6},{6,7},{7,4},{8,9},{9,10},{10,1... | collective-permute-start | bytes 1179656 | tf_op jit(solution)/shard_map/ppermute | solution.py:28
  150.9 34.4 %collective-permute-start.16 = (bf16[256,1536]{1,0:T(8,128)(2,1)}, bf16[256,1536]{1,0:T(8,128)(2,1)}, u32[]{:S(2)}, u32[]{:S(2)}) collective-permute-start(bf16[256,1536]{1,0:T(8,128)(2,1)} %get-tuple-element.42), channel_id=1, source_target_pairs={{0,1},{1,2},{2,3},{3,0},{4,5},{5,6},{6,7},{7,4},{8,9},{9,10},{10,1... | collective-permute-start | bytes 2359304 | tf_op jit(solution)/shard_map/ppermute | solution.py:28
  150.9 34.4 %collective-permute-start.18 = (bf16[256,1536]{1,0:T(8,128)(2,1)}, bf16[256,1536]{1,0:T(8,128)(2,1)}, u32[]{:S(2)}, u32[]{:S(2)}) collective-permute-start(bf16[256,1536]{1,0:T(8,128)(2,1)} %add_convert_fusion), channel_id=1, source_target_pairs={{0,3},{1,0},{2,1},{3,2},{4,7},{5,4},{6,5},{7,6},{8,11},{9,8},{10,9... | collective-permute-start | bytes 2359304 | tf_op jit(solution)/shard_map/ppermute | solution.py:28
  154.2 31.2 %collective-permute-start.14 = (bf16[256,1536]{1,0:T(8,128)(2,1)}, bf16[256,1536]{1,0:T(8,128)(2,1)}, u32[]{:S(2)}, u32[]{:S(2)}) collective-permute-start(bf16[256,1536]{1,0:T(8,128)(2,1)} %add_convert_fusion.1), channel_id=1, source_target_pairs={{0,1},{1,2},{2,3},{3,0},{4,5},{5,6},{6,7},{7,4},{8,9},{9,10},{10,1... | collective-permute-start | bytes 2359304 | tf_op jit(solution)/shard_map/ppermute | solution.py:28
  167.8 17.6 %copy-start.15 = (f32[256,1536]{1,0:T(8,128)S(1)}, f32[256,1536]{1,0:T(8,128)}, u32[]{:S(2)}) copy-start(f32[256,1536]{1,0:T(8,128)} %copy-done.14) | copy-start | bytes 4718596
  167.8 34.3 %all-to-all-start.1 = ((bf16[128,8,384]{2,1,0:T(8,128)(2,1)}), bf16[128,8,384]{2,1,0:T(8,128)(2,1)S(1)}, u32[]{:S(2)}, u32[]{:S(2)}) async-start(bf16[128,8,384]{2,1,0:T(8,128)(2,1)} %shard_map.70), calls=%async_computation.1 | async-start | bytes 1572864 | tf_op jit(solution)/shard_map/all_to_all | solution.py:293
  202.1 28.3 %all-to-all-start = ((bf16[128,16,384]{2,1,0:T(8,128)(2,1)}), bf16[128,16,384]{2,1,0:T(8,128)(2,1)S(1)}, u32[]{:S(2)}, u32[]{:S(2)}) async-start(bf16[128,16,384]{2,1,0:T(8,128)(2,1)} %shard_map.69), calls=%async_computation | async-start | bytes 3145728 | tf_op jit(solution)/shard_map/all_to_all | solution.py:293
  (20 other events, 86.4 us)

commit v5 on v3

--- a/solution.py
+++ b/solution.py
@@ -34,11 +34,14 @@
         lefts = (own.at[0], own.at[1])
     rights = []
     for n in picks:
-        if n == 0:
-            rights += [own.at[0], own.at[1]]
-        else:
+        if n == 3:
             rights += refs[:2]
             refs = refs[2:]
+        elif n:
+            rights += [refs[0].at[0], refs[0].at[1]]
+            refs = refs[1:]
+        else:
+            rights += [own.at[0], own.at[1]]
     begun, refs = refs[: 2 * started], refs[2 * started :]
     out_a, out_b, left_buf, right_buf, gamma, across, left_sem, right_sem = refs
     outs = (out_a, out_b)
@@ -173,7 +176,7 @@
             pltpu.VMEM((24, 384, 128), jnp.float32),
             pltpu.VMEM((6, 192, 128), jnp.float32),
         ],
-        compiler_params=pltpu.CompilerParams(vmem_limit_bytes=32 << 20),
+        compiler_params=pltpu.CompilerParams(vmem_limit_bytes=20 << 20),
         name="pack",
     )(own_a, own_b, up_a, down_a, up_b, down_b)
 
@@ -215,7 +218,7 @@
         ],
         out_specs=pl.BlockSpec((rows, 96, 768), lambda s: (s, 0, 0)),
         scratch_shapes=[pltpu.VMEM((3, 128 * 24, 128), jnp.float32)],
-        compiler_params=pltpu.CompilerParams(vmem_limit_bytes=32 << 20),
+        compiler_params=pltpu.CompilerParams(vmem_limit_bytes=20 << 20),
         name="finish",
     )(blocks, coeff)
 
@@ -229,18 +232,16 @@
 
 def local(b_three, e_occ, e_vir, c_occ, pair_list, pair_live):
     device = lax.axis_index("row") * 16 + lax.axis_index("col")
+
+    right_low = send(b_three, "right", 1)
+    right_high = send(b_three, "right", -1)
     own_a, own_b = b_three[0], b_three[1]
-
-    right_low_a = send(own_a, "right", 1)
-    right_high_b = send(own_b, "right", -1)
-    right_low_b = send(own_b, "right", 1)
-    right_high_a = send(own_a, "right", -1)
     info = jnp.concatenate([pair_list.reshape(1, 32), pair_live.reshape(1, 16)], 1)
     tables = [info] + [send(info, "left", step) for step in (1, -1, 2)]
     near_low_a = send(own_a, "left", 1)
     near_high_b = send(own_b, "left", -1)
-    right_far_a = send(right_low_a, "right", 1)
-    right_far_b = send(right_high_b, "right", -1)
+    right_far_a = send(right_low[0], "right", 1)
+    right_far_b = send(right_high[1], "right", -1)
     far_a = send(near_low_a, "left", 1)
     far_b = send(near_high_b, "left", -1)
     own_a, own_b, right_far_a, right_far_b, far_a, far_b = lax.optimization_barrier(
@@ -248,12 +249,7 @@
     )
     late_low_b = send(own_b, "left", 1)
     late_high_a = send(own_a, "left", -1)
-    rights = (
-        None,
-        (right_low_a, right_low_b),
-        (right_high_a, right_high_b),
-        (right_far_a, right_far_b),
-    )
+    rights = ((), (right_low,), (right_high,), (right_far_a, right_far_b))
 
     def partial(lefts, which, slots, dtype=jnp.bfloat16, picks=(0, 1, 2, 3), begun=()):
         scalars = [device.reshape(1)] + [tables[k] for k in which] + [e_occ]
@@ -264,13 +260,12 @@
     far_a, far_b = partial((far_a, far_b), (3, 3), (0, 1))
     relay_a = send(far_a, "left", 1)
     relay_b = send(far_b, "left", -1)
+    low_b, high_a = partial((late_low_b, late_high_a), (1, 2), (1, 0))
+    up_a = send(add(high_a, relay_a), "left", 1)
+    down_b = send(add(low_b, relay_b), "left", -1)
     low_a, high_b = partial(near, (1, 2), (0, 1), picks=(3,), begun=begun)
-    low_b, high_a = partial((late_low_b, late_high_a), (1, 2), (1, 0))
     up_b = send(high_b, "left", 1)
     down_a = send(low_a, "left", -1)
-    joint_a, joint_b = add(high_a, relay_a), add(low_b, relay_b)
-    up_a = send(joint_a, "left", 1)
-    down_b = send(joint_b, "left", -1)
     sum_a, sum_b = partial((b_three, b_three), (0, 0), (0, 1), jnp.float32)
 
     blocks = pack(sum_a, sum_b, up_a, down_a, up_b, down_b)

time: 221 us -> 210 us (0.950)
  starting transfers between devices: 68.1 us -> 49.1 us
  local copies, waits for them, and re-layouts: 7.95 us -> 11.8 us
  Pallas kernels: 43.4 us -> 46.7 us
    all_to_all x1, starting transfers between devices: 31.5 us -> 17.3 us  [local(): lax.all_to_all(blocks, AXES, split_axis=0, concat_axis=0, tiled=True)]
    ppermute x21 -> x19, starting transfers between devices: 36.5 us -> 31.7 us  [send(): return lax.ppermute(value, AXES, shifted(kind, step))]
    pallas_call x5, Pallas kernels: 34.6 us -> 38 us  [partial_gamma(): pl.pallas_call(functools.partial(pair_body, slots=slots, picks=picks, sta...]
    unnamed x17 -> x27, local copies, waits for them, and re-layouts: 3.37 us -> 6.29 us
    squeeze x0 -> x2, local copies, waits for them, and re-layouts: none -> 2.45 us  [the longest x1 1.27 us: local(): right_far_a = send(right_low[0], 'right', 1)]
    ppermute x21 -> x19, waiting for transfers between devices: 66.1 us -> 66.5 us  [send(): return lax.ppermute(value, AXES, shifted(kind, step))]
  transfers between devices with their start and end apart: 22 -> 20, of which waited for: 12 -> 9; matrix products, arithmetic and copies ran while one was open for 3% -> 5% of each run, Pallas kernels for 16% -> 18%
where the time goes in v5:
time: 210 us; the launch traced here: 209 us
  waiting for transfers between devices  97.7 us (47%)
  starting transfers between devices  49.1 us (23%)
  Pallas kernels  46.7 us (22%)
  local copies, waits for them, and re-layouts  11.8 us (6%)
  other arithmetic  4 us (2%)
    ppermute x19, waiting for transfers between devices, send(): return lax.ppermute(value, AXES, shifted(kind, step))  66.5 us
    pallas_call x5, Pallas kernels, partial_gamma(): pl.pallas_call(functools.partial(pair_body, slots=slots, picks=picks, sta...  38 us
    ppermute x19, starting transfers between devices, send(): return lax.ppermute(value, AXES, shifted(kind, step))  31.7 us
    all_to_all x1, waiting for transfers between devices, local(): lax.all_to_all(blocks, AXES, split_axis=0, concat_axis=0, tiled=True)  31.2 us
    all_to_all x1, starting transfers between devices, local(): lax.all_to_all(blocks, AXES, split_axis=0, concat_axis=0, tiled=True)  17.3 us
    unnamed x27, local copies, waits for them, and re-layouts  6.29 us
    pallas_call x1, Pallas kernels, finish(): pl.pallas_call(finish_body, grid=(48 // rows,), out_shape=jax.ShapeDtypeS...  4.76 us
  transfers between devices with their start and end apart: 20, of which 9 were waited for; matrix products, arithmetic and copies ran while one was open for 5% of the time, Pallas kernels for 18%

profile of v5, /device:TPU:1, one launch (start us, length us, event | category | flops | bytes accessed | tf_op | source)
XLA Modules:
  0.0 209.4 jit_solution(18310032412448284473)
XLA Ops:
  0.0 2.0 collective-permute-start
  3.3 1.8 slice_bitcast_fusion.2
  5.1 1.9 collective-permute-start.4
  7.0 2.2 %collective-permute-start.6 = (bf16[384,1536]{1,0:T(8,128)(2,1)S(1)}, bf16[384,1536]{1,0:T(8,128)(2,1)}, u32[]{:S(2)}, u32[]{:S(2)}) collective-permute-start(bf16[384,1536]{1,0:T(8,128)(2,1)S(1)} %get-tuple-element.25), channel_id=1, source_target_pairs={{0,3},{1,0},{2,1},{3,2},{4,7},{5,4},{6,5},{7,6},{8,11},{9,8},{10,9... | collective-permute-start | bytes 3538952 | tf_op jit(solution)/shard_map/ppermute | solution.py:27
  9.2 26.5 %collective-permute-done.4.refs_0_ = bf16[384,1536]{1,0:T(8,128)(2,1)} collective-permute-done((bf16[384,1536]{1,0:T(8,128)(2,1)S(1)}, bf16[384,1536]{1,0:T(8,128)(2,1)}, u32[]{:S(2)}, u32[]{:S(2)}) %collective-permute-start.4) | collective-permute-done | bytes 1179680 | tf_op jit(solution)/shard_map/ppermute | solution.py:27
  35.8 2.7 %collective-permute-start.7 = (bf16[384,1536]{1,0:T(8,128)(2,1)}, bf16[384,1536]{1,0:T(8,128)(2,1)}, u32[]{:S(2)}, u32[]{:S(2)}) collective-permute-start(bf16[384,1536]{1,0:T(8,128)(2,1)} %collective-permute-done.6.refs_1_), channel_id=1, source_target_pairs={{0,3},{1,0},{2,1},{3,2},{4,7},{5,4},{6,5},{7,6},{8,11},{9,8},{10,9... | collective-permute-start | bytes 3538952 | tf_op jit(solution)/shard_map/ppermute | solution.py:27
  38.5 4.8 %collective-permute-done.refs_2_ = bf16[2,384,1536]{2,1,0:T(8,128)(2,1)S(1)} collective-permute-done((bf16[2,384,1536]{2,1,0:T(8,128)(2,1)}, bf16[2,384,1536]{2,1,0:T(8,128)(2,1)S(1)}, u32[]{:S(2)}, u32[]{:S(2)}) %collective-permute-start) | collective-permute-done | bytes 2359328 | tf_op jit(solution)/shard_map/ppermute | solution.py:27
  45.1 1.6 collective-permute-start.2
  47.9 1.4 copy-done.4
  52.7 5.8 %collective-permute-start.12 = (s32[1,48]{1,0:T(1,128)S(1)}, s32[1,48]{1,0:T(1,128)S(1)}, u32[]{:S(2)}, u32[]{:S(2)}) collective-permute-start(s32[1,48]{1,0:T(1,128)S(1)} %pad_add_fusion.table_a.table_b), channel_id=1, source_target_pairs={{0,2},{1,3},{2,0},{3,1},{4,6},{5,7},{6,4},{7,5},{8,10},{9,11},{10,... | collective-permute-start | bytes 584 | tf_op jit(solution)/shard_map/ppermute | solution.py:27
  58.5 9.5 %collective-permute-done.2.refs_4_.refs_2_ = bf16[384,1536]{1,0:T(8,128)(2,1)S(1)} collective-permute-done((bf16[384,1536]{1,0:T(8,128)(2,1)}, bf16[384,1536]{1,0:T(8,128)(2,1)S(1)}, u32[]{:S(2)}, u32[]{:S(2)}) %collective-permute-start.2) | collective-permute-done | bytes 1179680 | tf_op jit(solution)/shard_map/ppermute | solution.py:27
  68.3 1.6 collective-permute-start.10
  69.9 2.1 %collective-permute-start.11 = (bf16[384,1536]{1,0:T(8,128)(2,1)}, bf16[384,1536]{1,0:T(8,128)(2,1)S(1)}, u32[]{:S(2)}, u32[]{:S(2)}) collective-permute-start(bf16[384,1536]{1,0:T(8,128)(2,1)} %copy-done.9), channel_id=1, source_target_pairs={{0,3},{1,0},{2,1},{3,2},{4,7},{5,4},{6,5},{7,6},{8,11},{9,8},{10,9... | collective-permute-start | bytes 3538952 | tf_op jit(solution)/shard_map/ppermute | solution.py:27
  72.1 1.7 copy-done.2
  73.7 1.7 copy-done.5
  75.4 11.6 %shard_map.66 = (bf16[384,1536]{1,0:T(8,128)(2,1)}, bf16[384,1536]{1,0:T(8,128)(2,1)}) custom-call(s32[1]{0:T(128)} %bitcast.device, s32[1,48]{1,0:T(1,128)S(1)} %collective-permute-done.12.table_a.table_b, s32[1,48]{1,0:T(1,128)S(1)} %collective-permute-done.12.table_a.table_b, f32[256]{0:T(256)S(1)} %copy-done.8, f32[384]{0:T(512)S(1)} %copy-done.7, ...), custom_call_target="tpu_custom_call" | custom-call | tf_op jit(solution)/shard_map/pallas_call | solution.py:121
  87.0 1.5 collective-permute-start.13
  88.5 15.5 %collective-permute-done.8.table_a = s32[1,48]{1,0:T(1,128)S(1)} collective-permute-done((s32[1,48]{1,0:T(1,128)S(1)}, s32[1,48]{1,0:T(1,128)S(1)}, u32[]{:S(2)}, u32[]{:S(2)}) %collective-permute-start.8) | collective-permute-done | bytes 224 | tf_op jit(solution)/shard_map/ppermute | solution.py:27
  104.5 2.3 %collective-permute-done.9.table_b = s32[1,48]{1,0:T(1,128)S(1)} collective-permute-done((s32[1,48]{1,0:T(1,128)S(1)}, s32[1,48]{1,0:T(1,128)S(1)}, u32[]{:S(2)}, u32[]{:S(2)}) %collective-permute-start.9) | collective-permute-done | bytes 224 | tf_op jit(solution)/shard_map/ppermute | solution.py:27
  106.8 8.6 %shard_map.67 = (f32[384,1536]{1,0:T(8,128)S(1)}, f32[384,1536]{1,0:T(8,128)S(1)}) custom-call(s32[1]{0:T(128)} %bitcast.device, s32[1,48]{1,0:T(1,128)S(1)} %collective-permute-done.8.table_a, s32[1,48]{1,0:T(1,128)S(1)} %collective-permute-done.9.table_b, f32[256]{0:T(256)S(1)} %copy-done.8, f32[384]{0:T(512)S(1)} %copy-done.7, ...), custom_call_target="tpu_custom_call" | custom-call | tf_op jit(solution)/shard_map/pallas_call | solution.py:121
  115.4 6.2 %shard_map.68 = (bf16[384,1536]{1,0:T(8,128)(2,1)}, bf16[384,1536]{1,0:T(8,128)(2,1)}) custom-call(s32[1]{0:T(128)} %bitcast.device, s32[1,48]{1,0:T(1,128)S(1)} %collective-permute-done.8.table_a, s32[1,48]{1,0:T(1,128)S(1)} %collective-permute-done.9.table_b, f32[256]{0:T(256)S(1)} %copy-done.8, f32[384]{0:T(512)S(1)} %copy-done.7, ...), custom_call_target="tpu_custom_call" | custom-call | tf_op jit(solution)/shard_map/pallas_call | solution.py:121
  121.8 2.1 collective-permute-start.16
  123.8 2.1 %shard_map.65 = (bf16[384,1536]{1,0:T(8,128)(2,1)S(1)}, bf16[384,1536]{1,0:T(8,128)(2,1)S(1)}) custom-call(s32[1]{0:T(128)} %bitcast.device, s32[1,48]{1,0:T(1,128)S(1)} %collective-permute-done.8.table_a, s32[1,48]{1,0:T(1,128)S(1)} %collective-permute-done.9.table_b, f32[256]{0:T(256)S(1)} %copy-done.8, f32[384]{0:T(512)S(1)} %copy-done.7, ...), custom_call_target="tpu_custom_call" | custom-call | tf_op jit(solution)/shard_map/pallas_call | solution.py:121
  126.0 1.6 add_convert_fusion
  127.5 4.4 %collective-permute-start.18 = (bf16[384,1536]{1,0:T(8,128)(2,1)S(1)}, bf16[384,1536]{1,0:T(8,128)(2,1)S(1)}, u32[]{:S(2)}, u32[]{:S(2)}) collective-permute-start(bf16[384,1536]{1,0:T(8,128)(2,1)S(1)} %add_convert_fusion), channel_id=1, source_target_pairs={{0,3},{1,0},{2,1},{3,2},{4,7},{5,4},{6,5},{7,6},{8,11},{9,8},{10,9... | collective-permute-start | bytes 3538952 | tf_op jit(solution)/shard_map/ppermute | solution.py:27
  131.9 1.7 add_convert_fusion.1
  134.2 9.5 %shard_map.64 = (f32[384,1536]{1,0:T(8,128)S(1)}, f32[384,1536]{1,0:T(8,128)S(1)}) custom-call(s32[1]{0:T(128)} %bitcast.device, s32[1,48]{1,0:T(1,128)S(1)} %pad_add_fusion.table_a.table_b, s32[1,48]{1,0:T(1,128)S(1)} %pad_add_fusion.table_a.table_b, f32[256]{0:T(256)S(1)} %copy-done.8, f32[384]{0:T(512)S(1)} %copy-done.7, ...), custom_call_target="tpu_custom_call" | custom-call | tf_op jit(solution)/shard_map/pallas_call | solution.py:121
  143.7 6.8 %collective-permute-done.18.down_b = bf16[384,1536]{1,0:T(8,128)(2,1)S(1)} collective-permute-done((bf16[384,1536]{1,0:T(8,128)(2,1)S(1)}, bf16[384,1536]{1,0:T(8,128)(2,1)S(1)}, u32[]{:S(2)}, u32[]{:S(2)}) %collective-permute-start.18) | collective-permute-done | bytes 1179680 | tf_op jit(solution)/shard_map/ppermute | solution.py:27
  151.2 4.0 %pack.1 = bf16[128,24,384]{2,1,0:T(8,128)(2,1)} custom-call(f32[384,1536]{1,0:T(8,128)S(1)} %get-tuple-element.23.own_a, f32[384,1536]{1,0:T(8,128)S(1)} %get-tuple-element.24.own_b, bf16[384,1536]{1,0:T(8,128)(2,1)S(1)} %collective-permute-done.14.up_a, bf16[384,1536]{1,0:T(8,128)(2,1)S(1)} %collective-permute-done.15.down_a, ...), custom_call_target="tpu_custom_call" | custom-call | tf_op jit(solution)/shard_map/pack/pallas_call | solution.py:170
  155.2 17.3 %all-to-all-start = ((bf16[128,24,384]{2,1,0:T(8,128)(2,1)}), bf16[128,24,384]{2,1,0:T(8,128)(2,1)S(1)}, u32[]{:S(2)}, u32[]{:S(2)}) async-start(bf16[128,24,384]{2,1,0:T(8,128)(2,1)} %pack.1), calls=%async_computation | async-start | bytes 4718592 | tf_op jit(solution)/shard_map/all_to_all | solution.py:272
  173.5 31.2 %all-to-all-done = bf16[128,24,384]{2,1,0:T(8,128)(2,1)S(1)} async-done(((bf16[128,24,384]{2,1,0:T(8,128)(2,1)}), bf16[128,24,384]{2,1,0:T(8,128)(2,1)S(1)}, u32[]{:S(2)}, u32[]{:S(2)}) %all-to-all-start) | async-done | bytes 2359328 | tf_op jit(solution)/shard_map/all_to_all | solution.py:272
  204.7 4.8 %finish.1 = bf16[48,96,768]{2,1,0:T(8,128)(2,1)} custom-call(bf16[3072,384]{1,0:T(8,128)(2,1)S(1)} %bitcast.17, bf16[768,256]{1,0:T(8,128)(2,1)S(1)} %bitcast.18), custom_call_target="tpu_custom_call" | custom-call | tf_op jit(solution)/shard_map/finish/pallas_call | solution.py:211
  (51 shorter events, 10.9 us)
Async XLA Ops:
  0.0 43.3 %collective-permute-start = (bf16[2,384,1536]{2,1,0:T(8,128)(2,1)}, bf16[2,384,1536]{2,1,0:T(8,128)(2,1)S(1)}, u32[]{:S(2)}, u32[]{:S(2)}) collective-permute-start(bf16[2,384,1536]{2,1,0:T(8,128)(2,1)} %own.9), channel_id=1, source_target_pairs={{0,4},{1,5},{2,6},{3,7},{4,8},{5,9},{6,10},{7,11},{8,12},{9,13},{1... | collective-permute-start | bytes 7077896 | tf_op jit(solution)/shard_map/ppermute | solution.py:27
  2.0 44.7 %collective-permute-start.1 = (bf16[2,384,1536]{2,1,0:T(8,128)(2,1)}, bf16[2,384,1536]{2,1,0:T(8,128)(2,1)S(1)}, u32[]{:S(2)}, u32[]{:S(2)}) collective-permute-start(bf16[2,384,1536]{2,1,0:T(8,128)(2,1)} %own.9), channel_id=1, source_target_pairs={{0,12},{1,13},{2,14},{3,15},{4,0},{5,1},{6,2},{7,3},{8,4},{9,5},{1... | collective-permute-start | bytes 7077896 | tf_op jit(solution)/shard_map/ppermute | solution.py:27
  5.1 42.8 %copy-start.9 = (bf16[384,1536]{1,0:T(8,128)(2,1)}, bf16[384,1536]{1,0:T(8,128)(2,1)S(1)}, u32[]{:S(2)}) copy-start(bf16[384,1536]{1,0:T(8,128)(2,1)S(1)} %get-tuple-element.26) | copy-start | bytes 3538948
  5.1 42.8 %copy-start.10 = (bf16[384,1536]{1,0:T(8,128)(2,1)}, bf16[384,1536]{1,0:T(8,128)(2,1)S(1)}, u32[]{:S(2)}) copy-start(bf16[384,1536]{1,0:T(8,128)(2,1)S(1)} %get-tuple-element.25) | copy-start | bytes 3538948
  5.1 30.7 %collective-permute-start.4 = (bf16[384,1536]{1,0:T(8,128)(2,1)S(1)}, bf16[384,1536]{1,0:T(8,128)(2,1)}, u32[]{:S(2)}, u32[]{:S(2)}) collective-permute-start(bf16[384,1536]{1,0:T(8,128)(2,1)S(1)} %get-tuple-element.26), channel_id=1, source_target_pairs={{0,1},{1,2},{2,3},{3,0},{4,5},{5,6},{6,7},{7,4},{8,9},{9,10},{10,1... | collective-permute-start | bytes 3538952 | tf_op jit(solution)/shard_map/ppermute | solution.py:27
  7.0 28.8 %collective-permute-start.6 = (bf16[384,1536]{1,0:T(8,128)(2,1)S(1)}, bf16[384,1536]{1,0:T(8,128)(2,1)}, u32[]{:S(2)}, u32[]{:S(2)}) collective-permute-start(bf16[384,1536]{1,0:T(8,128)(2,1)S(1)} %get-tuple-element.25), channel_id=1, source_target_pairs={{0,3},{1,0},{2,1},{3,2},{4,7},{5,4},{6,5},{7,6},{8,11},{9,8},{10,9... | collective-permute-start | bytes 3538952 | tf_op jit(solution)/shard_map/ppermute | solution.py:27
  35.8 22.7 %collective-permute-start.5 = (bf16[384,1536]{1,0:T(8,128)(2,1)}, bf16[384,1536]{1,0:T(8,128)(2,1)}, u32[]{:S(2)}, u32[]{:S(2)}) collective-permute-start(bf16[384,1536]{1,0:T(8,128)(2,1)} %collective-permute-done.4.refs_0_), channel_id=1, source_target_pairs={{0,1},{1,2},{2,3},{3,0},{4,5},{5,6},{6,7},{7,4},{8,9},{9,10},{10,1... | collective-permute-start | bytes 3538952 | tf_op jit(solution)/shard_map/ppermute | solution.py:27
  35.8 22.7 %collective-permute-start.7 = (bf16[384,1536]{1,0:T(8,128)(2,1)}, bf16[384,1536]{1,0:T(8,128)(2,1)}, u32[]{:S(2)}, u32[]{:S(2)}) collective-permute-start(bf16[384,1536]{1,0:T(8,128)(2,1)} %collective-permute-done.6.refs_1_), channel_id=1, source_target_pairs={{0,3},{1,0},{2,1},{3,2},{4,7},{5,4},{6,5},{7,6},{8,11},{9,8},{10,9... | collective-permute-start | bytes 3538952 | tf_op jit(solution)/shard_map/ppermute | solution.py:27
  43.3 1.8 copy-start.1
  45.1 26.9 %copy-start = (bf16[2,384,1536]{2,1,0:T(8,128)(2,1)S(1)}, bf16[2,384,1536]{2,1,0:T(8,128)(2,1)}, u32[]{:S(2)}) copy-start(bf16[2,384,1536]{2,1,0:T(8,128)(2,1)} %own.9) | copy-start | bytes 7077892
  45.1 26.9 %copy-start.7 = (f32[384]{0:T(512)S(1)}, f32[384]{0:T(512)}, u32[]{:S(2)}) copy-start(f32[384]{0:T(512)} %levels.9) | copy-start | bytes 4612
  45.1 26.9 %copy-start.8 = (f32[256]{0:T(256)S(1)}, f32[256]{0:T(256)}, u32[]{:S(2)}) copy-start(f32[256]{0:T(256)} %energies.9) | copy-start | bytes 3076
  45.1 22.9 %collective-permute-start.2 = (bf16[384,1536]{1,0:T(8,128)(2,1)}, bf16[384,1536]{1,0:T(8,128)(2,1)S(1)}, u32[]{:S(2)}, u32[]{:S(2)}) collective-permute-start(bf16[384,1536]{1,0:T(8,128)(2,1)} %slice_bitcast_fusion.1), channel_id=1, source_target_pairs={{0,4},{1,5},{2,6},{3,7},{4,8},{5,9},{6,10},{7,11},{8,12},{9,13},{1... | collective-permute-start | bytes 3538952 | tf_op jit(solution)/shard_map/ppermute | solution.py:27
  47.9 1.4 copy-start.4
  49.3 19.0 %collective-permute-start.3 = (bf16[384,1536]{1,0:T(8,128)(2,1)}, bf16[384,1536]{1,0:T(8,128)(2,1)}, u32[]{:S(2)}, u32[]{:S(2)}) collective-permute-start(bf16[384,1536]{1,0:T(8,128)(2,1)} %slice_bitcast_fusion), channel_id=1, source_target_pairs={{0,12},{1,13},{2,14},{3,15},{4,0},{5,1},{6,2},{7,3},{8,4},{9,5},{1... | collective-permute-start | bytes 3538952 | tf_op jit(solution)/shard_map/ppermute | solution.py:27
  52.7 19.4 %collective-permute-start.12 = (s32[1,48]{1,0:T(1,128)S(1)}, s32[1,48]{1,0:T(1,128)S(1)}, u32[]{:S(2)}, u32[]{:S(2)}) collective-permute-start(s32[1,48]{1,0:T(1,128)S(1)} %pad_add_fusion.table_a.table_b), channel_id=1, source_target_pairs={{0,2},{1,3},{2,0},{3,1},{4,6},{5,7},{6,4},{7,5},{8,10},{9,11},{10,... | collective-permute-start | bytes 584 | tf_op jit(solution)/shard_map/ppermute | solution.py:27
  68.3 53.5 %collective-permute-start.10 = (bf16[384,1536]{1,0:T(8,128)(2,1)}, bf16[384,1536]{1,0:T(8,128)(2,1)S(1)}, u32[]{:S(2)}, u32[]{:S(2)}) collective-permute-start(bf16[384,1536]{1,0:T(8,128)(2,1)} %copy-done.10), channel_id=1, source_target_pairs={{0,1},{1,2},{2,3},{3,0},{4,5},{5,6},{6,7},{7,4},{8,9},{9,10},{10,1... | collective-permute-start | bytes 3538952 | tf_op jit(solution)/shard_map/ppermute | solution.py:27
  69.9 53.9 %collective-permute-start.11 = (bf16[384,1536]{1,0:T(8,128)(2,1)}, bf16[384,1536]{1,0:T(8,128)(2,1)S(1)}, u32[]{:S(2)}, u32[]{:S(2)}) collective-permute-start(bf16[384,1536]{1,0:T(8,128)(2,1)} %copy-done.9), channel_id=1, source_target_pairs={{0,3},{1,0},{2,1},{3,2},{4,7},{5,4},{6,5},{7,6},{8,11},{9,8},{10,9... | collective-permute-start | bytes 3538952 | tf_op jit(solution)/shard_map/ppermute | solution.py:27
  72.0 1.7 copy-start.2
  73.7 1.7 copy-start.5
  87.0 39.0 %collective-permute-start.17 = (bf16[384,1536]{1,0:T(8,128)(2,1)}, bf16[384,1536]{1,0:T(8,128)(2,1)}, u32[]{:S(2)}, u32[]{:S(2)}) collective-permute-start(bf16[384,1536]{1,0:T(8,128)(2,1)} %get-tuple-element.36), channel_id=1, source_target_pairs={{0,3},{1,0},{2,1},{3,2},{4,7},{5,4},{6,5},{7,6},{8,11},{9,8},{10,9... | collective-permute-start | bytes 3538952 | tf_op jit(solution)/shard_map/ppermute | solution.py:27
  87.0 44.9 %collective-permute-start.13 = (bf16[384,1536]{1,0:T(8,128)(2,1)}, bf16[384,1536]{1,0:T(8,128)(2,1)}, u32[]{:S(2)}, u32[]{:S(2)}) collective-permute-start(bf16[384,1536]{1,0:T(8,128)(2,1)} %get-tuple-element.30), channel_id=1, source_target_pairs={{0,1},{1,2},{2,3},{3,0},{4,5},{5,6},{6,7},{7,4},{8,9},{9,10},{10,1... | collective-permute-start | bytes 3538952 | tf_op jit(solution)/shard_map/ppermute | solution.py:27
  88.5 15.5 %collective-permute-start.8 = (s32[1,48]{1,0:T(1,128)S(1)}, s32[1,48]{1,0:T(1,128)S(1)}, u32[]{:S(2)}, u32[]{:S(2)}) collective-permute-start(s32[1,48]{1,0:T(1,128)S(1)} %pad_add_fusion.table_a.table_b), channel_id=1, source_target_pairs={{0,1},{1,2},{2,3},{3,0},{4,5},{5,6},{6,7},{7,4},{8,9},{9,10},{10,1... | collective-permute-start | bytes 584 | tf_op jit(solution)/shard_map/ppermute | solution.py:27
  104.0 2.8 %collective-permute-start.9 = (s32[1,48]{1,0:T(1,128)S(1)}, s32[1,48]{1,0:T(1,128)S(1)}, u32[]{:S(2)}, u32[]{:S(2)}) collective-permute-start(s32[1,48]{1,0:T(1,128)S(1)} %pad_add_fusion.table_a.table_b), channel_id=1, source_target_pairs={{0,3},{1,0},{2,1},{3,2},{4,7},{5,4},{6,5},{7,6},{8,11},{9,8},{10,9... | collective-permute-start | bytes 584 | tf_op jit(solution)/shard_map/ppermute | solution.py:27
  115.4 8.4 %copy-start.6 = (bf16[2,384,1536]{2,1,0:T(8,128)(2,1)S(1)}, bf16[2,384,1536]{2,1,0:T(8,128)(2,1)}, u32[]{:S(2)}) copy-start(bf16[2,384,1536]{2,1,0:T(8,128)(2,1)} %copy-done.4) | copy-start | bytes 7077892
  121.7 22.0 %collective-permute-start.15 = (bf16[384,1536]{1,0:T(8,128)(2,1)}, bf16[384,1536]{1,0:T(8,128)(2,1)S(1)}, u32[]{:S(2)}, u32[]{:S(2)}) collective-permute-start(bf16[384,1536]{1,0:T(8,128)(2,1)} %get-tuple-element.33), channel_id=1, source_target_pairs={{0,3},{1,0},{2,1},{3,2},{4,7},{5,4},{6,5},{7,6},{8,11},{9,8},{10,9... | collective-permute-start | bytes 3538952 | tf_op jit(solution)/shard_map/ppermute | solution.py:27
  121.8 21.9 %collective-permute-start.16 = (bf16[384,1536]{1,0:T(8,128)(2,1)}, bf16[384,1536]{1,0:T(8,128)(2,1)S(1)}, u32[]{:S(2)}, u32[]{:S(2)}) collective-permute-start(bf16[384,1536]{1,0:T(8,128)(2,1)} %get-tuple-element.34), channel_id=1, source_target_pairs={{0,1},{1,2},{2,3},{3,0},{4,5},{5,6},{6,7},{7,4},{8,9},{9,10},{10,1... | collective-permute-start | bytes 3538952 | tf_op jit(solution)/shard_map/ppermute | solution.py:27
  127.5 22.9 %collective-permute-start.18 = (bf16[384,1536]{1,0:T(8,128)(2,1)S(1)}, bf16[384,1536]{1,0:T(8,128)(2,1)S(1)}, u32[]{:S(2)}, u32[]{:S(2)}) collective-permute-start(bf16[384,1536]{1,0:T(8,128)(2,1)S(1)} %add_convert_fusion), channel_id=1, source_target_pairs={{0,3},{1,0},{2,1},{3,2},{4,7},{5,4},{6,5},{7,6},{8,11},{9,8},{10,9... | collective-permute-start | bytes 3538952 | tf_op jit(solution)/shard_map/ppermute | solution.py:27
  131.9 2.3 %copy-start.3 = (bf16[2,384,1536]{2,1,0:T(8,128)(2,1)S(1)}, bf16[2,384,1536]{2,1,0:T(8,128)(2,1)}, u32[]{:S(2)}) copy-start(bf16[2,384,1536]{2,1,0:T(8,128)(2,1)} %copy-done.1) | copy-start | bytes 7077892
  133.6 17.6 %collective-permute-start.14 = (bf16[384,1536]{1,0:T(8,128)(2,1)S(1)}, bf16[384,1536]{1,0:T(8,128)(2,1)S(1)}, u32[]{:S(2)}, u32[]{:S(2)}) collective-permute-start(bf16[384,1536]{1,0:T(8,128)(2,1)S(1)} %add_convert_fusion.1), channel_id=1, source_target_pairs={{0,1},{1,2},{2,3},{3,0},{4,5},{5,6},{6,7},{7,4},{8,9},{9,10},{10,1... | collective-permute-start | bytes 3538952 | tf_op jit(solution)/shard_map/ppermute | solution.py:27
  155.2 17.3 %copy-start.11 = (bf16[768,256]{1,0:T(8,128)(2,1)S(1)}, bf16[768,256]{1,0:T(8,128)(2,1)}, u32[]{:S(2)}) copy-start(bf16[768,256]{1,0:T(8,128)(2,1)} %param.9) | copy-start | bytes 1179652
  155.2 49.5 %all-to-all-start = ((bf16[128,24,384]{2,1,0:T(8,128)(2,1)}), bf16[128,24,384]{2,1,0:T(8,128)(2,1)S(1)}, u32[]{:S(2)}, u32[]{:S(2)}) async-start(bf16[128,24,384]{2,1,0:T(8,128)(2,1)} %pack.1), calls=%async_computation | async-start | bytes 4718592 | tf_op jit(solution)/shard_map/all_to_all | solution.py:272

commit v6 on v5

--- a/solution.py
+++ b/solution.py
@@ -223,6 +223,31 @@
     )(blocks, coeff)
 
 
+def split_body(low, high, out_a, out_b, sems):
+    copies = [
+        pltpu.make_async_copy(low.at[0], out_a, sems.at[0]),
+        pltpu.make_async_copy(high.at[1], out_b, sems.at[1]),
+    ]
+    for copy in copies:
+        copy.start()
+    for copy in copies:
+        copy.wait()
+
+
+def split(low, high):
+    slab = jax.ShapeDtypeStruct(low.shape[1:], low.dtype)
+    hbm = pl.BlockSpec(memory_space=pltpu.HBM)
+    return pl.pallas_call(
+        split_body,
+        out_shape=(slab, slab),
+        in_specs=[hbm, hbm],
+        out_specs=(hbm, hbm),
+        scratch_shapes=[pltpu.SemaphoreType.DMA((2,))],
+        compiler_params=pltpu.CompilerParams(vmem_limit_bytes=60 << 20),
+        name="split",
+    )(low, high)
+
+
 def add(first, *others):
     total = first.astype(jnp.float32)
     for other in others:
@@ -240,8 +265,9 @@
     tables = [info] + [send(info, "left", step) for step in (1, -1, 2)]
     near_low_a = send(own_a, "left", 1)
     near_high_b = send(own_b, "left", -1)
-    right_far_a = send(right_low[0], "right", 1)
-    right_far_b = send(right_high[1], "right", -1)
+    onward_a, onward_b = split(right_low, right_high)
+    right_far_a = send(onward_a, "right", 1)
+    right_far_b = send(onward_b, "right", -1)
     far_a = send(near_low_a, "left", 1)
     far_b = send(near_high_b, "left", -1)
     own_a, own_b, right_far_a, right_far_b, far_a, far_b = lax.optimization_barrier(

time: 210 us -> 278 us (1.32)
  Pallas kernels: 46.7 us -> 119 us
  local copies, waits for them, and re-layouts: 11.8 us -> 7.15 us
  starting transfers between devices: 49.1 us -> 52.8 us
    pallas_call x0 -> x1, Pallas kernels: none -> 72.6 us  [split(): pl.pallas_call(split_body, out_shape=(slab, slab), in_specs=[hbm, hbm], o...]
    unnamed x27 -> x21, local copies, waits for them, and re-layouts: 6.29 us -> 4.08 us
  transfers between devices with their start and end apart: 20 -> 20, of which waited for: 9 -> 9; matrix products, arithmetic and copies ran while one was open for 5% -> 3% of each run, Pallas kernels for 18% -> 40%
where the time goes in v6:
time: 278 us
  Pallas kernels  119 us (43%)
  waiting for transfers between devices  95 us (34%)
  starting transfers between devices  52.8 us (19%)
  local copies, waits for them, and re-layouts  7.15 us (3%)
  other arithmetic  3.82 us (1%)
    pallas_call x1, Pallas kernels, split(): pl.pallas_call(split_body, out_shape=(slab, slab), in_specs=[hbm, hbm], o...  72.6 us
    ppermute x19, waiting for transfers between devices, send(): return lax.ppermute(value, AXES, shifted(kind, step))  63.8 us
    pallas_call x5, Pallas kernels, partial_gamma(): pl.pallas_call(functools.partial(pair_body, slots=slots, picks=picks, sta...  37.5 us
    ppermute x19, starting transfers between devices, send(): return lax.ppermute(value, AXES, shifted(kind, step))  33.6 us
    all_to_all x1, waiting for transfers between devices, local(): lax.all_to_all(blocks, AXES, split_axis=0, concat_axis=0, tiled=True)  31.2 us
    all_to_all x1, starting transfers between devices, local(): lax.all_to_all(blocks, AXES, split_axis=0, concat_axis=0, tiled=True)  19.2 us
  transfers between devices with their start and end apart: 20, of which 9 were waited for; matrix products, arithmetic and copies ran while one was open for 3% of the time, Pallas kernels for 40%

profile of v6, /device:TPU:1, one launch (start us, length us, event | category | flops | bytes accessed | tf_op | source)
XLA Modules:
  0.0 277.9 jit_solution(10638294302200704383)
XLA Ops:
  0.0 2.0 collective-permute-start
  3.3 1.8 slice_bitcast_fusion
  5.1 1.9 collective-permute-start.4
  7.0 2.2 collective-permute-start.6
  9.2 26.5 %collective-permute-done.4.refs_0_ = bf16[384,1536]{1,0:T(8,128)(2,1)} collective-permute-done((bf16[384,1536]{1,0:T(8,128)(2,1)S(1)}, bf16[384,1536]{1,0:T(8,128)(2,1)}, u32[]{:S(2)}, u32[]{:S(2)}) %collective-permute-start.4) | collective-permute-done | bytes 1179680 | tf_op jit(solution)/shard_map/ppermute | solution.py:27
  35.8 2.8 collective-permute-start.7
  38.5 4.8 %collective-permute-done.low.refs_2_ = bf16[2,384,1536]{2,1,0:T(8,128)(2,1)S(1)} collective-permute-done((bf16[2,384,1536]{2,1,0:T(8,128)(2,1)}, bf16[2,384,1536]{2,1,0:T(8,128)(2,1)S(1)}, u32[]{:S(2)}, u32[]{:S(2)}) %collective-permute-start) | collective-permute-done | bytes 2359328 | tf_op jit(solution)/shard_map/ppermute | solution.py:27
  43.3 1.4 copy-done.1
  44.7 72.6 %split.1 = (bf16[384,1536]{1,0:T(8,128)(2,1)}, bf16[384,1536]{1,0:T(8,128)(2,1)}) custom-call(bf16[2,384,1536]{2,1,0:T(8,128)(2,1)} %copy-done.1, bf16[2,384,1536]{2,1,0:T(8,128)(2,1)} %collective-permute-done.1.high.refs_3_), custom_call_target="tpu_custom_call" | custom-call | tf_op jit(solution)/shard_map/split/pallas_call | solution.py:240
  117.3 1.7 collective-permute-start.2
  122.4 5.7 %collective-permute-start.12 = (s32[1,48]{1,0:T(1,128)S(1)}, s32[1,48]{1,0:T(1,128)S(1)}, u32[]{:S(2)}, u32[]{:S(2)}) collective-permute-start(s32[1,48]{1,0:T(1,128)S(1)} %pad_add_fusion.table_a.table_b), channel_id=1, source_target_pairs={{0,2},{1,3},{2,0},{3,1},{4,6},{5,7},{6,4},{7,5},{8,10},{9,11},{10,... | collective-permute-start | bytes 584 | tf_op jit(solution)/shard_map/ppermute | solution.py:27
  128.2 6.2 %collective-permute-done.2.refs_4_.refs_2_ = bf16[384,1536]{1,0:T(8,128)(2,1)S(1)} collective-permute-done((bf16[384,1536]{1,0:T(8,128)(2,1)}, bf16[384,1536]{1,0:T(8,128)(2,1)S(1)}, u32[]{:S(2)}, u32[]{:S(2)}) %collective-permute-start.2) | collective-permute-done | bytes 1179680 | tf_op jit(solution)/shard_map/ppermute | solution.py:27
  134.6 3.7 %collective-permute-start.10 = (bf16[384,1536]{1,0:T(8,128)(2,1)}, bf16[384,1536]{1,0:T(8,128)(2,1)S(1)}, u32[]{:S(2)}, u32[]{:S(2)}) collective-permute-start(bf16[384,1536]{1,0:T(8,128)(2,1)} %copy-done.7), channel_id=1, source_target_pairs={{0,1},{1,2},{2,3},{3,0},{4,5},{5,6},{6,7},{7,4},{8,9},{9,10},{10,1... | collective-permute-start | bytes 3538952 | tf_op jit(solution)/shard_map/ppermute | solution.py:27
  138.3 2.1 collective-permute-start.11
  140.5 1.7 copy-done.2
  142.1 11.3 %shard_map.66 = (bf16[384,1536]{1,0:T(8,128)(2,1)}, bf16[384,1536]{1,0:T(8,128)(2,1)}) custom-call(s32[1]{0:T(128)} %bitcast.device, s32[1,48]{1,0:T(1,128)S(1)} %collective-permute-done.12.table_a.table_b, s32[1,48]{1,0:T(1,128)S(1)} %collective-permute-done.12.table_a.table_b, f32[256]{0:T(256)S(1)} %copy-done.5, f32[384]{0:T(512)S(1)} %copy-done.4, ...), custom_call_target="tpu_custom_call" | custom-call | tf_op jit(solution)/shard_map/pallas_call | solution.py:121
  153.6 1.5 collective-permute-start.13
  155.0 15.5 %collective-permute-done.8.table_a = s32[1,48]{1,0:T(1,128)S(1)} collective-permute-done((s32[1,48]{1,0:T(1,128)S(1)}, s32[1,48]{1,0:T(1,128)S(1)}, u32[]{:S(2)}, u32[]{:S(2)}) %collective-permute-start.8) | collective-permute-done | bytes 224 | tf_op jit(solution)/shard_map/ppermute | solution.py:27
  171.0 2.3 collective-permute-done.9.table_b
  173.3 8.6 %shard_map.67 = (f32[384,1536]{1,0:T(8,128)S(1)}, f32[384,1536]{1,0:T(8,128)S(1)}) custom-call(s32[1]{0:T(128)} %bitcast.device, s32[1,48]{1,0:T(1,128)S(1)} %collective-permute-done.8.table_a, s32[1,48]{1,0:T(1,128)S(1)} %collective-permute-done.9.table_b, f32[256]{0:T(256)S(1)} %copy-done.5, f32[384]{0:T(512)S(1)} %copy-done.4, ...), custom_call_target="tpu_custom_call" | custom-call | tf_op jit(solution)/shard_map/pallas_call | solution.py:121
  182.0 6.2 %shard_map.68 = (bf16[384,1536]{1,0:T(8,128)(2,1)}, bf16[384,1536]{1,0:T(8,128)(2,1)}) custom-call(s32[1]{0:T(128)} %bitcast.device, s32[1,48]{1,0:T(1,128)S(1)} %collective-permute-done.8.table_a, s32[1,48]{1,0:T(1,128)S(1)} %collective-permute-done.9.table_b, f32[256]{0:T(256)S(1)} %copy-done.5, f32[384]{0:T(512)S(1)} %copy-done.4, ...), custom_call_target="tpu_custom_call" | custom-call | tf_op jit(solution)/shard_map/pallas_call | solution.py:121
  188.3 1.8 collective-permute-start.16
  190.1 2.1 shard_map.65
  192.2 1.5 add_convert_fusion
  193.8 4.6 %collective-permute-start.18 = (bf16[384,1536]{1,0:T(8,128)(2,1)S(1)}, bf16[384,1536]{1,0:T(8,128)(2,1)S(1)}, u32[]{:S(2)}, u32[]{:S(2)}) collective-permute-start(bf16[384,1536]{1,0:T(8,128)(2,1)S(1)} %add_convert_fusion), channel_id=1, source_target_pairs={{0,3},{1,0},{2,1},{3,2},{4,7},{5,4},{6,5},{7,6},{8,11},{9,8},{10,9... | collective-permute-start | bytes 3538952 | tf_op jit(solution)/shard_map/ppermute | solution.py:27
  198.4 1.5 add_convert_fusion.1
  200.3 9.2 %shard_map.64 = (f32[384,1536]{1,0:T(8,128)S(1)}, f32[384,1536]{1,0:T(8,128)S(1)}) custom-call(s32[1]{0:T(128)} %bitcast.device, s32[1,48]{1,0:T(1,128)S(1)} %pad_add_fusion.table_a.table_b, s32[1,48]{1,0:T(1,128)S(1)} %pad_add_fusion.table_a.table_b, f32[256]{0:T(256)S(1)} %copy-done.5, f32[384]{0:T(512)S(1)} %copy-done.4, ...), custom_call_target="tpu_custom_call" | custom-call | tf_op jit(solution)/shard_map/pallas_call | solution.py:121
  209.5 7.2 %collective-permute-done.18.down_b = bf16[384,1536]{1,0:T(8,128)(2,1)S(1)} collective-permute-done((bf16[384,1536]{1,0:T(8,128)(2,1)S(1)}, bf16[384,1536]{1,0:T(8,128)(2,1)S(1)}, u32[]{:S(2)}, u32[]{:S(2)}) %collective-permute-start.18) | collective-permute-done | bytes 1179680 | tf_op jit(solution)/shard_map/ppermute | solution.py:27
  217.8 4.0 %pack.1 = bf16[128,24,384]{2,1,0:T(8,128)(2,1)} custom-call(f32[384,1536]{1,0:T(8,128)S(1)} %get-tuple-element.27.own_a, f32[384,1536]{1,0:T(8,128)S(1)} %get-tuple-element.28.own_b, bf16[384,1536]{1,0:T(8,128)(2,1)S(1)} %collective-permute-done.14.up_a, bf16[384,1536]{1,0:T(8,128)(2,1)S(1)} %collective-permute-done.15.down_a, ...), custom_call_target="tpu_custom_call" | custom-call | tf_op jit(solution)/shard_map/pack/pallas_call | solution.py:170
  221.8 19.2 %all-to-all-start = ((bf16[128,24,384]{2,1,0:T(8,128)(2,1)}), bf16[128,24,384]{2,1,0:T(8,128)(2,1)S(1)}, u32[]{:S(2)}, u32[]{:S(2)}) async-start(bf16[128,24,384]{2,1,0:T(8,128)(2,1)} %pack.1), calls=%async_computation | async-start | bytes 4718592 | tf_op jit(solution)/shard_map/all_to_all | solution.py:298
  241.9 31.2 %all-to-all-done = bf16[128,24,384]{2,1,0:T(8,128)(2,1)S(1)} async-done(((bf16[128,24,384]{2,1,0:T(8,128)(2,1)}), bf16[128,24,384]{2,1,0:T(8,128)(2,1)S(1)}, u32[]{:S(2)}, u32[]{:S(2)}) %all-to-all-start) | async-done | bytes 2359328 | tf_op jit(solution)/shard_map/all_to_all | solution.py:298
  273.1 4.8 %finish.1 = bf16[48,96,768]{2,1,0:T(8,128)(2,1)} custom-call(bf16[3072,384]{1,0:T(8,128)(2,1)S(1)} %bitcast.13, bf16[768,256]{1,0:T(8,128)(2,1)S(1)} %bitcast.14), custom_call_target="tpu_custom_call" | custom-call | tf_op jit(solution)/shard_map/finish/pallas_call | solution.py:211
  (44 shorter events, 8.0 us)
Async XLA Ops:
  0.0 43.3 %collective-permute-start = (bf16[2,384,1536]{2,1,0:T(8,128)(2,1)}, bf16[2,384,1536]{2,1,0:T(8,128)(2,1)S(1)}, u32[]{:S(2)}, u32[]{:S(2)}) collective-permute-start(bf16[2,384,1536]{2,1,0:T(8,128)(2,1)} %own.9), channel_id=1, source_target_pairs={{0,4},{1,5},{2,6},{3,7},{4,8},{5,9},{6,10},{7,11},{8,12},{9,13},{1... | collective-permute-start | bytes 7077896 | tf_op jit(solution)/shard_map/ppermute | solution.py:27
  2.0 42.7 %collective-permute-start.1 = (bf16[2,384,1536]{2,1,0:T(8,128)(2,1)}, bf16[2,384,1536]{2,1,0:T(8,128)(2,1)}, u32[]{:S(2)}, u32[]{:S(2)}) collective-permute-start(bf16[2,384,1536]{2,1,0:T(8,128)(2,1)} %own.9), channel_id=1, source_target_pairs={{0,12},{1,13},{2,14},{3,15},{4,0},{5,1},{6,2},{7,3},{8,4},{9,5},{1... | collective-permute-start | bytes 7077896 | tf_op jit(solution)/shard_map/ppermute | solution.py:27
  5.1 38.2 %copy-start.7 = (bf16[384,1536]{1,0:T(8,128)(2,1)}, bf16[384,1536]{1,0:T(8,128)(2,1)S(1)}, u32[]{:S(2)}) copy-start(bf16[384,1536]{1,0:T(8,128)(2,1)S(1)} %get-tuple-element.29) | copy-start | bytes 3538948
  5.1 112.2 %copy-start.6 = (bf16[384,1536]{1,0:T(8,128)(2,1)}, bf16[384,1536]{1,0:T(8,128)(2,1)S(1)}, u32[]{:S(2)}) copy-start(bf16[384,1536]{1,0:T(8,128)(2,1)S(1)} %get-tuple-element.30) | copy-start | bytes 3538948
  5.1 30.7 %collective-permute-start.4 = (bf16[384,1536]{1,0:T(8,128)(2,1)S(1)}, bf16[384,1536]{1,0:T(8,128)(2,1)}, u32[]{:S(2)}, u32[]{:S(2)}) collective-permute-start(bf16[384,1536]{1,0:T(8,128)(2,1)S(1)} %get-tuple-element.30), channel_id=1, source_target_pairs={{0,1},{1,2},{2,3},{3,0},{4,5},{5,6},{6,7},{7,4},{8,9},{9,10},{10,1... | collective-permute-start | bytes 3538952 | tf_op jit(solution)/shard_map/ppermute | solution.py:27
  7.0 133.4 %copy-start.4 = (f32[384]{0:T(512)S(1)}, f32[384]{0:T(512)}, u32[]{:S(2)}) copy-start(f32[384]{0:T(512)} %levels.9) | copy-start | bytes 4612
  7.0 133.4 %copy-start.5 = (f32[256]{0:T(256)S(1)}, f32[256]{0:T(256)}, u32[]{:S(2)}) copy-start(f32[256]{0:T(256)} %energies.9) | copy-start | bytes 3076
  7.0 28.8 %collective-permute-start.6 = (bf16[384,1536]{1,0:T(8,128)(2,1)S(1)}, bf16[384,1536]{1,0:T(8,128)(2,1)}, u32[]{:S(2)}, u32[]{:S(2)}) collective-permute-start(bf16[384,1536]{1,0:T(8,128)(2,1)S(1)} %get-tuple-element.29), channel_id=1, source_target_pairs={{0,3},{1,0},{2,1},{3,2},{4,7},{5,4},{6,5},{7,6},{8,11},{9,8},{10,9... | collective-permute-start | bytes 3538952 | tf_op jit(solution)/shard_map/ppermute | solution.py:27
  35.8 92.4 %collective-permute-start.5 = (bf16[384,1536]{1,0:T(8,128)(2,1)}, bf16[384,1536]{1,0:T(8,128)(2,1)}, u32[]{:S(2)}, u32[]{:S(2)}) collective-permute-start(bf16[384,1536]{1,0:T(8,128)(2,1)} %collective-permute-done.4.refs_0_), channel_id=1, source_target_pairs={{0,1},{1,2},{2,3},{3,0},{4,5},{5,6},{6,7},{7,4},{8,9},{9,10},{10,1... | collective-permute-start | bytes 3538952 | tf_op jit(solution)/shard_map/ppermute | solution.py:27
  35.8 92.4 %collective-permute-start.7 = (bf16[384,1536]{1,0:T(8,128)(2,1)}, bf16[384,1536]{1,0:T(8,128)(2,1)}, u32[]{:S(2)}, u32[]{:S(2)}) collective-permute-start(bf16[384,1536]{1,0:T(8,128)(2,1)} %collective-permute-done.6.refs_1_), channel_id=1, source_target_pairs={{0,3},{1,0},{2,1},{3,2},{4,7},{5,4},{6,5},{7,6},{8,11},{9,8},{10,9... | collective-permute-start | bytes 3538952 | tf_op jit(solution)/shard_map/ppermute | solution.py:27
  43.3 1.4 copy-start.1
  44.7 95.7 %copy-start = (bf16[2,384,1536]{2,1,0:T(8,128)(2,1)S(1)}, bf16[2,384,1536]{2,1,0:T(8,128)(2,1)}, u32[]{:S(2)}) copy-start(bf16[2,384,1536]{2,1,0:T(8,128)(2,1)} %own.9) | copy-start | bytes 7077892
  117.3 17.0 %collective-permute-start.2 = (bf16[384,1536]{1,0:T(8,128)(2,1)}, bf16[384,1536]{1,0:T(8,128)(2,1)S(1)}, u32[]{:S(2)}, u32[]{:S(2)}) collective-permute-start(bf16[384,1536]{1,0:T(8,128)(2,1)} %get-tuple-element.23), channel_id=1, source_target_pairs={{0,4},{1,5},{2,6},{3,7},{4,8},{5,9},{6,10},{7,11},{8,12},{9,13},{1... | collective-permute-start | bytes 3538952 | tf_op jit(solution)/shard_map/ppermute | solution.py:27
  119.0 15.7 %collective-permute-start.3 = (bf16[384,1536]{1,0:T(8,128)(2,1)}, bf16[384,1536]{1,0:T(8,128)(2,1)}, u32[]{:S(2)}, u32[]{:S(2)}) collective-permute-start(bf16[384,1536]{1,0:T(8,128)(2,1)} %get-tuple-element.24), channel_id=1, source_target_pairs={{0,12},{1,13},{2,14},{3,15},{4,0},{5,1},{6,2},{7,3},{8,4},{9,5},{1... | collective-permute-start | bytes 3538952 | tf_op jit(solution)/shard_map/ppermute | solution.py:27
  122.4 18.0 %collective-permute-start.12 = (s32[1,48]{1,0:T(1,128)S(1)}, s32[1,48]{1,0:T(1,128)S(1)}, u32[]{:S(2)}, u32[]{:S(2)}) collective-permute-start(s32[1,48]{1,0:T(1,128)S(1)} %pad_add_fusion.table_a.table_b), channel_id=1, source_target_pairs={{0,2},{1,3},{2,0},{3,1},{4,6},{5,7},{6,4},{7,5},{8,10},{9,11},{10,... | collective-permute-start | bytes 584 | tf_op jit(solution)/shard_map/ppermute | solution.py:27
  134.6 53.6 %collective-permute-start.10 = (bf16[384,1536]{1,0:T(8,128)(2,1)}, bf16[384,1536]{1,0:T(8,128)(2,1)S(1)}, u32[]{:S(2)}, u32[]{:S(2)}) collective-permute-start(bf16[384,1536]{1,0:T(8,128)(2,1)} %copy-done.7), channel_id=1, source_target_pairs={{0,1},{1,2},{2,3},{3,0},{4,5},{5,6},{6,7},{7,4},{8,9},{9,10},{10,1... | collective-permute-start | bytes 3538952 | tf_op jit(solution)/shard_map/ppermute | solution.py:27
  138.3 51.8 %collective-permute-start.11 = (bf16[384,1536]{1,0:T(8,128)(2,1)}, bf16[384,1536]{1,0:T(8,128)(2,1)S(1)}, u32[]{:S(2)}, u32[]{:S(2)}) collective-permute-start(bf16[384,1536]{1,0:T(8,128)(2,1)} %copy-done.6), channel_id=1, source_target_pairs={{0,3},{1,0},{2,1},{3,2},{4,7},{5,4},{6,5},{7,6},{8,11},{9,8},{10,9... | collective-permute-start | bytes 3538952 | tf_op jit(solution)/shard_map/ppermute | solution.py:27
  140.5 1.7 copy-start.2
  153.5 38.8 %collective-permute-start.17 = (bf16[384,1536]{1,0:T(8,128)(2,1)}, bf16[384,1536]{1,0:T(8,128)(2,1)}, u32[]{:S(2)}, u32[]{:S(2)}) collective-permute-start(bf16[384,1536]{1,0:T(8,128)(2,1)} %get-tuple-element.40), channel_id=1, source_target_pairs={{0,3},{1,0},{2,1},{3,2},{4,7},{5,4},{6,5},{7,6},{8,11},{9,8},{10,9... | collective-permute-start | bytes 3538952 | tf_op jit(solution)/shard_map/ppermute | solution.py:27
  153.6 44.9 %collective-permute-start.13 = (bf16[384,1536]{1,0:T(8,128)(2,1)}, bf16[384,1536]{1,0:T(8,128)(2,1)}, u32[]{:S(2)}, u32[]{:S(2)}) collective-permute-start(bf16[384,1536]{1,0:T(8,128)(2,1)} %get-tuple-element.34), channel_id=1, source_target_pairs={{0,1},{1,2},{2,3},{3,0},{4,5},{5,6},{6,7},{7,4},{8,9},{9,10},{10,1... | collective-permute-start | bytes 3538952 | tf_op jit(solution)/shard_map/ppermute | solution.py:27
  155.0 15.5 %collective-permute-start.8 = (s32[1,48]{1,0:T(1,128)S(1)}, s32[1,48]{1,0:T(1,128)S(1)}, u32[]{:S(2)}, u32[]{:S(2)}) collective-permute-start(s32[1,48]{1,0:T(1,128)S(1)} %pad_add_fusion.table_a.table_b), channel_id=1, source_target_pairs={{0,1},{1,2},{2,3},{3,0},{4,5},{5,6},{6,7},{7,4},{8,9},{9,10},{10,1... | collective-permute-start | bytes 584 | tf_op jit(solution)/shard_map/ppermute | solution.py:27
  170.5 2.8 %collective-permute-start.9 = (s32[1,48]{1,0:T(1,128)S(1)}, s32[1,48]{1,0:T(1,128)S(1)}, u32[]{:S(2)}, u32[]{:S(2)}) collective-permute-start(s32[1,48]{1,0:T(1,128)S(1)} %pad_add_fusion.table_a.table_b), channel_id=1, source_target_pairs={{0,3},{1,0},{2,1},{3,2},{4,7},{5,4},{6,5},{7,6},{8,11},{9,8},{10,9... | collective-permute-start | bytes 584 | tf_op jit(solution)/shard_map/ppermute | solution.py:27
  182.0 8.2 %copy-start.3 = (bf16[2,384,1536]{2,1,0:T(8,128)(2,1)S(1)}, bf16[2,384,1536]{2,1,0:T(8,128)(2,1)}, u32[]{:S(2)}) copy-start(bf16[2,384,1536]{2,1,0:T(8,128)(2,1)} %copy-done.1) | copy-start | bytes 7077892
  188.2 21.3 %collective-permute-start.15 = (bf16[384,1536]{1,0:T(8,128)(2,1)}, bf16[384,1536]{1,0:T(8,128)(2,1)S(1)}, u32[]{:S(2)}, u32[]{:S(2)}) collective-permute-start(bf16[384,1536]{1,0:T(8,128)(2,1)} %get-tuple-element.37), channel_id=1, source_target_pairs={{0,3},{1,0},{2,1},{3,2},{4,7},{5,4},{6,5},{7,6},{8,11},{9,8},{10,9... | collective-permute-start | bytes 3538952 | tf_op jit(solution)/shard_map/ppermute | solution.py:27
  188.3 21.2 %collective-permute-start.16 = (bf16[384,1536]{1,0:T(8,128)(2,1)}, bf16[384,1536]{1,0:T(8,128)(2,1)S(1)}, u32[]{:S(2)}, u32[]{:S(2)}) collective-permute-start(bf16[384,1536]{1,0:T(8,128)(2,1)} %get-tuple-element.38), channel_id=1, source_target_pairs={{0,1},{1,2},{2,3},{3,0},{4,5},{5,6},{6,7},{7,4},{8,9},{9,10},{10,1... | collective-permute-start | bytes 3538952 | tf_op jit(solution)/shard_map/ppermute | solution.py:27
  193.8 23.0 %collective-permute-start.18 = (bf16[384,1536]{1,0:T(8,128)(2,1)S(1)}, bf16[384,1536]{1,0:T(8,128)(2,1)S(1)}, u32[]{:S(2)}, u32[]{:S(2)}) collective-permute-start(bf16[384,1536]{1,0:T(8,128)(2,1)S(1)} %add_convert_fusion), channel_id=1, source_target_pairs={{0,3},{1,0},{2,1},{3,2},{4,7},{5,4},{6,5},{7,6},{8,11},{9,8},{10,9... | collective-permute-start | bytes 3538952 | tf_op jit(solution)/shard_map/ppermute | solution.py:27
  200.0 17.8 %collective-permute-start.14 = (bf16[384,1536]{1,0:T(8,128)(2,1)S(1)}, bf16[384,1536]{1,0:T(8,128)(2,1)S(1)}, u32[]{:S(2)}, u32[]{:S(2)}) collective-permute-start(bf16[384,1536]{1,0:T(8,128)(2,1)S(1)} %add_convert_fusion.1), channel_id=1, source_target_pairs={{0,1},{1,2},{2,3},{3,0},{4,5},{5,6},{6,7},{7,4},{8,9},{9,10},{10,1... | collective-permute-start | bytes 3538952 | tf_op jit(solution)/shard_map/ppermute | solution.py:27
  221.8 19.2 %copy-start.8 = (bf16[768,256]{1,0:T(8,128)(2,1)S(1)}, bf16[768,256]{1,0:T(8,128)(2,1)}, u32[]{:S(2)}) copy-start(bf16[768,256]{1,0:T(8,128)(2,1)} %param.9) | copy-start | bytes 1179652
  221.8 51.3 %all-to-all-start = ((bf16[128,24,384]{2,1,0:T(8,128)(2,1)}), bf16[128,24,384]{2,1,0:T(8,128)(2,1)S(1)}, u32[]{:S(2)}, u32[]{:S(2)}) async-start(bf16[128,24,384]{2,1,0:T(8,128)(2,1)} %pack.1), calls=%async_computation | async-start | bytes 4718592 | tf_op jit(solution)/shard_map/all_to_all | solution.py:298

commit v7 on v6

--- a/solution.py
+++ b/solution.py
@@ -135,7 +135,7 @@
             pltpu.SemaphoreType.DMA((2,)),
             pltpu.SemaphoreType.DMA((2 * len(picks),)),
         ],
-        compiler_params=pltpu.CompilerParams(vmem_limit_bytes=40 << 20),
+        compiler_params=pltpu.CompilerParams(vmem_limit_bytes=(28 + 3 * len(picks)) << 20),
     )(*scalars, levels, own, *lefts, *used, *begun)
 
 
@@ -241,9 +241,8 @@
         split_body,
         out_shape=(slab, slab),
         in_specs=[hbm, hbm],
-        out_specs=(hbm, hbm),
+        out_specs=[pl.BlockSpec(memory_space=pltpu.VMEM)] * 2,
         scratch_shapes=[pltpu.SemaphoreType.DMA((2,))],
-        compiler_params=pltpu.CompilerParams(vmem_limit_bytes=60 << 20),
         name="split",
     )(low, high)
 
@@ -270,8 +269,8 @@
     right_far_b = send(onward_b, "right", -1)
     far_a = send(near_low_a, "left", 1)
     far_b = send(near_high_b, "left", -1)
-    own_a, own_b, right_far_a, right_far_b, far_a, far_b = lax.optimization_barrier(
-        (own_a, own_b, right_far_a, right_far_b, far_a, far_b)
+    own_a, own_b, right_far_a, right_far_b = lax.optimization_barrier(
+        (own_a, own_b, right_far_a, right_far_b)
     )
     late_low_b = send(own_b, "left", 1)
     late_high_a = send(own_a, "left", -1)
@@ -283,7 +282,9 @@
 
     near = (near_low_a, near_high_b)
     begun = partial(near, (1, 2), (0, 1), jnp.float32, (0, 1, 2))
-    far_a, far_b = partial((far_a, far_b), (3, 3), (0, 1))
+    far = (far_a, far_b)
+    ahead = partial(far, (3, 3), (0, 1), jnp.float32, (0, 1, 2))
+    far_a, far_b = partial(far, (3, 3), (0, 1), picks=(3,), begun=ahead)
     relay_a = send(far_a, "left", 1)
     relay_b = send(far_b, "left", -1)
     low_b, high_a = partial((late_low_b, late_high_a), (1, 2), (1, 0))

time: 278 us -> 206 us (0.74)
  Pallas kernels: 119 us -> 52.2 us
  starting transfers between devices: 52.8 us -> 49.1 us
    pallas_call x1, Pallas kernels: 72.6 us -> 3.3 us  [split(): pl.pallas_call(split_body, out_shape=(slab, slab), in_specs=[hbm, hbm], o...]
    pallas_call x5 -> x6, Pallas kernels: 37.5 us -> 40.1 us  [partial_gamma(): pl.pallas_call(functools.partial(pair_body, slots=slots, picks=picks, sta...]
  transfers between devices with their start and end apart: 20 -> 20, of which waited for: 9 -> 8; matrix products, arithmetic and copies ran while one was open for 3% -> 4% of each run, Pallas kernels for 40% -> 21%
where the time goes in v7:
time: 206 us; the launch traced here: 205 us
  waiting for transfers between devices  92.7 us (45%)
  Pallas kernels  52.2 us (25%)
  starting transfers between devices  49.1 us (24%)
  local copies, waits for them, and re-layouts  7.13 us (3%)
  other arithmetic  3.85 us (2%)
    ppermute x19, waiting for transfers between devices, send(): return lax.ppermute(value, AXES, shifted(kind, step))  61.4 us
    pallas_call x6, Pallas kernels, partial_gamma(): pl.pallas_call(functools.partial(pair_body, slots=slots, picks=picks, sta...  40.1 us
    ppermute x19, starting transfers between devices, send(): return lax.ppermute(value, AXES, shifted(kind, step))  32.4 us
    all_to_all x1, waiting for transfers between devices, local(): lax.all_to_all(blocks, AXES, split_axis=0, concat_axis=0, tiled=True)  31.2 us
    all_to_all x1, starting transfers between devices, local(): lax.all_to_all(blocks, AXES, split_axis=0, concat_axis=0, tiled=True)  16.8 us
    pallas_call x1, Pallas kernels, finish(): pl.pallas_call(finish_body, grid=(48 // rows,), out_shape=jax.ShapeDtypeS...  4.77 us
  transfers between devices with their start and end apart: 20, of which 8 were waited for; matrix products, arithmetic and copies ran while one was open for 4% of the time, Pallas kernels for 21%

profile of v7, /device:TPU:1, one launch (start us, length us, event | category | flops | bytes accessed | tf_op | source)
XLA Modules:
  0.0 205.2 jit_solution(9573152946152168067)
XLA Ops:
  0.0 2.0 collective-permute-start
  3.3 1.8 slice_bitcast_fusion
  5.1 1.9 collective-permute-start.9
  7.0 2.2 %collective-permute-start.11 = (bf16[384,1536]{1,0:T(8,128)(2,1)S(1)}, bf16[384,1536]{1,0:T(8,128)(2,1)}, u32[]{:S(2)}, u32[]{:S(2)}) collective-permute-start(bf16[384,1536]{1,0:T(8,128)(2,1)S(1)} %get-tuple-element.29), channel_id=1, source_target_pairs={{0,3},{1,0},{2,1},{3,2},{4,7},{5,4},{6,5},{7,6},{8,11},{9,8},{10,9... | collective-permute-start | bytes 3538952 | tf_op jit(solution)/shard_map/ppermute | solution.py:27
  9.2 26.5 %collective-permute-done.9.refs_0_ = bf16[384,1536]{1,0:T(8,128)(2,1)} collective-permute-done((bf16[384,1536]{1,0:T(8,128)(2,1)S(1)}, bf16[384,1536]{1,0:T(8,128)(2,1)}, u32[]{:S(2)}, u32[]{:S(2)}) %collective-permute-start.9) | collective-permute-done | bytes 1179680 | tf_op jit(solution)/shard_map/ppermute | solution.py:27
  35.8 2.8 %collective-permute-start.12 = (bf16[384,1536]{1,0:T(8,128)(2,1)}, bf16[384,1536]{1,0:T(8,128)(2,1)}, u32[]{:S(2)}, u32[]{:S(2)}) collective-permute-start(bf16[384,1536]{1,0:T(8,128)(2,1)} %collective-permute-done.11.refs_1_), channel_id=1, source_target_pairs={{0,3},{1,0},{2,1},{3,2},{4,7},{5,4},{6,5},{7,6},{8,11},{9,8},{10,9... | collective-permute-start | bytes 3538952 | tf_op jit(solution)/shard_map/ppermute | solution.py:27
  38.5 4.8 %collective-permute-done.low.refs_2_ = bf16[2,384,1536]{2,1,0:T(8,128)(2,1)S(1)} collective-permute-done((bf16[2,384,1536]{2,1,0:T(8,128)(2,1)}, bf16[2,384,1536]{2,1,0:T(8,128)(2,1)S(1)}, u32[]{:S(2)}, u32[]{:S(2)}) %collective-permute-start) | collective-permute-done | bytes 2359328 | tf_op jit(solution)/shard_map/ppermute | solution.py:27
  43.3 1.4 copy-done.1
  44.7 3.3 %split.1 = (bf16[384,1536]{1,0:T(8,128)(2,1)}, bf16[384,1536]{1,0:T(8,128)(2,1)}) custom-call(bf16[2,384,1536]{2,1,0:T(8,128)(2,1)} %copy-done.1, bf16[2,384,1536]{2,1,0:T(8,128)(2,1)} %collective-permute-done.1.high.refs_3_), custom_call_target="tpu_custom_call" | custom-call | tf_op jit(solution)/shard_map/split/pallas_call | solution.py:240
  48.0 1.7 collective-permute-start.2
  53.1 5.7 %collective-permute-start.8 = (s32[1,48]{1,0:T(1,128)S(1)}, s32[1,48]{1,0:T(1,128)S(1)}, u32[]{:S(2)}, u32[]{:S(2)}) collective-permute-start(s32[1,48]{1,0:T(1,128)S(1)} %pad_add_fusion.table_a.table_b), channel_id=1, source_target_pairs={{0,2},{1,3},{2,0},{3,1},{4,6},{5,7},{6,4},{7,5},{8,10},{9,11},{10,... | collective-permute-start | bytes 584 | tf_op jit(solution)/shard_map/ppermute | solution.py:27
  59.9 1.7 copy-done.2
  61.5 8.5 %shard_map.66 = (f32[384,1536]{1,0:T(8,128)S(1)}, f32[384,1536]{1,0:T(8,128)S(1)}) custom-call(s32[1]{0:T(128)} %bitcast.device, s32[1,48]{1,0:T(1,128)S(1)} %collective-permute-done.8.table_a.table_b, s32[1,48]{1,0:T(1,128)S(1)} %collective-permute-done.8.table_a.table_b, f32[256]{0:T(256)S(1)} %copy-done.5, f32[384]{0:T(512)S(1)} %copy-done.4, ...), custom_call_target="tpu_custom_call" | custom-call | tf_op jit(solution)/shard_map/pallas_call | solution.py:121
  70.2 3.2 %collective-permute-start.7 = (bf16[384,1536]{1,0:T(8,128)(2,1)S(1)}, bf16[384,1536]{1,0:T(8,128)(2,1)S(1)}, u32[]{:S(2)}, u32[]{:S(2)}) collective-permute-start(bf16[384,1536]{1,0:T(8,128)(2,1)S(1)} %copy-done.7), channel_id=1, source_target_pairs={{0,3},{1,0},{2,1},{3,2},{4,7},{5,4},{6,5},{7,6},{8,11},{9,8},{10,9... | collective-permute-start | bytes 3538952 | tf_op jit(solution)/shard_map/ppermute | solution.py:27
  73.4 5.4 %shard_map.67 = (bf16[384,1536]{1,0:T(8,128)(2,1)S(1)}, bf16[384,1536]{1,0:T(8,128)(2,1)S(1)}) custom-call(s32[1]{0:T(128)} %bitcast.device, s32[1,48]{1,0:T(1,128)S(1)} %collective-permute-done.8.table_a.table_b, s32[1,48]{1,0:T(1,128)S(1)} %collective-permute-done.8.table_a.table_b, f32[256]{0:T(256)S(1)} %copy-done.5, f32[384]{0:T(512)S(1)} %copy-done.4, ...), custom_call_target="tpu_custom_call" | custom-call | tf_op jit(solution)/shard_map/pallas_call | solution.py:121
  78.9 1.5 collective-permute-start.13
  80.4 19.5 %collective-permute-done.4.table_a = s32[1,48]{1,0:T(1,128)S(1)} collective-permute-done((s32[1,48]{1,0:T(1,128)S(1)}, s32[1,48]{1,0:T(1,128)S(1)}, u32[]{:S(2)}, u32[]{:S(2)}) %collective-permute-start.4) | collective-permute-done | bytes 224 | tf_op jit(solution)/shard_map/ppermute | solution.py:27
  99.9 1.5 collective-permute-start.5
  101.4 1.4 collective-permute-done.5.table_b
  102.7 8.8 %shard_map.68 = (f32[384,1536]{1,0:T(8,128)S(1)}, f32[384,1536]{1,0:T(8,128)S(1)}) custom-call(s32[1]{0:T(128)} %bitcast.device, s32[1,48]{1,0:T(1,128)S(1)} %collective-permute-done.4.table_a, s32[1,48]{1,0:T(1,128)S(1)} %collective-permute-done.5.table_b, f32[256]{0:T(256)S(1)} %copy-done.5, f32[384]{0:T(512)S(1)} %copy-done.4, ...), custom_call_target="tpu_custom_call" | custom-call | tf_op jit(solution)/shard_map/pallas_call | solution.py:121
  111.5 5.9 %shard_map.69 = (bf16[384,1536]{1,0:T(8,128)(2,1)}, bf16[384,1536]{1,0:T(8,128)(2,1)}) custom-call(s32[1]{0:T(128)} %bitcast.device, s32[1,48]{1,0:T(1,128)S(1)} %collective-permute-done.4.table_a, s32[1,48]{1,0:T(1,128)S(1)} %collective-permute-done.5.table_b, f32[256]{0:T(256)S(1)} %copy-done.5, f32[384]{0:T(512)S(1)} %copy-done.4, ...), custom_call_target="tpu_custom_call" | custom-call | tf_op jit(solution)/shard_map/pallas_call | solution.py:121
  119.0 2.1 %shard_map.65 = (bf16[384,1536]{1,0:T(8,128)(2,1)S(1)}, bf16[384,1536]{1,0:T(8,128)(2,1)S(1)}) custom-call(s32[1]{0:T(128)} %bitcast.device, s32[1,48]{1,0:T(1,128)S(1)} %collective-permute-done.4.table_a, s32[1,48]{1,0:T(1,128)S(1)} %collective-permute-done.5.table_b, f32[256]{0:T(256)S(1)} %copy-done.5, f32[384]{0:T(512)S(1)} %copy-done.4, ...), custom_call_target="tpu_custom_call" | custom-call | tf_op jit(solution)/shard_map/pallas_call | solution.py:121
  121.1 1.6 add_convert_fusion
  122.7 5.5 %collective-permute-start.18 = (bf16[384,1536]{1,0:T(8,128)(2,1)S(1)}, bf16[384,1536]{1,0:T(8,128)(2,1)S(1)}, u32[]{:S(2)}, u32[]{:S(2)}) collective-permute-start(bf16[384,1536]{1,0:T(8,128)(2,1)S(1)} %add_convert_fusion), channel_id=1, source_target_pairs={{0,3},{1,0},{2,1},{3,2},{4,7},{5,4},{6,5},{7,6},{8,11},{9,8},{10,9... | collective-permute-start | bytes 3538952 | tf_op jit(solution)/shard_map/ppermute | solution.py:27
  128.2 1.6 add_convert_fusion.1
  129.8 9.4 %shard_map.64 = (f32[384,1536]{1,0:T(8,128)S(1)}, f32[384,1536]{1,0:T(8,128)S(1)}) custom-call(s32[1]{0:T(128)} %bitcast.device, s32[1,48]{1,0:T(1,128)S(1)} %pad_add_fusion.table_a.table_b, s32[1,48]{1,0:T(1,128)S(1)} %pad_add_fusion.table_a.table_b, f32[256]{0:T(256)S(1)} %copy-done.5, f32[384]{0:T(512)S(1)} %copy-done.4, ...), custom_call_target="tpu_custom_call" | custom-call | tf_op jit(solution)/shard_map/pallas_call | solution.py:121
  139.3 6.4 %collective-permute-done.18.down_b = bf16[384,1536]{1,0:T(8,128)(2,1)S(1)} collective-permute-done((bf16[384,1536]{1,0:T(8,128)(2,1)S(1)}, bf16[384,1536]{1,0:T(8,128)(2,1)S(1)}, u32[]{:S(2)}, u32[]{:S(2)}) %collective-permute-start.18) | collective-permute-done | bytes 1179680 | tf_op jit(solution)/shard_map/ppermute | solution.py:27
  145.7 1.8 collective-permute-done.14.up_a
  147.6 4.0 %pack.1 = bf16[128,24,384]{2,1,0:T(8,128)(2,1)} custom-call(f32[384,1536]{1,0:T(8,128)S(1)} %get-tuple-element.27.own_a, f32[384,1536]{1,0:T(8,128)S(1)} %get-tuple-element.28.own_b, bf16[384,1536]{1,0:T(8,128)(2,1)S(1)} %collective-permute-done.14.up_a, bf16[384,1536]{1,0:T(8,128)(2,1)S(1)} %collective-permute-done.15.down_a, ...), custom_call_target="tpu_custom_call" | custom-call | tf_op jit(solution)/shard_map/pack/pallas_call | solution.py:170
  151.5 16.8 %all-to-all-start = ((bf16[128,24,384]{2,1,0:T(8,128)(2,1)}), bf16[128,24,384]{2,1,0:T(8,128)(2,1)S(1)}, u32[]{:S(2)}, u32[]{:S(2)}) async-start(bf16[128,24,384]{2,1,0:T(8,128)(2,1)} %pack.1), calls=%async_computation | async-start | bytes 4718592 | tf_op jit(solution)/shard_map/all_to_all | solution.py:299
  169.2 31.2 %all-to-all-done = bf16[128,24,384]{2,1,0:T(8,128)(2,1)S(1)} async-done(((bf16[128,24,384]{2,1,0:T(8,128)(2,1)}), bf16[128,24,384]{2,1,0:T(8,128)(2,1)S(1)}, u32[]{:S(2)}, u32[]{:S(2)}) %all-to-all-start) | async-done | bytes 2359328 | tf_op jit(solution)/shard_map/all_to_all | solution.py:299
  200.4 4.8 %finish.1 = bf16[48,96,768]{2,1,0:T(8,128)(2,1)} custom-call(bf16[3072,384]{1,0:T(8,128)(2,1)S(1)} %bitcast.13, bf16[768,256]{1,0:T(8,128)(2,1)S(1)} %bitcast.14), custom_call_target="tpu_custom_call" | custom-call | tf_op jit(solution)/shard_map/finish/pallas_call | solution.py:211
  (49 shorter events, 8.4 us)
Async XLA Ops:
  0.0 43.3 %collective-permute-start = (bf16[2,384,1536]{2,1,0:T(8,128)(2,1)}, bf16[2,384,1536]{2,1,0:T(8,128)(2,1)S(1)}, u32[]{:S(2)}, u32[]{:S(2)}) collective-permute-start(bf16[2,384,1536]{2,1,0:T(8,128)(2,1)} %own.11), channel_id=1, source_target_pairs={{0,4},{1,5},{2,6},{3,7},{4,8},{5,9},{6,10},{7,11},{8,12},{9,13},{1... | collective-permute-start | bytes 7077896 | tf_op jit(solution)/shard_map/ppermute | solution.py:27
  2.0 42.7 %collective-permute-start.1 = (bf16[2,384,1536]{2,1,0:T(8,128)(2,1)}, bf16[2,384,1536]{2,1,0:T(8,128)(2,1)}, u32[]{:S(2)}, u32[]{:S(2)}) collective-permute-start(bf16[2,384,1536]{2,1,0:T(8,128)(2,1)} %own.11), channel_id=1, source_target_pairs={{0,12},{1,13},{2,14},{3,15},{4,0},{5,1},{6,2},{7,3},{8,4},{9,5},{1... | collective-permute-start | bytes 7077896 | tf_op jit(solution)/shard_map/ppermute | solution.py:27
  5.1 38.2 %copy-start.6 = (bf16[384,1536]{1,0:T(8,128)(2,1)}, bf16[384,1536]{1,0:T(8,128)(2,1)S(1)}, u32[]{:S(2)}) copy-start(bf16[384,1536]{1,0:T(8,128)(2,1)S(1)} %get-tuple-element.30) | copy-start | bytes 3538948
  5.1 38.2 %copy-start.8 = (bf16[384,1536]{1,0:T(8,128)(2,1)}, bf16[384,1536]{1,0:T(8,128)(2,1)S(1)}, u32[]{:S(2)}) copy-start(bf16[384,1536]{1,0:T(8,128)(2,1)S(1)} %get-tuple-element.29) | copy-start | bytes 3538948
  5.1 30.7 %collective-permute-start.9 = (bf16[384,1536]{1,0:T(8,128)(2,1)S(1)}, bf16[384,1536]{1,0:T(8,128)(2,1)}, u32[]{:S(2)}, u32[]{:S(2)}) collective-permute-start(bf16[384,1536]{1,0:T(8,128)(2,1)S(1)} %get-tuple-element.30), channel_id=1, source_target_pairs={{0,1},{1,2},{2,3},{3,0},{4,5},{5,6},{6,7},{7,4},{8,9},{9,10},{10,1... | collective-permute-start | bytes 3538952 | tf_op jit(solution)/shard_map/ppermute | solution.py:27
  7.0 52.8 %copy-start.4 = (f32[384]{0:T(512)S(1)}, f32[384]{0:T(512)}, u32[]{:S(2)}) copy-start(f32[384]{0:T(512)} %levels.11) | copy-start | bytes 4612
  7.0 52.8 %copy-start.5 = (f32[256]{0:T(256)S(1)}, f32[256]{0:T(256)}, u32[]{:S(2)}) copy-start(f32[256]{0:T(256)} %energies.11) | copy-start | bytes 3076
  7.0 28.8 %collective-permute-start.11 = (bf16[384,1536]{1,0:T(8,128)(2,1)S(1)}, bf16[384,1536]{1,0:T(8,128)(2,1)}, u32[]{:S(2)}, u32[]{:S(2)}) collective-permute-start(bf16[384,1536]{1,0:T(8,128)(2,1)S(1)} %get-tuple-element.29), channel_id=1, source_target_pairs={{0,3},{1,0},{2,1},{3,2},{4,7},{5,4},{6,5},{7,6},{8,11},{9,8},{10,9... | collective-permute-start | bytes 3538952 | tf_op jit(solution)/shard_map/ppermute | solution.py:27
  35.8 24.1 %collective-permute-start.10 = (bf16[384,1536]{1,0:T(8,128)(2,1)}, bf16[384,1536]{1,0:T(8,128)(2,1)}, u32[]{:S(2)}, u32[]{:S(2)}) collective-permute-start(bf16[384,1536]{1,0:T(8,128)(2,1)} %collective-permute-done.9.refs_0_), channel_id=1, source_target_pairs={{0,1},{1,2},{2,3},{3,0},{4,5},{5,6},{6,7},{7,4},{8,9},{9,10},{10,1... | collective-permute-start | bytes 3538952 | tf_op jit(solution)/shard_map/ppermute | solution.py:27
  35.8 24.1 %collective-permute-start.12 = (bf16[384,1536]{1,0:T(8,128)(2,1)}, bf16[384,1536]{1,0:T(8,128)(2,1)}, u32[]{:S(2)}, u32[]{:S(2)}) collective-permute-start(bf16[384,1536]{1,0:T(8,128)(2,1)} %collective-permute-done.11.refs_1_), channel_id=1, source_target_pairs={{0,3},{1,0},{2,1},{3,2},{4,7},{5,4},{6,5},{7,6},{8,11},{9,8},{10,9... | collective-permute-start | bytes 3538952 | tf_op jit(solution)/shard_map/ppermute | solution.py:27
  43.3 1.4 copy-start.1
  44.7 15.1 %copy-start = (bf16[2,384,1536]{2,1,0:T(8,128)(2,1)S(1)}, bf16[2,384,1536]{2,1,0:T(8,128)(2,1)}, u32[]{:S(2)}) copy-start(bf16[2,384,1536]{2,1,0:T(8,128)(2,1)} %own.11) | copy-start | bytes 7077892
  48.0 22.0 %collective-permute-start.2 = (bf16[384,1536]{1,0:T(8,128)(2,1)}, bf16[384,1536]{1,0:T(8,128)(2,1)S(1)}, u32[]{:S(2)}, u32[]{:S(2)}) collective-permute-start(bf16[384,1536]{1,0:T(8,128)(2,1)} %get-tuple-element.23), channel_id=1, source_target_pairs={{0,4},{1,5},{2,6},{3,7},{4,8},{5,9},{6,10},{7,11},{8,12},{9,13},{1... | collective-permute-start | bytes 3538952 | tf_op jit(solution)/shard_map/ppermute | solution.py:27
  49.7 20.4 %collective-permute-start.3 = (bf16[384,1536]{1,0:T(8,128)(2,1)}, bf16[384,1536]{1,0:T(8,128)(2,1)}, u32[]{:S(2)}, u32[]{:S(2)}) collective-permute-start(bf16[384,1536]{1,0:T(8,128)(2,1)} %get-tuple-element.24), channel_id=1, source_target_pairs={{0,12},{1,13},{2,14},{3,15},{4,0},{5,1},{6,2},{7,3},{8,4},{9,5},{1... | collective-permute-start | bytes 3538952 | tf_op jit(solution)/shard_map/ppermute | solution.py:27
  53.1 6.7 %collective-permute-start.8 = (s32[1,48]{1,0:T(1,128)S(1)}, s32[1,48]{1,0:T(1,128)S(1)}, u32[]{:S(2)}, u32[]{:S(2)}) collective-permute-start(s32[1,48]{1,0:T(1,128)S(1)} %pad_add_fusion.table_a.table_b), channel_id=1, source_target_pairs={{0,2},{1,3},{2,0},{3,1},{4,6},{5,7},{6,4},{7,5},{8,10},{9,11},{10,... | collective-permute-start | bytes 584 | tf_op jit(solution)/shard_map/ppermute | solution.py:27
  59.9 1.7 copy-start.2
  61.5 8.5 %copy-start.9 = (bf16[384,1536]{1,0:T(8,128)(2,1)S(1)}, bf16[384,1536]{1,0:T(8,128)(2,1)}, u32[]{:S(2)}) copy-start(bf16[384,1536]{1,0:T(8,128)(2,1)} %copy-done.8) | copy-start | bytes 3538948
  61.5 8.6 %copy-start.7 = (bf16[384,1536]{1,0:T(8,128)(2,1)S(1)}, bf16[384,1536]{1,0:T(8,128)(2,1)}, u32[]{:S(2)}) copy-start(bf16[384,1536]{1,0:T(8,128)(2,1)} %copy-done.6) | copy-start | bytes 3538948
  70.1 48.1 %collective-permute-start.6 = (bf16[384,1536]{1,0:T(8,128)(2,1)S(1)}, bf16[384,1536]{1,0:T(8,128)(2,1)S(1)}, u32[]{:S(2)}, u32[]{:S(2)}) collective-permute-start(bf16[384,1536]{1,0:T(8,128)(2,1)S(1)} %copy-done.9), channel_id=1, source_target_pairs={{0,1},{1,2},{2,3},{3,0},{4,5},{5,6},{6,7},{7,4},{8,9},{9,10},{10,1... | collective-permute-start | bytes 3538952 | tf_op jit(solution)/shard_map/ppermute | solution.py:27
  70.2 48.8 %collective-permute-start.7 = (bf16[384,1536]{1,0:T(8,128)(2,1)S(1)}, bf16[384,1536]{1,0:T(8,128)(2,1)S(1)}, u32[]{:S(2)}, u32[]{:S(2)}) collective-permute-start(bf16[384,1536]{1,0:T(8,128)(2,1)S(1)} %copy-done.7), channel_id=1, source_target_pairs={{0,3},{1,0},{2,1},{3,2},{4,7},{5,4},{6,5},{7,6},{8,11},{9,8},{10,9... | collective-permute-start | bytes 3538952 | tf_op jit(solution)/shard_map/ppermute | solution.py:27
  73.4 29.4 %copy-start.3 = (bf16[2,384,1536]{2,1,0:T(8,128)(2,1)S(1)}, bf16[2,384,1536]{2,1,0:T(8,128)(2,1)}, u32[]{:S(2)}) copy-start(bf16[2,384,1536]{2,1,0:T(8,128)(2,1)} %copy-done.1) | copy-start | bytes 7077892
  78.8 42.3 %collective-permute-start.17 = (bf16[384,1536]{1,0:T(8,128)(2,1)S(1)}, bf16[384,1536]{1,0:T(8,128)(2,1)}, u32[]{:S(2)}, u32[]{:S(2)}) collective-permute-start(bf16[384,1536]{1,0:T(8,128)(2,1)S(1)} %get-tuple-element.40), channel_id=1, source_target_pairs={{0,3},{1,0},{2,1},{3,2},{4,7},{5,4},{6,5},{7,6},{8,11},{9,8},{10,9... | collective-permute-start | bytes 3538952 | tf_op jit(solution)/shard_map/ppermute | solution.py:27
  78.9 49.3 %collective-permute-start.13 = (bf16[384,1536]{1,0:T(8,128)(2,1)S(1)}, bf16[384,1536]{1,0:T(8,128)(2,1)}, u32[]{:S(2)}, u32[]{:S(2)}) collective-permute-start(bf16[384,1536]{1,0:T(8,128)(2,1)S(1)} %get-tuple-element.34), channel_id=1, source_target_pairs={{0,1},{1,2},{2,3},{3,0},{4,5},{5,6},{6,7},{7,4},{8,9},{9,10},{10,1... | collective-permute-start | bytes 3538952 | tf_op jit(solution)/shard_map/ppermute | solution.py:27
  80.3 19.6 %collective-permute-start.4 = (s32[1,48]{1,0:T(1,128)S(1)}, s32[1,48]{1,0:T(1,128)S(1)}, u32[]{:S(2)}, u32[]{:S(2)}) collective-permute-start(s32[1,48]{1,0:T(1,128)S(1)} %pad_add_fusion.table_a.table_b), channel_id=1, source_target_pairs={{0,1},{1,2},{2,3},{3,0},{4,5},{5,6},{6,7},{7,4},{8,9},{9,10},{10,1... | collective-permute-start | bytes 584 | tf_op jit(solution)/shard_map/ppermute | solution.py:27
  99.9 2.8 %collective-permute-start.5 = (s32[1,48]{1,0:T(1,128)S(1)}, s32[1,48]{1,0:T(1,128)S(1)}, u32[]{:S(2)}, u32[]{:S(2)}) collective-permute-start(s32[1,48]{1,0:T(1,128)S(1)} %pad_add_fusion.table_a.table_b), channel_id=1, source_target_pairs={{0,3},{1,0},{2,1},{3,2},{4,7},{5,4},{6,5},{7,6},{8,11},{9,8},{10,9... | collective-permute-start | bytes 584 | tf_op jit(solution)/shard_map/ppermute | solution.py:27
  117.4 21.8 %collective-permute-start.15 = (bf16[384,1536]{1,0:T(8,128)(2,1)}, bf16[384,1536]{1,0:T(8,128)(2,1)S(1)}, u32[]{:S(2)}, u32[]{:S(2)}) collective-permute-start(bf16[384,1536]{1,0:T(8,128)(2,1)} %get-tuple-element.37), channel_id=1, source_target_pairs={{0,3},{1,0},{2,1},{3,2},{4,7},{5,4},{6,5},{7,6},{8,11},{9,8},{10,9... | collective-permute-start | bytes 3538952 | tf_op jit(solution)/shard_map/ppermute | solution.py:27
  118.1 21.1 %collective-permute-start.16 = (bf16[384,1536]{1,0:T(8,128)(2,1)}, bf16[384,1536]{1,0:T(8,128)(2,1)S(1)}, u32[]{:S(2)}, u32[]{:S(2)}) collective-permute-start(bf16[384,1536]{1,0:T(8,128)(2,1)} %get-tuple-element.38), channel_id=1, source_target_pairs={{0,1},{1,2},{2,3},{3,0},{4,5},{5,6},{6,7},{7,4},{8,9},{9,10},{10,1... | collective-permute-start | bytes 3538952 | tf_op jit(solution)/shard_map/ppermute | solution.py:27
  122.7 23.0 %collective-permute-start.18 = (bf16[384,1536]{1,0:T(8,128)(2,1)S(1)}, bf16[384,1536]{1,0:T(8,128)(2,1)S(1)}, u32[]{:S(2)}, u32[]{:S(2)}) collective-permute-start(bf16[384,1536]{1,0:T(8,128)(2,1)S(1)} %add_convert_fusion), channel_id=1, source_target_pairs={{0,3},{1,0},{2,1},{3,2},{4,7},{5,4},{6,5},{7,6},{8,11},{9,8},{10,9... | collective-permute-start | bytes 3538952 | tf_op jit(solution)/shard_map/ppermute | solution.py:27
  129.8 17.8 %collective-permute-start.14 = (bf16[384,1536]{1,0:T(8,128)(2,1)S(1)}, bf16[384,1536]{1,0:T(8,128)(2,1)S(1)}, u32[]{:S(2)}, u32[]{:S(2)}) collective-permute-start(bf16[384,1536]{1,0:T(8,128)(2,1)S(1)} %add_convert_fusion.1), channel_id=1, source_target_pairs={{0,1},{1,2},{2,3},{3,0},{4,5},{5,6},{6,7},{7,4},{8,9},{9,10},{10,1... | collective-permute-start | bytes 3538952 | tf_op jit(solution)/shard_map/ppermute | solution.py:27
  151.5 16.8 %copy-start.10 = (bf16[768,256]{1,0:T(8,128)(2,1)S(1)}, bf16[768,256]{1,0:T(8,128)(2,1)}, u32[]{:S(2)}) copy-start(bf16[768,256]{1,0:T(8,128)(2,1)} %param.9) | copy-start | bytes 1179652
  151.5 48.9 %all-to-all-start = ((bf16[128,24,384]{2,1,0:T(8,128)(2,1)}), bf16[128,24,384]{2,1,0:T(8,128)(2,1)S(1)}, u32[]{:S(2)}, u32[]{:S(2)}) async-start(bf16[128,24,384]{2,1,0:T(8,128)(2,1)} %pack.1), calls=%async_computation | async-start | bytes 4718592 | tf_op jit(solution)/shard_map/all_to_all | solution.py:299

commit v8 on v6

--- a/solution.py
+++ b/solution.py
@@ -135,7 +135,7 @@
             pltpu.SemaphoreType.DMA((2,)),
             pltpu.SemaphoreType.DMA((2 * len(picks),)),
         ],
-        compiler_params=pltpu.CompilerParams(vmem_limit_bytes=40 << 20),
+        compiler_params=pltpu.CompilerParams(vmem_limit_bytes=(28 + 3 * len(picks)) << 20),
     )(*scalars, levels, own, *lefts, *used, *begun)
 
 
@@ -241,9 +241,8 @@
         split_body,
         out_shape=(slab, slab),
         in_specs=[hbm, hbm],
-        out_specs=(hbm, hbm),
+        out_specs=[pl.BlockSpec(memory_space=pltpu.VMEM)] * 2,
         scratch_shapes=[pltpu.SemaphoreType.DMA((2,))],
-        compiler_params=pltpu.CompilerParams(vmem_limit_bytes=60 << 20),
         name="split",
     )(low, high)
 

time: 278 us -> 207 us (0.74)
  Pallas kernels: 119 us -> 48.3 us
  starting transfers between devices: 52.8 us -> 49.3 us
    pallas_call x1, Pallas kernels: 72.6 us -> 3.3 us  [split(): pl.pallas_call(split_body, out_shape=(slab, slab), in_specs=[hbm, hbm], o...]
  transfers between devices with their start and end apart: 20 -> 20, of which waited for: 9 -> 9; matrix products, arithmetic and copies ran while one was open for 3% -> 4% of each run, Pallas kernels for 40% -> 19%
where the time goes in v8:
time: 207 us; the launch traced here: 206 us
  waiting for transfers between devices  97.7 us (47%)
  starting transfers between devices  49.3 us (24%)
  Pallas kernels  48.3 us (23%)
  local copies, waits for them, and re-layouts  7.14 us (3%)
  other arithmetic  3.82 us (2%)
    ppermute x19, waiting for transfers between devices, send(): return lax.ppermute(value, AXES, shifted(kind, step))  66.5 us
    pallas_call x5, Pallas kernels, partial_gamma(): pl.pallas_call(functools.partial(pair_body, slots=slots, picks=picks, sta...  36.3 us
    ppermute x19, starting transfers between devices, send(): return lax.ppermute(value, AXES, shifted(kind, step))  31.6 us
    all_to_all x1, waiting for transfers between devices, local(): lax.all_to_all(blocks, AXES, split_axis=0, concat_axis=0, tiled=True)  31.2 us
    all_to_all x1, starting transfers between devices, local(): lax.all_to_all(blocks, AXES, split_axis=0, concat_axis=0, tiled=True)  17.6 us
    pallas_call x1, Pallas kernels, finish(): pl.pallas_call(finish_body, grid=(48 // rows,), out_shape=jax.ShapeDtypeS...  4.76 us
  transfers between devices with their start and end apart: 20, of which 9 were waited for; matrix products, arithmetic and copies ran while one was open for 4% of the time, Pallas kernels for 19%

profile of v8, /device:TPU:1, one launch (start us, length us, event | category | flops | bytes accessed | tf_op | source)
XLA Modules:
  0.0 206.5 jit_solution(5160873157982485319)
XLA Ops:
  0.0 2.0 collective-permute-start
  3.3 1.8 slice_bitcast_fusion
  5.1 1.9 collective-permute-start.4
  7.0 2.2 %collective-permute-start.6 = (bf16[384,1536]{1,0:T(8,128)(2,1)S(1)}, bf16[384,1536]{1,0:T(8,128)(2,1)}, u32[]{:S(2)}, u32[]{:S(2)}) collective-permute-start(bf16[384,1536]{1,0:T(8,128)(2,1)S(1)} %get-tuple-element.29), channel_id=1, source_target_pairs={{0,3},{1,0},{2,1},{3,2},{4,7},{5,4},{6,5},{7,6},{8,11},{9,8},{10,9... | collective-permute-start | bytes 3538952 | tf_op jit(solution)/shard_map/ppermute | solution.py:27
  9.2 26.5 %collective-permute-done.4.refs_0_ = bf16[384,1536]{1,0:T(8,128)(2,1)} collective-permute-done((bf16[384,1536]{1,0:T(8,128)(2,1)S(1)}, bf16[384,1536]{1,0:T(8,128)(2,1)}, u32[]{:S(2)}, u32[]{:S(2)}) %collective-permute-start.4) | collective-permute-done | bytes 1179680 | tf_op jit(solution)/shard_map/ppermute | solution.py:27
  35.8 2.8 %collective-permute-start.7 = (bf16[384,1536]{1,0:T(8,128)(2,1)}, bf16[384,1536]{1,0:T(8,128)(2,1)}, u32[]{:S(2)}, u32[]{:S(2)}) collective-permute-start(bf16[384,1536]{1,0:T(8,128)(2,1)} %collective-permute-done.6.refs_1_), channel_id=1, source_target_pairs={{0,3},{1,0},{2,1},{3,2},{4,7},{5,4},{6,5},{7,6},{8,11},{9,8},{10,9... | collective-permute-start | bytes 3538952 | tf_op jit(solution)/shard_map/ppermute | solution.py:27
  38.5 4.8 %collective-permute-done.low.refs_2_ = bf16[2,384,1536]{2,1,0:T(8,128)(2,1)S(1)} collective-permute-done((bf16[2,384,1536]{2,1,0:T(8,128)(2,1)}, bf16[2,384,1536]{2,1,0:T(8,128)(2,1)S(1)}, u32[]{:S(2)}, u32[]{:S(2)}) %collective-permute-start) | collective-permute-done | bytes 2359328 | tf_op jit(solution)/shard_map/ppermute | solution.py:27
  43.3 1.4 copy-done.1
  44.7 3.3 %split.1 = (bf16[384,1536]{1,0:T(8,128)(2,1)}, bf16[384,1536]{1,0:T(8,128)(2,1)}) custom-call(bf16[2,384,1536]{2,1,0:T(8,128)(2,1)} %copy-done.1, bf16[2,384,1536]{2,1,0:T(8,128)(2,1)} %collective-permute-done.1.high.refs_3_), custom_call_target="tpu_custom_call" | custom-call | tf_op jit(solution)/shard_map/split/pallas_call | solution.py:240
  48.0 1.7 collective-permute-start.2
  53.2 5.7 %collective-permute-start.12 = (s32[1,48]{1,0:T(1,128)S(1)}, s32[1,48]{1,0:T(1,128)S(1)}, u32[]{:S(2)}, u32[]{:S(2)}) collective-permute-start(s32[1,48]{1,0:T(1,128)S(1)} %pad_add_fusion.table_a.table_b), channel_id=1, source_target_pairs={{0,2},{1,3},{2,0},{3,1},{4,6},{5,7},{6,4},{7,5},{8,10},{9,11},{10,... | collective-permute-start | bytes 584 | tf_op jit(solution)/shard_map/ppermute | solution.py:27
  58.9 9.1 %collective-permute-done.2.refs_4_.refs_2_ = bf16[384,1536]{1,0:T(8,128)(2,1)S(1)} collective-permute-done((bf16[384,1536]{1,0:T(8,128)(2,1)}, bf16[384,1536]{1,0:T(8,128)(2,1)S(1)}, u32[]{:S(2)}, u32[]{:S(2)}) %collective-permute-start.2) | collective-permute-done | bytes 1179680 | tf_op jit(solution)/shard_map/ppermute | solution.py:27
  68.3 1.6 collective-permute-start.10
  69.9 2.1 %collective-permute-start.11 = (bf16[384,1536]{1,0:T(8,128)(2,1)}, bf16[384,1536]{1,0:T(8,128)(2,1)S(1)}, u32[]{:S(2)}, u32[]{:S(2)}) collective-permute-start(bf16[384,1536]{1,0:T(8,128)(2,1)} %copy-done.6), channel_id=1, source_target_pairs={{0,3},{1,0},{2,1},{3,2},{4,7},{5,4},{6,5},{7,6},{8,11},{9,8},{10,9... | collective-permute-start | bytes 3538952 | tf_op jit(solution)/shard_map/ppermute | solution.py:27
  72.1 1.7 copy-done.2
  73.7 11.5 %shard_map.66 = (bf16[384,1536]{1,0:T(8,128)(2,1)}, bf16[384,1536]{1,0:T(8,128)(2,1)}) custom-call(s32[1]{0:T(128)} %bitcast.device, s32[1,48]{1,0:T(1,128)S(1)} %collective-permute-done.12.table_a.table_b, s32[1,48]{1,0:T(1,128)S(1)} %collective-permute-done.12.table_a.table_b, f32[256]{0:T(256)S(1)} %copy-done.5, f32[384]{0:T(512)S(1)} %copy-done.4, ...), custom_call_target="tpu_custom_call" | custom-call | tf_op jit(solution)/shard_map/pallas_call | solution.py:121
  85.3 1.5 collective-permute-start.13
  86.8 15.5 %collective-permute-done.8.table_a = s32[1,48]{1,0:T(1,128)S(1)} collective-permute-done((s32[1,48]{1,0:T(1,128)S(1)}, s32[1,48]{1,0:T(1,128)S(1)}, u32[]{:S(2)}, u32[]{:S(2)}) %collective-permute-start.8) | collective-permute-done | bytes 224 | tf_op jit(solution)/shard_map/ppermute | solution.py:27
  102.8 2.3 %collective-permute-done.9.table_b = s32[1,48]{1,0:T(1,128)S(1)} collective-permute-done((s32[1,48]{1,0:T(1,128)S(1)}, s32[1,48]{1,0:T(1,128)S(1)}, u32[]{:S(2)}, u32[]{:S(2)}) %collective-permute-start.9) | collective-permute-done | bytes 224 | tf_op jit(solution)/shard_map/ppermute | solution.py:27
  105.1 8.6 %shard_map.67 = (f32[384,1536]{1,0:T(8,128)S(1)}, f32[384,1536]{1,0:T(8,128)S(1)}) custom-call(s32[1]{0:T(128)} %bitcast.device, s32[1,48]{1,0:T(1,128)S(1)} %collective-permute-done.8.table_a, s32[1,48]{1,0:T(1,128)S(1)} %collective-permute-done.9.table_b, f32[256]{0:T(256)S(1)} %copy-done.5, f32[384]{0:T(512)S(1)} %copy-done.4, ...), custom_call_target="tpu_custom_call" | custom-call | tf_op jit(solution)/shard_map/pallas_call | solution.py:121
  113.7 4.8 %shard_map.68 = (bf16[384,1536]{1,0:T(8,128)(2,1)S(1)}, bf16[384,1536]{1,0:T(8,128)(2,1)S(1)}) custom-call(s32[1]{0:T(128)} %bitcast.device, s32[1,48]{1,0:T(1,128)S(1)} %collective-permute-done.8.table_a, s32[1,48]{1,0:T(1,128)S(1)} %collective-permute-done.9.table_b, f32[256]{0:T(256)S(1)} %copy-done.5, f32[384]{0:T(512)S(1)} %copy-done.4, ...), custom_call_target="tpu_custom_call" | custom-call | tf_op jit(solution)/shard_map/pallas_call | solution.py:121
  118.7 1.8 collective-permute-start.16
  120.5 2.1 %shard_map.65 = (bf16[384,1536]{1,0:T(8,128)(2,1)S(1)}, bf16[384,1536]{1,0:T(8,128)(2,1)S(1)}) custom-call(s32[1]{0:T(128)} %bitcast.device, s32[1,48]{1,0:T(1,128)S(1)} %collective-permute-done.8.table_a, s32[1,48]{1,0:T(1,128)S(1)} %collective-permute-done.9.table_b, f32[256]{0:T(256)S(1)} %copy-done.5, f32[384]{0:T(512)S(1)} %copy-done.4, ...), custom_call_target="tpu_custom_call" | custom-call | tf_op jit(solution)/shard_map/pallas_call | solution.py:121
  122.6 1.5 add_convert_fusion
  124.2 4.6 %collective-permute-start.18 = (bf16[384,1536]{1,0:T(8,128)(2,1)S(1)}, bf16[384,1536]{1,0:T(8,128)(2,1)S(1)}, u32[]{:S(2)}, u32[]{:S(2)}) collective-permute-start(bf16[384,1536]{1,0:T(8,128)(2,1)S(1)} %add_convert_fusion), channel_id=1, source_target_pairs={{0,3},{1,0},{2,1},{3,2},{4,7},{5,4},{6,5},{7,6},{8,11},{9,8},{10,9... | collective-permute-start | bytes 3538952 | tf_op jit(solution)/shard_map/ppermute | solution.py:27
  128.8 1.5 add_convert_fusion.1
  130.6 9.2 %shard_map.64 = (f32[384,1536]{1,0:T(8,128)S(1)}, f32[384,1536]{1,0:T(8,128)S(1)}) custom-call(s32[1]{0:T(128)} %bitcast.device, s32[1,48]{1,0:T(1,128)S(1)} %pad_add_fusion.table_a.table_b, s32[1,48]{1,0:T(1,128)S(1)} %pad_add_fusion.table_a.table_b, f32[256]{0:T(256)S(1)} %copy-done.5, f32[384]{0:T(512)S(1)} %copy-done.4, ...), custom_call_target="tpu_custom_call" | custom-call | tf_op jit(solution)/shard_map/pallas_call | solution.py:121
  139.9 7.0 %collective-permute-done.18.down_b = bf16[384,1536]{1,0:T(8,128)(2,1)S(1)} collective-permute-done((bf16[384,1536]{1,0:T(8,128)(2,1)S(1)}, bf16[384,1536]{1,0:T(8,128)(2,1)S(1)}, u32[]{:S(2)}, u32[]{:S(2)}) %collective-permute-start.18) | collective-permute-done | bytes 1179680 | tf_op jit(solution)/shard_map/ppermute | solution.py:27
  147.9 4.0 %pack.1 = bf16[128,24,384]{2,1,0:T(8,128)(2,1)} custom-call(f32[384,1536]{1,0:T(8,128)S(1)} %get-tuple-element.27.own_a, f32[384,1536]{1,0:T(8,128)S(1)} %get-tuple-element.28.own_b, bf16[384,1536]{1,0:T(8,128)(2,1)S(1)} %collective-permute-done.14.up_a, bf16[384,1536]{1,0:T(8,128)(2,1)S(1)} %collective-permute-done.15.down_a, ...), custom_call_target="tpu_custom_call" | custom-call | tf_op jit(solution)/shard_map/pack/pallas_call | solution.py:170
  151.9 17.6 %all-to-all-start = ((bf16[128,24,384]{2,1,0:T(8,128)(2,1)}), bf16[128,24,384]{2,1,0:T(8,128)(2,1)S(1)}, u32[]{:S(2)}, u32[]{:S(2)}) async-start(bf16[128,24,384]{2,1,0:T(8,128)(2,1)} %pack.1), calls=%async_computation | async-start | bytes 4718592 | tf_op jit(solution)/shard_map/all_to_all | solution.py:297
  170.5 31.2 %all-to-all-done = bf16[128,24,384]{2,1,0:T(8,128)(2,1)S(1)} async-done(((bf16[128,24,384]{2,1,0:T(8,128)(2,1)}), bf16[128,24,384]{2,1,0:T(8,128)(2,1)S(1)}, u32[]{:S(2)}, u32[]{:S(2)}) %all-to-all-start) | async-done | bytes 2359328 | tf_op jit(solution)/shard_map/all_to_all | solution.py:297
  201.7 4.8 %finish.1 = bf16[48,96,768]{2,1,0:T(8,128)(2,1)} custom-call(bf16[3072,384]{1,0:T(8,128)(2,1)S(1)} %bitcast.13, bf16[768,256]{1,0:T(8,128)(2,1)S(1)} %bitcast.14), custom_call_target="tpu_custom_call" | custom-call | tf_op jit(solution)/shard_map/finish/pallas_call | solution.py:211
  (44 shorter events, 8.0 us)
Async XLA Ops:
  0.0 43.3 %collective-permute-start = (bf16[2,384,1536]{2,1,0:T(8,128)(2,1)}, bf16[2,384,1536]{2,1,0:T(8,128)(2,1)S(1)}, u32[]{:S(2)}, u32[]{:S(2)}) collective-permute-start(bf16[2,384,1536]{2,1,0:T(8,128)(2,1)} %own.9), channel_id=1, source_target_pairs={{0,4},{1,5},{2,6},{3,7},{4,8},{5,9},{6,10},{7,11},{8,12},{9,13},{1... | collective-permute-start | bytes 7077896 | tf_op jit(solution)/shard_map/ppermute | solution.py:27
  2.0 42.7 %collective-permute-start.1 = (bf16[2,384,1536]{2,1,0:T(8,128)(2,1)}, bf16[2,384,1536]{2,1,0:T(8,128)(2,1)}, u32[]{:S(2)}, u32[]{:S(2)}) collective-permute-start(bf16[2,384,1536]{2,1,0:T(8,128)(2,1)} %own.9), channel_id=1, source_target_pairs={{0,12},{1,13},{2,14},{3,15},{4,0},{5,1},{6,2},{7,3},{8,4},{9,5},{1... | collective-permute-start | bytes 7077896 | tf_op jit(solution)/shard_map/ppermute | solution.py:27
  5.1 38.2 %copy-start.7 = (bf16[384,1536]{1,0:T(8,128)(2,1)}, bf16[384,1536]{1,0:T(8,128)(2,1)S(1)}, u32[]{:S(2)}) copy-start(bf16[384,1536]{1,0:T(8,128)(2,1)S(1)} %get-tuple-element.29) | copy-start | bytes 3538948
  5.1 42.9 %copy-start.6 = (bf16[384,1536]{1,0:T(8,128)(2,1)}, bf16[384,1536]{1,0:T(8,128)(2,1)S(1)}, u32[]{:S(2)}) copy-start(bf16[384,1536]{1,0:T(8,128)(2,1)S(1)} %get-tuple-element.30) | copy-start | bytes 3538948
  5.1 30.7 %collective-permute-start.4 = (bf16[384,1536]{1,0:T(8,128)(2,1)S(1)}, bf16[384,1536]{1,0:T(8,128)(2,1)}, u32[]{:S(2)}, u32[]{:S(2)}) collective-permute-start(bf16[384,1536]{1,0:T(8,128)(2,1)S(1)} %get-tuple-element.30), channel_id=1, source_target_pairs={{0,1},{1,2},{2,3},{3,0},{4,5},{5,6},{6,7},{7,4},{8,9},{9,10},{10,1... | collective-permute-start | bytes 3538952 | tf_op jit(solution)/shard_map/ppermute | solution.py:27
  7.0 65.0 %copy-start.4 = (f32[384]{0:T(512)S(1)}, f32[384]{0:T(512)}, u32[]{:S(2)}) copy-start(f32[384]{0:T(512)} %levels.9) | copy-start | bytes 4612
  7.0 65.0 %copy-start.5 = (f32[256]{0:T(256)S(1)}, f32[256]{0:T(256)}, u32[]{:S(2)}) copy-start(f32[256]{0:T(256)} %energies.9) | copy-start | bytes 3076
  7.0 28.8 %collective-permute-start.6 = (bf16[384,1536]{1,0:T(8,128)(2,1)S(1)}, bf16[384,1536]{1,0:T(8,128)(2,1)}, u32[]{:S(2)}, u32[]{:S(2)}) collective-permute-start(bf16[384,1536]{1,0:T(8,128)(2,1)S(1)} %get-tuple-element.29), channel_id=1, source_target_pairs={{0,3},{1,0},{2,1},{3,2},{4,7},{5,4},{6,5},{7,6},{8,11},{9,8},{10,9... | collective-permute-start | bytes 3538952 | tf_op jit(solution)/shard_map/ppermute | solution.py:27
  35.8 23.1 %collective-permute-start.5 = (bf16[384,1536]{1,0:T(8,128)(2,1)}, bf16[384,1536]{1,0:T(8,128)(2,1)}, u32[]{:S(2)}, u32[]{:S(2)}) collective-permute-start(bf16[384,1536]{1,0:T(8,128)(2,1)} %collective-permute-done.4.refs_0_), channel_id=1, source_target_pairs={{0,1},{1,2},{2,3},{3,0},{4,5},{5,6},{6,7},{7,4},{8,9},{9,10},{10,1... | collective-permute-start | bytes 3538952 | tf_op jit(solution)/shard_map/ppermute | solution.py:27
  35.8 23.1 %collective-permute-start.7 = (bf16[384,1536]{1,0:T(8,128)(2,1)}, bf16[384,1536]{1,0:T(8,128)(2,1)}, u32[]{:S(2)}, u32[]{:S(2)}) collective-permute-start(bf16[384,1536]{1,0:T(8,128)(2,1)} %collective-permute-done.6.refs_1_), channel_id=1, source_target_pairs={{0,3},{1,0},{2,1},{3,2},{4,7},{5,4},{6,5},{7,6},{8,11},{9,8},{10,9... | collective-permute-start | bytes 3538952 | tf_op jit(solution)/shard_map/ppermute | solution.py:27
  43.3 1.4 copy-start.1
  44.7 27.3 %copy-start = (bf16[2,384,1536]{2,1,0:T(8,128)(2,1)S(1)}, bf16[2,384,1536]{2,1,0:T(8,128)(2,1)}, u32[]{:S(2)}) copy-start(bf16[2,384,1536]{2,1,0:T(8,128)(2,1)} %own.9) | copy-start | bytes 7077892
  48.0 19.9 %collective-permute-start.2 = (bf16[384,1536]{1,0:T(8,128)(2,1)}, bf16[384,1536]{1,0:T(8,128)(2,1)S(1)}, u32[]{:S(2)}, u32[]{:S(2)}) collective-permute-start(bf16[384,1536]{1,0:T(8,128)(2,1)} %get-tuple-element.23), channel_id=1, source_target_pairs={{0,4},{1,5},{2,6},{3,7},{4,8},{5,9},{6,10},{7,11},{8,12},{9,13},{1... | collective-permute-start | bytes 3538952 | tf_op jit(solution)/shard_map/ppermute | solution.py:27
  49.7 18.6 %collective-permute-start.3 = (bf16[384,1536]{1,0:T(8,128)(2,1)}, bf16[384,1536]{1,0:T(8,128)(2,1)}, u32[]{:S(2)}, u32[]{:S(2)}) collective-permute-start(bf16[384,1536]{1,0:T(8,128)(2,1)} %get-tuple-element.24), channel_id=1, source_target_pairs={{0,12},{1,13},{2,14},{3,15},{4,0},{5,1},{6,2},{7,3},{8,4},{9,5},{1... | collective-permute-start | bytes 3538952 | tf_op jit(solution)/shard_map/ppermute | solution.py:27
  53.2 18.9 %collective-permute-start.12 = (s32[1,48]{1,0:T(1,128)S(1)}, s32[1,48]{1,0:T(1,128)S(1)}, u32[]{:S(2)}, u32[]{:S(2)}) collective-permute-start(s32[1,48]{1,0:T(1,128)S(1)} %pad_add_fusion.table_a.table_b), channel_id=1, source_target_pairs={{0,2},{1,3},{2,0},{3,1},{4,6},{5,7},{6,4},{7,5},{8,10},{9,11},{10,... | collective-permute-start | bytes 584 | tf_op jit(solution)/shard_map/ppermute | solution.py:27
  68.3 50.4 %collective-permute-start.10 = (bf16[384,1536]{1,0:T(8,128)(2,1)}, bf16[384,1536]{1,0:T(8,128)(2,1)S(1)}, u32[]{:S(2)}, u32[]{:S(2)}) collective-permute-start(bf16[384,1536]{1,0:T(8,128)(2,1)} %copy-done.7), channel_id=1, source_target_pairs={{0,1},{1,2},{2,3},{3,0},{4,5},{5,6},{6,7},{7,4},{8,9},{9,10},{10,1... | collective-permute-start | bytes 3538952 | tf_op jit(solution)/shard_map/ppermute | solution.py:27
  69.9 50.6 %collective-permute-start.11 = (bf16[384,1536]{1,0:T(8,128)(2,1)}, bf16[384,1536]{1,0:T(8,128)(2,1)S(1)}, u32[]{:S(2)}, u32[]{:S(2)}) collective-permute-start(bf16[384,1536]{1,0:T(8,128)(2,1)} %copy-done.6), channel_id=1, source_target_pairs={{0,3},{1,0},{2,1},{3,2},{4,7},{5,4},{6,5},{7,6},{8,11},{9,8},{10,9... | collective-permute-start | bytes 3538952 | tf_op jit(solution)/shard_map/ppermute | solution.py:27
  72.0 1.7 copy-start.2
  73.7 31.4 %copy-start.3 = (bf16[2,384,1536]{2,1,0:T(8,128)(2,1)S(1)}, bf16[2,384,1536]{2,1,0:T(8,128)(2,1)}, u32[]{:S(2)}) copy-start(bf16[2,384,1536]{2,1,0:T(8,128)(2,1)} %copy-done.1) | copy-start | bytes 7077892
  85.3 37.3 %collective-permute-start.17 = (bf16[384,1536]{1,0:T(8,128)(2,1)}, bf16[384,1536]{1,0:T(8,128)(2,1)}, u32[]{:S(2)}, u32[]{:S(2)}) collective-permute-start(bf16[384,1536]{1,0:T(8,128)(2,1)} %get-tuple-element.40), channel_id=1, source_target_pairs={{0,3},{1,0},{2,1},{3,2},{4,7},{5,4},{6,5},{7,6},{8,11},{9,8},{10,9... | collective-permute-start | bytes 3538952 | tf_op jit(solution)/shard_map/ppermute | solution.py:27
  85.3 43.4 %collective-permute-start.13 = (bf16[384,1536]{1,0:T(8,128)(2,1)}, bf16[384,1536]{1,0:T(8,128)(2,1)}, u32[]{:S(2)}, u32[]{:S(2)}) collective-permute-start(bf16[384,1536]{1,0:T(8,128)(2,1)} %get-tuple-element.34), channel_id=1, source_target_pairs={{0,1},{1,2},{2,3},{3,0},{4,5},{5,6},{6,7},{7,4},{8,9},{9,10},{10,1... | collective-permute-start | bytes 3538952 | tf_op jit(solution)/shard_map/ppermute | solution.py:27
  86.8 15.5 %collective-permute-start.8 = (s32[1,48]{1,0:T(1,128)S(1)}, s32[1,48]{1,0:T(1,128)S(1)}, u32[]{:S(2)}, u32[]{:S(2)}) collective-permute-start(s32[1,48]{1,0:T(1,128)S(1)} %pad_add_fusion.table_a.table_b), channel_id=1, source_target_pairs={{0,1},{1,2},{2,3},{3,0},{4,5},{5,6},{6,7},{7,4},{8,9},{9,10},{10,1... | collective-permute-start | bytes 584 | tf_op jit(solution)/shard_map/ppermute | solution.py:27
  102.3 2.8 %collective-permute-start.9 = (s32[1,48]{1,0:T(1,128)S(1)}, s32[1,48]{1,0:T(1,128)S(1)}, u32[]{:S(2)}, u32[]{:S(2)}) collective-permute-start(s32[1,48]{1,0:T(1,128)S(1)} %pad_add_fusion.table_a.table_b), channel_id=1, source_target_pairs={{0,3},{1,0},{2,1},{3,2},{4,7},{5,4},{6,5},{7,6},{8,11},{9,8},{10,9... | collective-permute-start | bytes 584 | tf_op jit(solution)/shard_map/ppermute | solution.py:27
  118.6 21.3 %collective-permute-start.15 = (bf16[384,1536]{1,0:T(8,128)(2,1)S(1)}, bf16[384,1536]{1,0:T(8,128)(2,1)S(1)}, u32[]{:S(2)}, u32[]{:S(2)}) collective-permute-start(bf16[384,1536]{1,0:T(8,128)(2,1)S(1)} %get-tuple-element.37), channel_id=1, source_target_pairs={{0,3},{1,0},{2,1},{3,2},{4,7},{5,4},{6,5},{7,6},{8,11},{9,8},{10,9... | collective-permute-start | bytes 3538952 | tf_op jit(solution)/shard_map/ppermute | solution.py:27
  118.7 21.2 %collective-permute-start.16 = (bf16[384,1536]{1,0:T(8,128)(2,1)S(1)}, bf16[384,1536]{1,0:T(8,128)(2,1)S(1)}, u32[]{:S(2)}, u32[]{:S(2)}) collective-permute-start(bf16[384,1536]{1,0:T(8,128)(2,1)S(1)} %get-tuple-element.38), channel_id=1, source_target_pairs={{0,1},{1,2},{2,3},{3,0},{4,5},{5,6},{6,7},{7,4},{8,9},{9,10},{10,1... | collective-permute-start | bytes 3538952 | tf_op jit(solution)/shard_map/ppermute | solution.py:27
  124.2 22.8 %collective-permute-start.18 = (bf16[384,1536]{1,0:T(8,128)(2,1)S(1)}, bf16[384,1536]{1,0:T(8,128)(2,1)S(1)}, u32[]{:S(2)}, u32[]{:S(2)}) collective-permute-start(bf16[384,1536]{1,0:T(8,128)(2,1)S(1)} %add_convert_fusion), channel_id=1, source_target_pairs={{0,3},{1,0},{2,1},{3,2},{4,7},{5,4},{6,5},{7,6},{8,11},{9,8},{10,9... | collective-permute-start | bytes 3538952 | tf_op jit(solution)/shard_map/ppermute | solution.py:27
  130.3 17.6 %collective-permute-start.14 = (bf16[384,1536]{1,0:T(8,128)(2,1)S(1)}, bf16[384,1536]{1,0:T(8,128)(2,1)S(1)}, u32[]{:S(2)}, u32[]{:S(2)}) collective-permute-start(bf16[384,1536]{1,0:T(8,128)(2,1)S(1)} %add_convert_fusion.1), channel_id=1, source_target_pairs={{0,1},{1,2},{2,3},{3,0},{4,5},{5,6},{6,7},{7,4},{8,9},{9,10},{10,1... | collective-permute-start | bytes 3538952 | tf_op jit(solution)/shard_map/ppermute | solution.py:27
  151.9 17.6 %copy-start.8 = (bf16[768,256]{1,0:T(8,128)(2,1)S(1)}, bf16[768,256]{1,0:T(8,128)(2,1)}, u32[]{:S(2)}) copy-start(bf16[768,256]{1,0:T(8,128)(2,1)} %param.9) | copy-start | bytes 1179652
  151.9 49.8 %all-to-all-start = ((bf16[128,24,384]{2,1,0:T(8,128)(2,1)}), bf16[128,24,384]{2,1,0:T(8,128)(2,1)S(1)}, u32[]{:S(2)}, u32[]{:S(2)}) async-start(bf16[128,24,384]{2,1,0:T(8,128)(2,1)} %pack.1), calls=%async_computation | async-start | bytes 4718592 | tf_op jit(solution)/shard_map/all_to_all | solution.py:297
